TPU v7x, 256 devices: a whole 4x4x8 slice. The times are simulated.
256 devices in a mesh: box: 64 (over y, x, z_hi, core), term: 4 (over z_lo).
Axes of the slice: x: 4, y: 4, z: 8 (z_hi: 2, z_lo: 4; z = z_hi * 4 + z_lo), core: 2. Of those that a mesh axis runs over, the one named last changes fastest.
Arguments:
- fine_coeffs: bfloat16 [4, 512, 32, 1024], P(None, 'box'), may hold values from -6 to 6
- fine_blocks: bfloat16 [16, 3, 32, 32], replicated, may hold values from -0.625 to 0.625
- coarse_blocks: bfloat16 [16, 3, 32, 32], replicated, may hold values from -0.625 to 0.625
- two_scale: bfloat16 [32, 64], replicated, may hold values from -0.75 to 0.75
- term_exponent: int32 [8], replicated, may hold values from 0 to 15
Outputs:
- applied: float32 [4, 512, 32, 1024], P(None, ('box', 'term'))
All inputs are finite; a program needn't handle non-finite values.
Results may differ from a plain program's by a relative error of at most 0.0047.
Values may be sent and summed in bfloat16 or wider, within the bound.
No kernel may reach another device: no remote copies, remote signals or barrier semaphores. Data moves between devices by JAX's collectives and lax.ppermute only.
A program may use at most 128 MiB of HBM per device.

v0:
```python
import jax
import jax.numpy as jnp
from jax import lax
from jax.sharding import PartitionSpec as P


def from_behind(block, axis, distance):
    devices = range(lax.axis_size(axis))
    route = [((i - distance) % len(devices), i) for i in devices]
    return lax.ppermute(block, axis, route)


def side_count(total):
    return [guess for guess in range(1, 65) if guess * guess * guess == total][0]


def to_cells(box_rows, amount, breadth):
    cube = box_rows.reshape(amount, 2, 2, 2, breadth, breadth, breadth)
    cube = cube.transpose(0, 1, 4, 2, 5, 3, 6)
    return cube.reshape(amount, 2 * breadth, 2 * breadth, 2 * breadth)


def from_cells(fine_cells, breadth):
    amount = fine_cells.shape[0]
    cube = fine_cells.reshape(amount, 2, breadth, 2, breadth, 2, breadth)
    cube = cube.transpose(0, 1, 3, 5, 2, 4, 6)
    return cube.reshape(amount, 8, breadth, breadth * breadth)


def banded(blocks, own_boxes):
    breadth = blocks.shape[-1]
    matrix = jnp.zeros(((own_boxes + 2) * breadth, own_boxes * breadth), blocks.dtype)
    for column in range(own_boxes):
        for offset in range(3):
            source = column + offset
            matrix = matrix.at[
                source * breadth : (source + 1) * breadth, column * breadth : (column + 1) * breadth
            ].set(blocks[offset])
    return matrix


def margins_z(region, breadth):
    from_below = from_behind(region[:, :, :, -breadth:], "box", 1)
    from_above = from_behind(region[:, :, :, :breadth], "box", -1)
    return jnp.concatenate([from_below, region, from_above], axis=3)


def margins_y(region, breadth, grid_side):
    from_below = from_behind(region[:, :, -breadth:, :], "box", grid_side)
    from_above = from_behind(region[:, :, :breadth, :], "box", -grid_side)
    return jnp.concatenate([from_below, region, from_above], axis=2)


def margins_x(region, breadth, grid_side):
    from_below = from_behind(region[:, -breadth:, :, :], "box", grid_side * grid_side)
    from_above = from_behind(region[:, :breadth, :, :], "box", -grid_side * grid_side)
    return jnp.concatenate([from_below, region, from_above], axis=1)


def sweep(extended_z, matrix, breadth, grid_side):
    along_z = jnp.einsum(
        "fxyz,zw->fxyw", extended_z, matrix, preferred_element_type=jnp.float32
    ).astype(jnp.bfloat16)
    wider_y = margins_y(along_z, breadth, grid_side)
    along_y = jnp.einsum(
        "fxyw,yv->fxvw", wider_y, matrix, preferred_element_type=jnp.float32
    ).astype(jnp.bfloat16)
    wider_x = margins_x(along_y, breadth, grid_side)
    return jnp.einsum("fxvw,xu->fuvw", wider_x, matrix, preferred_element_type=jnp.float32)


def apply_levels(chosen, fine_blocks, coarse_blocks, two_scale, exponents, grid_side):
    breadth = two_scale.shape[0]
    amount = chosen.shape[0]
    fine_cells = to_cells(chosen, amount, breadth)
    parent = jnp.einsum(
        "fxyz,kz->fxyk", fine_cells, two_scale, preferred_element_type=jnp.float32
    ).astype(jnp.bfloat16)
    parent = jnp.einsum(
        "fxyk,jy->fxjk", parent, two_scale, preferred_element_type=jnp.float32
    ).astype(jnp.bfloat16)
    parent = jnp.einsum(
        "fxjk,ix->fijk", parent, two_scale, preferred_element_type=jnp.float32
    ).astype(jnp.bfloat16)
    fine_region = margins_z(fine_cells, breadth)
    coarse_region = margins_z(parent, breadth)
    selector = (
        exponents[:, None] == jnp.arange(fine_blocks.shape[0], dtype=jnp.int32)[None, :]
    ).astype(jnp.float32)
    fine_terms = jnp.einsum("te,eaij->taij", selector, fine_blocks.astype(jnp.float32)).astype(
        jnp.bfloat16
    )
    coarse_terms = jnp.einsum("te,eaij->taij", selector, coarse_blocks.astype(jnp.float32)).astype(
        jnp.bfloat16
    )
    fine_sum = jnp.zeros(fine_cells.shape, jnp.float32)
    coarse_sum = jnp.zeros(parent.shape, jnp.float32)
    for term_index in range(exponents.shape[0]):
        fine_sum = fine_sum + sweep(
            fine_region, banded(fine_terms[term_index], 2), breadth, grid_side
        )
        coarse_sum = coarse_sum + sweep(
            coarse_region, banded(coarse_terms[term_index], 1), breadth, grid_side
        )
    exact_mode = lax.Precision.HIGHEST
    scale_wide = two_scale.astype(jnp.float32)
    spread_out = jnp.einsum("fijk,kz->fijz", coarse_sum, scale_wide, precision=exact_mode)
    spread_out = jnp.einsum("fijz,jy->fiyz", spread_out, scale_wide, precision=exact_mode)
    spread_out = jnp.einsum("fiyz,ix->fxyz", spread_out, scale_wide, precision=exact_mode)
    return fine_sum + spread_out


def on_device(fine_coeffs, fine_blocks, coarse_blocks, two_scale, term_exponent):
    grid_side = side_count(lax.axis_size("box"))
    breadth = two_scale.shape[0]
    groups = lax.axis_size("term")
    total_terms = term_exponent.shape[0]
    own_terms = total_terms // groups
    exponents = lax.dynamic_slice_in_dim(
        term_exponent, lax.axis_index("term") * own_terms, own_terms, 0
    )
    result = apply_levels(fine_coeffs, fine_blocks, coarse_blocks, two_scale, exponents, grid_side)
    box_rows = from_cells(result, breadth)
    summed = lax.psum(box_rows, "term")
    portion = box_rows.shape[1] // groups
    return lax.dynamic_slice_in_dim(summed, lax.axis_index("term") * portion, portion, 1)


def solution(mesh):
    placed = (P(None, "box", None, None), P(), P(), P(), P())
    return jax.shard_map(
        on_device,
        mesh=mesh,
        in_specs=placed,
        out_specs=P(None, ("box", "term"), None, None),
        check_vma=False,
    )
```

profile of v0, /device:TPU:30, one launch (start us, length us, event | category | flops | bytes accessed | tf_op | source)
XLA Modules:
  0.0 718.1 jit_solution(14842954793799196121)
XLA Ops:
  6.5 11.0 %reshape.526 = bf16[4,2,2,2,32,32,32]{6,5,4,3,2,1,0:T(8,128)(2,1)} reshape(bf16[4,8,32,1024]{3,2,1,0:T(8,128)(2,1)} %param.41) | data formatting | bytes 4194304 | tf_op jit(solution)/shard_map/reshape | solution.py:18
  17.5 16.4 %copy.154 = bf16[4,2,2,2,32,32,32]{6,3,5,2,4,1,0:T(2,128)(2,1)} copy(bf16[4,2,2,2,32,32,32]{6,5,4,3,2,1,0:T(8,128)(2,1)} %reshape.526) | data formatting | bytes 4194304 | tf_op jit(solution)/shard_map/reshape | solution.py:18
  33.9 14.2 %reshape.527 = bf16[4,64,64,64]{3,2,1,0:T(8,128)(2,1)} reshape(bf16[4,2,32,2,32,2,32]{6,5,4,3,2,1,0:T(2,128)(2,1)} %bitcast.122) | data formatting | bytes 4194304 | tf_op jit(solution)/shard_map/reshape | solution.py:20
  48.1 6.8 convert_bitcast_fusion.2
  54.9 3.1 copy.65
  59.7 7.0 collective-permute-start.11
  66.7 7.7 %fusion.91 = (bf16[4,64,64,32]{3,2,1,0:T(8,128)(2,1)}, bf16[4,64,64,32]{3,2,1,0:T(8,128)(2,1)}) fusion(bf16[4,64,64,64]{3,2,1,0:T(8,128)(2,1)} %reshape.527), kind=kLoop, calls=%fused_computation.115 | loop fusion | bytes 4194304 | tf_op jit(solution)/shard_map/slice | solution.py:43
  74.4 4.8 copy.50
  81.8 6.5 collective-permute-done.10
  88.3 8.2 %collective-permute-done.11 = bf16[4,32,32,32]{3,1,2,0:T(8,128)(2,1)S(1)} collective-permute-done((bf16[4,32,32,32]{3,1,2,0:T(8,128)(2,1)S(1)}, bf16[4,32,32,32]{3,1,2,0:T(8,128)(2,1)S(1)}, u32[]{:S(2)}, u32[]{:S(2)}) %collective-permute-start.11) | collective-permute-done | bytes 262176 | tf_op jit(solution)/shard_map/ppermute | solution.py:10
  99.2 5.1 collective-permute-start.12
  106.0 5.4 collective-permute-start.16
  111.5 32.0 %collective-permute-done.12 = bf16[4,32,32,32]{2,3,1,0:T(8,128)(2,1)S(1)} collective-permute-done((bf16[4,32,32,32]{2,3,1,0:T(8,128)(2,1)S(1)}, bf16[4,32,32,32]{2,3,1,0:T(8,128)(2,1)S(1)}, u32[]{:S(2)}, u32[]{:S(2)}) %collective-permute-start.12) | collective-permute-done | bytes 262176 | tf_op jit(solution)/shard_map/ppermute | solution.py:10
  147.1 18.8 %collective-permute-done.16 = bf16[4,32,32,32]{2,3,1,0:T(8,128)(2,1)S(1)} collective-permute-done((bf16[4,32,32,32]{2,3,1,0:T(8,128)(2,1)S(1)}, bf16[4,32,32,32]{2,3,1,0:T(8,128)(2,1)S(1)}, u32[]{:S(2)}, u32[]{:S(2)}) %collective-permute-start.16) | collective-permute-done | bytes 262176 | tf_op jit(solution)/shard_map/ppermute | solution.py:10
  169.8 4.8 copy.51
  183.6 2.9 copy.69
  186.5 2.9 copy.71
  189.4 4.3 collective-permute-done.18
  195.9 5.2 collective-permute-done.19
  201.1 2.4 copy.78
  209.3 4.8 copy.52
  214.1 4.8 copy.53
  218.9 8.6 %convolution_convert_fusion = bf16[4,64,64,64]{3,2,1,0:T(8,128)(2,1)S(1)} fusion(bf16[128,64]{1,0:T(8,128)(2,1)S(1)} %scatter.79, bf16[4,64,64,32]{3,2,1,0:T(8,128)(2,1)} %copy.53, bf16[4,64,64,64]{3,2,1,0:T(8,128)(2,1)} %reshape.527, bf16[4,64,64,32]{3,2,1,0:T(8,128)(2,1)} %copy.52), kind=kOutput, calls=%fused_computation.23 | convolution fusion | flops 282066944 | bytes 6307840 | tf_op jit(solution)/shard_map/fxyz,zw->fxyw/dot_general | solution.py:61
  227.5 3.2 fusion.90
  230.7 17.9 %collective-permute-start.6 = (bf16[4,64,32,64]{3,2,1,0:T(8,128)(2,1)}, bf16[4,64,32,64]{3,2,1,0:T(8,128)(2,1)}, u32[]{:S(2)}, u32[]{:S(2)}) collective-permute-start(bf16[4,64,32,64]{3,2,1,0:T(8,128)(2,1)} %get-tuple-element.227), channel_id=1, source_target_pairs={{240,0},{244,4},{248,8},{252,12},{0,16},{4,20},{8,24},{12,28},{16,... | collective-permute-start | bytes 3145736 | tf_op jit(solution)/shard_map/ppermute | solution.py:10
  249.0 5.1 convolution_bitcast_fusion
  254.1 6.3 copy.81
  260.4 8.6 %convolution_convert_fusion.1 = bf16[4,64,64,64]{3,2,1,0:T(8,128)(2,1)S(1)} fusion(bf16[128,64]{1,0:T(8,128)(2,1)S(1)} %scatter.69, bf16[4,64,64,32]{3,2,1,0:T(8,128)(2,1)} %copy.53, bf16[4,64,64,64]{3,2,1,0:T(8,128)(2,1)} %reshape.527, bf16[4,64,64,32]{3,2,1,0:T(8,128)(2,1)} %copy.52), kind=kOutput, calls=%fused_computation.24 | convolution fusion | flops 282066944 | bytes 6307840 | tf_op jit(solution)/shard_map/fxyz,zw->fxyw/dot_general | solution.py:61
  271.2 5.3 collective-permute-start.2
  276.6 18.4 %collective-permute-done.6 = bf16[4,64,32,64]{3,2,1,0:T(8,128)(2,1)} collective-permute-done((bf16[4,64,32,64]{3,2,1,0:T(8,128)(2,1)}, bf16[4,64,32,64]{3,2,1,0:T(8,128)(2,1)}, u32[]{:S(2)}, u32[]{:S(2)}) %collective-permute-start.6) | collective-permute-done | bytes 1048608 | tf_op jit(solution)/shard_map/ppermute | solution.py:10
  294.9 6.2 collective-permute-done.7
  301.1 3.9 convert_bitcast_fusion
  305.1 2.8 fusion.89
  310.1 3.5 fusion.75
  313.6 25.4 %collective-permute-done.2 = bf16[4,64,32,64]{3,2,1,0:T(8,128)(2,1)} collective-permute-done((bf16[4,64,32,64]{3,2,1,0:T(8,128)(2,1)}, bf16[4,64,32,64]{3,2,1,0:T(8,128)(2,1)}, u32[]{:S(2)}, u32[]{:S(2)}) %collective-permute-start.2) | collective-permute-done | bytes 1048608 | tf_op jit(solution)/shard_map/ppermute | solution.py:10
  339.0 6.0 collective-permute-done.3
  344.9 3.9 convert_bitcast_fusion.1
  348.9 2.7 fusion.87
  353.9 36.0 %collective-permute-done.9 = bf16[4,32,64,64]{3,2,1,0:T(8,128)(2,1)} collective-permute-done((bf16[4,32,64,64]{3,2,1,0:T(8,128)(2,1)S(1)}, bf16[4,32,64,64]{3,2,1,0:T(8,128)(2,1)}, u32[]{:S(2)}, u32[]{:S(2)}) %collective-permute-start.9) | collective-permute-done | bytes 1048608 | tf_op jit(solution)/shard_map/ppermute | solution.py:10
  389.9 3.9 pad_maximum_fusion.1
  393.8 8.8 %fusion.12 = f32[64,4,64,64]{3,0,2,1:T(8,128)} fusion(bf16[4,128,64,64]{3,2,1,0:T(8,128)(2,1)S(1)} %pad_maximum_fusion.1, bf16[128,64]{1,0:T(8,128)(2,1)S(1)} %scatter.79), kind=kOutput, calls=%fused_computation.15 | convolution fusion | flops 268435456 | bytes 8404992 | tf_op jit(solution)/shard_map/fxvw,xu->fuvw/dot_general | solution.py:69
  402.6 32.1 %collective-permute-done.5 = bf16[4,32,64,64]{3,2,1,0:T(8,128)(2,1)} collective-permute-done((bf16[4,32,64,64]{3,2,1,0:T(8,128)(2,1)S(1)}, bf16[4,32,64,64]{3,2,1,0:T(8,128)(2,1)}, u32[]{:S(2)}, u32[]{:S(2)}) %collective-permute-start.5) | collective-permute-done | bytes 1048608 | tf_op jit(solution)/shard_map/ppermute | solution.py:10
  434.7 6.6 pad_maximum_fusion
  441.3 15.4 %bitcast_add_fusion = f32[4,64,64,64]{3,1,2,0:T(8,128)} fusion(f32[4,64,64,64]{2,3,1,0:T(8,128)S(1)} %fusion.75, f32[64,4,64,64]{3,0,2,1:T(8,128)} %fusion.12, bf16[4,128,64,64]{3,2,1,0:T(8,128)(2,1)} %pad_maximum_fusion, bf16[128,64]{1,0:T(8,128)(2,1)S(1)} %scatter.69), kind=kOutput, calls=%fused_computation.14 | convolution fusion | flops 270532608 | bytes 16793600 | tf_op jit(solution)/shard_map/fxvw,xu->fuvw/dot_general | solution.py:69
  456.8 17.1 %reshape.537 = f32[4,2,32,2,32,2,32]{6,5,2,1,4,3,0:T(2,128)} reshape(f32[4,64,64,64]{3,1,2,0:T(8,128)} %bitcast_add_fusion) | data formatting | bytes 8388608 | tf_op jit(solution)/shard_map/reshape | solution.py:25
  473.9 17.7 %copy.83 = f32[4,2,2,2,32,32,32]{6,5,4,3,2,1,0:T(8,128)} copy(f32[4,2,2,2,32,32,32]{6,3,4,1,5,2,0:T(2,128)} %bitcast.121) | data formatting | bytes 8388608 | tf_op jit(solution)/shard_map/transpose | solution.py:26
  491.6 13.7 %reshape.538 = f32[4,8,32,1024]{3,2,1,0:T(8,128)} reshape(f32[4,2,2,2,32,32,32]{6,5,4,3,2,1,0:T(8,128)} %copy.83) | data formatting | bytes 8388608 | tf_op jit(solution)/shard_map/reshape | solution.py:27
  505.4 203.1 %all-reduce.6.cloned.1.call-done = f32[4,8,32,1024]{3,2,1,0:T(8,128)} async-done(((f32[4,8,32,1024]{3,2,1,0:T(8,128)}), f32[4,8,32,1024]{3,2,1,0:T(8,128)}) %all-reduce.6.cloned.1.call-update) | async-done | bytes 4194320 | tf_op jit(solution)/shard_map/psum | solution.py:124
  (90 shorter events, 42.3 us)
Async XLA Ops:
  6.5 73.6 %copy-start = (bf16[16,3,32,32]{3,2,1,0:T(8,128)(2,1)S(1)}, bf16[16,3,32,32]{3,2,1,0:T(8,128)(2,1)}, u32[]{:S(2)}) copy-start(bf16[16,3,32,32]{3,2,1,0:T(8,128)(2,1)} %param.43) | copy-start | bytes 294916
  6.5 701.9 %all-reduce.6.cloned.1.call-start = ((), (), s32[]{:S(2)}) async-start(), calls=%async_computation | async-start | bytes 8388608 | tf_op jit(solution)/shard_map/psum | solution.py:124
  33.9 14.2 %copy-start.9 = (bf16[32,64]{1,0:T(8,128)(2,1)S(1)}, bf16[32,64]{1,0:T(8,128)(2,1)}, u32[]{:S(2)}) copy-start(bf16[32,64]{1,0:T(8,128)(2,1)} %param.44) | copy-start | bytes 12292
  59.7 28.7 %collective-permute-start.10 = (bf16[4,32,32,32]{3,1,2,0:T(8,128)(2,1)S(1)}, bf16[4,32,32,32]{3,1,2,0:T(8,128)(2,1)S(1)}, u32[]{:S(2)}, u32[]{:S(2)}) collective-permute-start(bf16[4,32,32,32]{3,1,2,0:T(8,128)(2,1)S(1)} %fusion.30), channel_id=1, source_target_pairs={{252,0},{0,4},{4,8},{8,12},{12,16},{16,20},{20,24},{24,28},{28,32}... | collective-permute-start | bytes 786440 | tf_op jit(solution)/shard_map/ppermute | solution.py:10
  59.7 36.8 %collective-permute-start.11 = (bf16[4,32,32,32]{3,1,2,0:T(8,128)(2,1)S(1)}, bf16[4,32,32,32]{3,1,2,0:T(8,128)(2,1)S(1)}, u32[]{:S(2)}, u32[]{:S(2)}) collective-permute-start(bf16[4,32,32,32]{3,1,2,0:T(8,128)(2,1)S(1)} %fusion.30), channel_id=1, source_target_pairs={{4,0},{8,4},{12,8},{16,12},{20,16},{24,20},{28,24},{32,28},{36,32}... | collective-permute-start | bytes 786440 | tf_op jit(solution)/shard_map/ppermute | solution.py:10
  74.4 5.6 copy-start.10
  79.3 130.0 %collective-permute-start = (bf16[4,64,64,32]{2,3,1,0:T(8,128)(2,1)}, bf16[4,64,64,32]{2,3,1,0:T(8,128)(2,1)}, u32[]{:S(2)}, u32[]{:S(2)}) collective-permute-start(bf16[4,64,64,32]{2,3,1,0:T(8,128)(2,1)} %copy.50), channel_id=1, source_target_pairs={{252,0},{0,4},{4,8},{8,12},{12,16},{16,20},{20,24},{24,28},{28,32}... | collective-permute-start | bytes 3145736 | tf_op jit(solution)/shard_map/ppermute | solution.py:10
  99.2 44.3 %collective-permute-start.12 = (bf16[4,32,32,32]{2,3,1,0:T(8,128)(2,1)S(1)}, bf16[4,32,32,32]{2,3,1,0:T(8,128)(2,1)S(1)}, u32[]{:S(2)}, u32[]{:S(2)}) collective-permute-start(bf16[4,32,32,32]{2,3,1,0:T(8,128)(2,1)S(1)} %convolution_convert_fusion.5), channel_id=1, source_target_pairs={{240,0},{244,4},{248,8},{252,12},{0,16},{4,20},{8,24},{12,28},{16,... | collective-permute-start | bytes 786440 | tf_op jit(solution)/shard_map/ppermute | solution.py:10
  104.3 39.2 %collective-permute-start.13 = (bf16[4,32,32,32]{2,3,1,0:T(8,128)(2,1)S(1)}, bf16[4,32,32,32]{2,3,1,0:T(8,128)(2,1)S(1)}, u32[]{:S(2)}, u32[]{:S(2)}) collective-permute-start(bf16[4,32,32,32]{2,3,1,0:T(8,128)(2,1)S(1)} %convolution_convert_fusion.5), channel_id=1, source_target_pairs={{16,0},{20,4},{24,8},{28,12},{32,16},{36,20},{40,24},{44,28},{48,3... | collective-permute-start | bytes 786440 | tf_op jit(solution)/shard_map/ppermute | solution.py:10
  106.0 60.0 %collective-permute-start.16 = (bf16[4,32,32,32]{2,3,1,0:T(8,128)(2,1)S(1)}, bf16[4,32,32,32]{2,3,1,0:T(8,128)(2,1)S(1)}, u32[]{:S(2)}, u32[]{:S(2)}) collective-permute-start(bf16[4,32,32,32]{2,3,1,0:T(8,128)(2,1)S(1)} %convolution_convert_fusion.3), channel_id=1, source_target_pairs={{240,0},{244,4},{248,8},{252,12},{0,16},{4,20},{8,24},{12,28},{16,... | collective-permute-start | bytes 786440 | tf_op jit(solution)/shard_map/ppermute | solution.py:10
  111.4 54.6 %collective-permute-start.17 = (bf16[4,32,32,32]{2,3,1,0:T(8,128)(2,1)S(1)}, bf16[4,32,32,32]{2,3,1,0:T(8,128)(2,1)S(1)}, u32[]{:S(2)}, u32[]{:S(2)}) collective-permute-start(bf16[4,32,32,32]{2,3,1,0:T(8,128)(2,1)S(1)} %convolution_convert_fusion.3), channel_id=1, source_target_pairs={{16,0},{20,4},{24,8},{28,12},{32,16},{36,20},{40,24},{44,28},{48,3... | collective-permute-start | bytes 786440 | tf_op jit(solution)/shard_map/ppermute | solution.py:10
  145.0 29.6 %collective-permute-start.14 = (bf16[4,32,32,32]{3,2,1,0:T(8,128)(2,1)S(1)}, bf16[4,32,32,32]{3,2,1,0:T(8,128)(2,1)S(1)}, u32[]{:S(2)}, u32[]{:S(2)}) collective-permute-start(bf16[4,32,32,32]{3,2,1,0:T(8,128)(2,1)S(1)} %fusion.31), channel_id=1, source_target_pairs={{192,0},{196,4},{200,8},{204,12},{208,16},{212,20},{216,24},{220,2... | collective-permute-start | bytes 786440 | tf_op jit(solution)/shard_map/ppermute | solution.py:10
  145.1 41.4 %collective-permute-start.15 = (bf16[4,32,32,32]{3,2,1,0:T(8,128)(2,1)S(1)}, bf16[4,32,32,32]{3,2,1,0:T(8,128)(2,1)}, u32[]{:S(2)}, u32[]{:S(2)}) collective-permute-start(bf16[4,32,32,32]{3,2,1,0:T(8,128)(2,1)S(1)} %fusion.31), channel_id=1, source_target_pairs={{64,0},{68,4},{72,8},{76,12},{80,16},{84,20},{88,24},{92,28},{96,3... | collective-permute-start | bytes 786440 | tf_op jit(solution)/shard_map/ppermute | solution.py:10
  167.5 26.2 %collective-permute-start.18 = (bf16[4,32,32,32]{3,2,1,0:T(8,128)(2,1)S(1)}, bf16[4,32,32,32]{3,2,1,0:T(8,128)(2,1)}, u32[]{:S(2)}, u32[]{:S(2)}) collective-permute-start(bf16[4,32,32,32]{3,2,1,0:T(8,128)(2,1)S(1)} %fusion.32), channel_id=1, source_target_pairs={{192,0},{196,4},{200,8},{204,12},{208,16},{212,20},{216,24},{220,2... | collective-permute-start | bytes 786440 | tf_op jit(solution)/shard_map/ppermute | solution.py:10
  167.6 33.5 %collective-permute-start.19 = (bf16[4,32,32,32]{3,2,1,0:T(8,128)(2,1)S(1)}, bf16[4,32,32,32]{3,2,1,0:T(8,128)(2,1)}, u32[]{:S(2)}, u32[]{:S(2)}) collective-permute-start(bf16[4,32,32,32]{3,2,1,0:T(8,128)(2,1)S(1)} %fusion.32), channel_id=1, source_target_pairs={{64,0},{68,4},{72,8},{76,12},{80,16},{84,20},{88,24},{92,28},{96,3... | collective-permute-start | bytes 786440 | tf_op jit(solution)/shard_map/ppermute | solution.py:10
  174.6 5.9 copy-start.8
  174.6 39.5 %collective-permute-start.1 = (bf16[4,64,64,32]{2,3,1,0:T(8,128)(2,1)}, bf16[4,64,64,32]{2,3,1,0:T(8,128)(2,1)}, u32[]{:S(2)}, u32[]{:S(2)}) collective-permute-start(bf16[4,64,64,32]{2,3,1,0:T(8,128)(2,1)} %copy.51), channel_id=1, source_target_pairs={{4,0},{8,4},{12,8},{16,12},{20,16},{24,20},{28,24},{32,28},{36,32}... | collective-permute-start | bytes 3145736 | tf_op jit(solution)/shard_map/ppermute | solution.py:10
  203.5 1.6 copy-start.5
  203.5 1.6 copy-start.6
  203.5 1.8 copy-start.7
  227.5 3.2 copy-start.3
  230.7 64.2 %collective-permute-start.6 = (bf16[4,64,32,64]{3,2,1,0:T(8,128)(2,1)}, bf16[4,64,32,64]{3,2,1,0:T(8,128)(2,1)}, u32[]{:S(2)}, u32[]{:S(2)}) collective-permute-start(bf16[4,64,32,64]{3,2,1,0:T(8,128)(2,1)} %get-tuple-element.227), channel_id=1, source_target_pairs={{240,0},{244,4},{248,8},{252,12},{0,16},{4,20},{8,24},{12,28},{16,... | collective-permute-start | bytes 3145736 | tf_op jit(solution)/shard_map/ppermute | solution.py:10
  248.6 52.5 %collective-permute-start.7 = (bf16[4,64,32,64]{3,2,1,0:T(8,128)(2,1)}, bf16[4,64,32,64]{3,2,1,0:T(8,128)(2,1)}, u32[]{:S(2)}, u32[]{:S(2)}) collective-permute-start(bf16[4,64,32,64]{3,2,1,0:T(8,128)(2,1)} %get-tuple-element.228), channel_id=1, source_target_pairs={{16,0},{20,4},{24,8},{28,12},{32,16},{36,20},{40,24},{44,28},{48,3... | collective-permute-start | bytes 3145736 | tf_op jit(solution)/shard_map/ppermute | solution.py:10
  268.9 32.2 %copy-start.4 = (bf16[4,64,64,64]{3,2,1,0:T(8,128)(2,1)S(1)}, bf16[4,64,64,64]{3,2,1,0:T(8,128)(2,1)}, u32[]{:S(2)}) copy-start(bf16[4,64,64,64]{3,2,1,0:T(8,128)(2,1)} %copy-done.3) | copy-start | bytes 6291460
  271.2 67.7 %collective-permute-start.2 = (bf16[4,64,32,64]{3,2,1,0:T(8,128)(2,1)}, bf16[4,64,32,64]{3,2,1,0:T(8,128)(2,1)}, u32[]{:S(2)}, u32[]{:S(2)}) collective-permute-start(bf16[4,64,32,64]{3,2,1,0:T(8,128)(2,1)} %get-tuple-element.223), channel_id=1, source_target_pairs={{240,0},{244,4},{248,8},{252,12},{0,16},{4,20},{8,24},{12,28},{16,... | collective-permute-start | bytes 3145736 | tf_op jit(solution)/shard_map/ppermute | solution.py:10
  276.5 68.4 %collective-permute-start.3 = (bf16[4,64,32,64]{3,2,1,0:T(8,128)(2,1)S(1)}, bf16[4,64,32,64]{3,2,1,0:T(8,128)(2,1)}, u32[]{:S(2)}, u32[]{:S(2)}) collective-permute-start(bf16[4,64,32,64]{3,2,1,0:T(8,128)(2,1)S(1)} %get-tuple-element.224), channel_id=1, source_target_pairs={{16,0},{20,4},{24,8},{28,12},{32,16},{36,20},{40,24},{44,28},{48,3... | collective-permute-start | bytes 3145736 | tf_op jit(solution)/shard_map/ppermute | solution.py:10
  305.1 5.0 copy-start.2
  307.9 46.0 %collective-permute-start.8 = (bf16[4,32,64,64]{3,2,1,0:T(8,128)(2,1)}, bf16[4,32,64,64]{3,2,1,0:T(8,128)(2,1)}, u32[]{:S(2)}, u32[]{:S(2)}) collective-permute-start(bf16[4,32,64,64]{3,2,1,0:T(8,128)(2,1)} %get-tuple-element.225), channel_id=1, source_target_pairs={{192,0},{196,4},{200,8},{204,12},{208,16},{212,20},{216,24},{220,2... | collective-permute-start | bytes 3145736 | tf_op jit(solution)/shard_map/ppermute | solution.py:10
  307.9 82.0 %collective-permute-start.9 = (bf16[4,32,64,64]{3,2,1,0:T(8,128)(2,1)S(1)}, bf16[4,32,64,64]{3,2,1,0:T(8,128)(2,1)}, u32[]{:S(2)}, u32[]{:S(2)}) collective-permute-start(bf16[4,32,64,64]{3,2,1,0:T(8,128)(2,1)S(1)} %get-tuple-element.226), channel_id=1, source_target_pairs={{64,0},{68,4},{72,8},{76,12},{80,16},{84,20},{88,24},{92,28},{96,3... | collective-permute-start | bytes 3145736 | tf_op jit(solution)/shard_map/ppermute | solution.py:10
  351.6 51.0 %collective-permute-start.4 = (bf16[4,32,64,64]{3,2,1,0:T(8,128)(2,1)}, bf16[4,32,64,64]{3,2,1,0:T(8,128)(2,1)}, u32[]{:S(2)}, u32[]{:S(2)}) collective-permute-start(bf16[4,32,64,64]{3,2,1,0:T(8,128)(2,1)} %get-tuple-element.221), channel_id=1, source_target_pairs={{192,0},{196,4},{200,8},{204,12},{208,16},{212,20},{216,24},{220,2... | collective-permute-start | bytes 3145736 | tf_op jit(solution)/shard_map/ppermute | solution.py:10
  351.6 83.1 %collective-permute-start.5 = (bf16[4,32,64,64]{3,2,1,0:T(8,128)(2,1)S(1)}, bf16[4,32,64,64]{3,2,1,0:T(8,128)(2,1)}, u32[]{:S(2)}, u32[]{:S(2)}) collective-permute-start(bf16[4,32,64,64]{3,2,1,0:T(8,128)(2,1)S(1)} %get-tuple-element.222), channel_id=1, source_target_pairs={{64,0},{68,4},{72,8},{76,12},{80,16},{84,20},{88,24},{92,28},{96,3... | collective-permute-start | bytes 3145736 | tf_op jit(solution)/shard_map/ppermute | solution.py:10
  491.6 219.2 %copy-start.1 = (bf16[16,3,32,32]{3,2,1,0:T(8,128)(2,1)S(1)}, bf16[16,3,32,32]{3,2,1,0:T(8,128)(2,1)}, u32[]{:S(2)}) copy-start(bf16[16,3,32,32]{3,2,1,0:T(8,128)(2,1)} %param.43) | copy-start | bytes 294916
Sparse Core Ops, SparseCore 0:
  505.5 202.9 all-reduce.5
where the time goes:
time: 729 us; the launch traced here: 718 us
  waiting for transfers between devices  402 us (55%)
  local copies, waits for them, and re-layouts  160 us (22%)
  matrix products  79.9 us (11%)
  starting transfers between devices  50.7 us (7%)
  between operations  14.3 us (2%)
  other arithmetic  11.4 us (2%)
    psum x1, waiting for transfers between devices, on_device(): summed = lax.psum(box_rows, 'term')  203 us
    ppermute x20, waiting for transfers between devices, from_behind(): return lax.ppermute(block, axis, route)  199 us
    ppermute x20, starting transfers between devices, from_behind(): return lax.ppermute(block, axis, route)  50.7 us
    dot_general x4, matrix products, sweep(): jnp.einsum('fxvw,xu->fuvw', wider_x, matrix, preferred_element_type=jnp.f...  27.4 us
    reshape x2, local copies, waits for them, and re-layouts, to_cells(): cube = box_rows.reshape(amount, 2, 2, 2, breadth, breadth, breadth)  27.4 us
    dot_general x4, matrix products, sweep(): jnp.einsum('fxyz,zw->fxyw', extended_z, matrix, preferred_element_type=jn...  20.5 us
    ppermute x6, local copies, waits for them, and re-layouts, from_behind(): return lax.ppermute(block, axis, route)  19.9 us
    transpose x1, local copies, waits for them, and re-layouts, from_cells(): cube = cube.transpose(0, 1, 3, 5, 2, 4, 6)  17.7 us
  transfers between devices with their start and end apart: 21, of which 13 were waited for; matrix products, arithmetic and copies ran while one was open for 15% of the time, Pallas kernels for 0%

commit v1 on v0

v1 whole, which is shorter than its diff:
```python
import jax
import jax.numpy as jnp
from jax import lax
from jax.experimental import pallas as pl
from jax.experimental.pallas import tpu as pltpu
from jax.sharding import PartitionSpec as P

BF = jnp.bfloat16
F32 = jnp.float32
INTERPRET = False
PARAMS = dict(compiler_params=pltpu.CompilerParams(vmem_limit_bytes=56 * 1024 * 1024))


def dot(a, b):
    return jnp.dot(a, b, preferred_element_type=F32)


def dot_t(a, b):
    return lax.dot_general(a, b, (((1,), (1,)), ((), ())), preferred_element_type=F32)


def split(value):
    hi = value.astype(BF)
    return hi, (value - hi.astype(F32)).astype(BF)


def call(kernel, outs, scratch=(), name=None):
    return pl.pallas_call(
        kernel,
        out_shape=outs,
        scratch_shapes=list(scratch),
        interpret=INTERPRET,
        name=name,
        **PARAMS,
    )


def lane_eye(count):
    return jnp.eye(count, dtype=BF)


def fine_weights(fb):
    placed = jnp.stack(
        [jnp.pad(fb, ((0, 0), (0, 1), (0, 0), (0, 0))), jnp.pad(fb, ((0, 0), (1, 0), (0, 0), (0, 0)))],
        axis=3,
    )
    wz = (
        placed[:, :, None, :, None] * lane_eye(4)[None, None, :, None, :, None, None]
    ).reshape(8, 512, 256)
    wx = placed.transpose(0, 3, 4, 1, 2).reshape(8, 64, 128)
    flipped = fb[:, ::-1]
    spread = jnp.stack(
        [jnp.pad(flipped, ((0, 0), (0, 1), (0, 0), (0, 0))), jnp.pad(flipped, ((0, 0), (1, 0), (0, 0), (0, 0)))],
        axis=1,
    )
    my = spread.reshape(8, 2, 4, 16, 2, 32).transpose(4, 2, 5, 0, 1, 3).reshape(256, 256)
    return wz, wx, my


def coarse_weights(cb):
    wz = (
        cb[:, :, None, :, None, :] * lane_eye(4)[None, None, :, None, :, None]
    ).reshape(4, 2, 384, 128).transpose(0, 2, 1, 3).reshape(4, 384, 256)
    wx = cb.transpose(0, 3, 1, 2).reshape(8, 32, 96)
    my = cb[:, ::-1].reshape(8, 3, 8, 4, 32).transpose(3, 1, 4, 0, 2).reshape(384, 64)
    return wz, wx, my


def scale_weights(two_scale):
    fz = (
        two_scale.T.reshape(2, 1, 32, 1, 32) * lane_eye(4)[None, :, None, :, None]
    ).reshape(256, 128)
    ky = (two_scale.T[:, None, :, None] * lane_eye(32)[None, :, None, :]).reshape(2048, 1024)
    st2 = jnp.concatenate([two_scale.T, two_scale.T], axis=1)
    return fz, ky, st2


def parent_kernel(own, fz, ky, s, out, rows, wide):
    for yg in range(16):
        cy, g = divmod(yg, 8)
        for cx in range(2):
            for cz in range(2):
                rows[yg * 64 + cx * 32 : yg * 64 + cx * 32 + 32, cz * 128 : cz * 128 + 128] = own[
                    4 * cx + 2 * cy + cz, :, g * 128 : g * 128 + 128
                ]
    along_z = dot(rows[...], fz[...]).astype(BF)
    for yg in range(16):
        wide[:, yg * 128 : yg * 128 + 128] = along_z[yg * 64 : yg * 64 + 64]
    along_y = dot(wide[...], ky[...]).astype(BF)
    out[...] = dot(s[...], along_y).astype(BF)


def parents_of(own, fz, ky, s):
    return call(
        parent_kernel,
        jax.ShapeDtypeStruct((32, 1024), BF),
        [pltpu.VMEM((1024, 256), BF), pltpu.VMEM((64, 2048), BF)],
        "parents",
    )(own, fz, ky, s)


def main_kernel(
    own, zm, zp, xm_own, xp_own, xm_far, xp_far, par, czm, czp,
    wz, wx, my, cwz, cwx, cmy,
    out, send_up, send_dn, out_c,
    left, mid, wide, done, left_c, mid_c, wide_c, done_c,
):
    for cy in range(2):
        sources = [
            [xm_far[cy], xm_own[2 * cy], xm_own[2 * cy + 1], xm_far[2 + cy]],
            [zm[cy], own[2 * cy], own[2 * cy + 1], zp[cy]],
            [zm[2 + cy], own[4 + 2 * cy], own[5 + 2 * cy], zp[2 + cy]],
            [xp_far[cy], xp_own[2 * cy], xp_own[2 * cy + 1], xp_far[2 + cy]],
        ]
        for xb in range(4):
            for zb in range(4):
                box = sources[xb][zb]
                for g in range(8):
                    row = (cy * 8 + g) * 128 + xb * 32
                    left[row : row + 32, zb * 128 : zb * 128 + 128] = box[:, g * 128 : g * 128 + 128]

    def fine_term(t, carry):
        weight = wz[t]
        for m in range(4):
            passed = dot(left[m * 512 : m * 512 + 512, :], weight).astype(BF)
            mid[m * 4 : m * 4 + 4] = passed.reshape(4, 128, 256)
        weight_x = wx[t]
        for yg in range(16):
            passed = dot(weight_x, mid[yg])
            base = (t * 32 + 2 * yg) * 64
            wide[pl.ds(base, 64), :] = passed[:, :128]
            wide[pl.ds(base + 64, 64), :] = passed[:, 128:]
        return carry

    lax.fori_loop(0, 8, fine_term, 0)

    def fine_rows(k, carry):
        u = 2 * k
        data = jnp.concatenate(
            [wide[pl.ds(u, 256, stride=64), :].astype(BF), wide[pl.ds(u + 1, 256, stride=64), :].astype(BF)], axis=1
        )
        passed = dot(my[...], data)
        for i in range(2):
            lanes = passed[:, i * 128 : i * 128 + 128]
            base = pl.multiple_of((u + i) * 128, 128)
            done[pl.ds(base, 128), :] = lanes[:128] + pltpu.roll(lanes[128:], 64, 1)
        return carry

    lax.fori_loop(0, 32, fine_rows, 0)

    lane64 = lax.broadcasted_iota(jnp.int32, (64, 128), 1) // 32

    def fine_lanes(g, carry):
        at = pl.multiple_of(g * 128, 128)
        for vb in range(4):
            parts = [done[pl.ds(vb * 32 + 4 * g + j, 64, stride=128), :] for j in range(4)]
            for cz in range(2):
                block = parts[0] if cz == 0 else pltpu.roll(parts[0], 96, 1)
                for j in range(1, 4):
                    turn = (32 * (j - cz)) % 128
                    moved = pltpu.roll(parts[j], turn, 1) if turn else parts[j]
                    block = jnp.where(lane64 == j, moved, block)
                for cx in range(2):
                    piece = block[cx * 32 : cx * 32 + 32]
                    if vb == 0:
                        send_dn[2 * cx + cz, :, pl.ds(at, 128)] = piece.astype(BF)
                    elif vb == 3:
                        send_up[2 * cx + cz, :, pl.ds(at, 128)] = piece.astype(BF)
                    else:
                        out[4 * cx + 2 * (vb - 1) + cz, :, pl.ds(at, 128)] = piece
        return carry

    lax.fori_loop(0, 8, fine_lanes, 0)

    sources = [
        [xm_far[5], xm_far[4], xm_far[6]],
        [czm[...], par[...], czp[...]],
        [xp_far[5], xp_far[4], xp_far[6]],
    ]
    for xb in range(3):
        for zb in range(3):
            for g in range(8):
                row = g * 96 + xb * 32
                left_c[row : row + 32, zb * 128 : zb * 128 + 128] = sources[xb][zb][:, g * 128 : g * 128 + 128]

    def coarse_pair(h, carry):
        passed = dot(left_c[...], cwz[h]).astype(BF)
        mid_c[...] = passed.reshape(8, 96, 256)
        for i in range(2):
            weight_x = cwx[2 * h + i]
            for g in range(0, 8, 2):
                data = jnp.concatenate(
                    [mid_c[g, :, i * 128 : i * 128 + 128], mid_c[g + 1, :, i * 128 : i * 128 + 128]], axis=1
                )
                moved = dot(weight_x, data)
                base = ((2 * h + i) * 8 + g) * 32
                wide_c[pl.ds(base, 32), :] = moved[:, :128]
                wide_c[pl.ds(base + 32, 32), :] = moved[:, 128:]
        return carry

    lax.fori_loop(0, 4, coarse_pair, 0)

    def coarse_rows(k, carry):
        u = 2 * k
        data = jnp.concatenate(
            [wide_c[pl.ds(u, 64, stride=32), :].astype(BF), wide_c[pl.ds(u + 1, 64, stride=32), :].astype(BF)], axis=1
        )
        passed = dot(cmy[...], data)
        for i in range(2):
            lanes = passed[:, i * 128 : i * 128 + 128]
            total = lanes[:96]
            for j in range(1, 4):
                total = total + pltpu.roll(lanes[j * 96 : j * 96 + 96], 128 - 32 * j, 1)
            base = pl.multiple_of((u + i) * 96, 32)
            done_c[pl.ds(base, 96), :] = total
        return carry

    lax.fori_loop(0, 16, coarse_rows, 0)

    lane32 = lax.broadcasted_iota(jnp.int32, (32, 128), 1) // 32

    def coarse_lanes(g, carry):
        at = pl.multiple_of(g * 128, 128)
        for vb in range(3):
            block = done_c[pl.ds(vb * 32 + 4 * g, 32, stride=96), :]
            for j in range(1, 4):
                part = done_c[pl.ds(vb * 32 + 4 * g + j, 32, stride=96), :]
                block = jnp.where(lane32 == j, pltpu.roll(part, 32 * j, 1), block)
            if vb == 0:
                send_dn[4, :, pl.ds(at, 128)] = block.astype(BF)
            elif vb == 2:
                send_up[4, :, pl.ds(at, 128)] = block.astype(BF)
            else:
                out_c[:, pl.ds(at, 128)] = block
        return carry

    lax.fori_loop(0, 8, coarse_lanes, 0)


def passes(*operands):
    return call(
        main_kernel,
        (
            jax.ShapeDtypeStruct((8, 32, 1024), F32),
            jax.ShapeDtypeStruct((5, 32, 1024), BF),
            jax.ShapeDtypeStruct((5, 32, 1024), BF),
            jax.ShapeDtypeStruct((32, 1024), F32),
        ),
        [
            pltpu.VMEM((2048, 512), BF),
            pltpu.VMEM((16, 128, 256), BF),
            pltpu.VMEM((16384, 128), F32),
            pltpu.VMEM((8192, 128), F32),
            pltpu.VMEM((768, 384), BF),
            pltpu.VMEM((8, 96, 256), BF),
            pltpu.VMEM((2048, 128), F32),
            pltpu.VMEM((3072, 128), F32),
        ],
        "passes",
    )(*operands)


def final_kernel(own, own_c, low, high, fz, ky, st2, out, rows, mixed, deep):
    total = own_c[...] + low[4].astype(F32) + high[4].astype(F32)
    hi, lo = split(total)
    for g in range(8):
        rows[g * 64 : g * 64 + 32, :] = hi[:, g * 128 : g * 128 + 128]
        rows[g * 64 + 32 : g * 64 + 64, :] = lo[:, g * 128 : g * 128 + 128]
    along_z = dot_t(rows[...], fz[...])
    for g in range(8):
        both = along_z[g * 64 : g * 64 + 32] + along_z[g * 64 + 32 : g * 64 + 64]
        hi, lo = split(both)
        for cz in range(2):
            mixed[cz * 64 : cz * 64 + 32, g * 128 : g * 128 + 128] = hi[:, cz * 128 : cz * 128 + 128]
            mixed[cz * 64 + 32 : cz * 64 + 64, g * 128 : g * 128 + 128] = lo[:, cz * 128 : cz * 128 + 128]
    along_y = dot_t(mixed[...], ky[...])
    for cz in range(2):
        hi, lo = split(along_y[cz * 64 : cz * 64 + 32] + along_y[cz * 64 + 32 : cz * 64 + 64])
        deep[:32, :] = hi
        deep[32:, :] = lo
        along_x = dot(st2[...], deep[...])
        for cx in range(2):
            for cy in range(2):
                added = (low if cy == 0 else high)[2 * cx + cz].astype(F32)
                spread = along_x[cx * 32 : cx * 32 + 32, cy * 1024 : cy * 1024 + 1024]
                box = 4 * cx + 2 * cy + cz
                out[box] = (own[box] + spread + added).astype(BF)


def finish(*operands):
    return call(
        final_kernel,
        jax.ShapeDtypeStruct((8, 32, 1024), BF),
        [pltpu.VMEM((512, 128), BF), pltpu.VMEM((128, 1024), BF), pltpu.VMEM((64, 2048), BF)],
        "finish",
    )(*operands)


def shift(block, distance):
    count = lax.axis_size("box")
    return lax.ppermute(block, "box", [(i, (i + distance) % count) for i in range(count)])


def crosses(p, step):
    return (p % 2 == 1) if step == 1 else (p % 2 == 0)


def shift_z(block, step):
    boxes, groups = lax.axis_size("box"), lax.axis_size("term")
    route = []
    for p in range(boxes):
        for t in range(groups):
            to = groups - 1 - t if crosses(p, step) else t
            route.append((p * groups + t, ((p + step) % boxes) * groups + to))
    return lax.ppermute(block, ("box", "term"), route)


def z_layer(fine_coeffs, step, p, t):
    other = lax.axis_size("term") - 1 - t
    cross = (p % 2 == 1) if step == 1 else (p % 2 == 0)
    chosen = lax.dynamic_index_in_dim(fine_coeffs, jnp.where(cross, other, t), 0, False)
    layer = chosen.reshape(4, 2, 32, 1024)[:, 1 if step == 1 else 0]
    return shift_z(layer, step)


def on_device(fine_coeffs, fine_blocks, coarse_blocks, two_scale, term_exponent):
    p = lax.axis_index("box")
    t = lax.axis_index("term")
    zm = z_layer(fine_coeffs, 1, p, t)
    zp = z_layer(fine_coeffs, -1, p, t)
    own = lax.dynamic_index_in_dim(fine_coeffs, t, 0, False)
    xm_own = shift(own[4:], 16)
    xp_own = shift(own[:4], -16)

    fz, ky, st2 = scale_weights(two_scale)
    par = parents_of(own, fz, ky, two_scale)
    czm = shift(par, 1)
    czp = shift(par, -1)

    far_up = jnp.concatenate([zm[2:], zp[2:], par[None], czm[None], czp[None]], axis=0)
    far_dn = jnp.concatenate([zm[:2], zp[:2], par[None], czm[None], czp[None]], axis=0)
    xm_far = shift(far_up, 16)
    xp_far = shift(far_dn, -16)

    wz, wx, my = fine_weights(jnp.take(fine_blocks, term_exponent, axis=0))
    cwz, cwx, cmy = coarse_weights(jnp.take(coarse_blocks, term_exponent, axis=0))
    out, send_up, send_dn, out_c = passes(
        own, zm, zp, xm_own, xp_own, xm_far, xp_far, par, czm, czp, wz, wx, my, cwz, cwx, cmy
    )
    low = shift(send_up, 4)
    high = shift(send_dn, -4)
    total = finish(out, out_c, low, high, fz, ky, st2)
    groups = lax.axis_size("term")
    mine = lax.all_to_all(total.reshape(groups, 2, 32, 1024), "term", 0, 0)
    return mine.astype(F32)


def solution(mesh):
    placed = (P(None, "box", None, None), P(), P(), P(), P())
    return jax.shard_map(
        on_device,
        mesh=mesh,
        in_specs=placed,
        out_specs=P(None, ("box", "term"), None, None),
        check_vma=False,
    )
```

time: 729 us -> 190 us (0.26); the launches traced: 718 us -> 189 us
  waiting for transfers between devices: 402 us -> 20.4 us
  local copies, waits for them, and re-layouts: 160 us -> 78.1 us
  matrix products: 79.9 us -> 0 us
  Pallas kernels: 0 us -> 44.8 us
  starting transfers between devices: 50.7 us -> 19.6 us
  blocking collectives: 0 us -> 14.9 us
  between operations: 14.3 us -> 0.28 us
    psum x1 -> x0, waiting for transfers between devices: 203 us -> none  [on_device(): summed = lax.psum(box_rows, 'term')]
    ppermute x20 -> x10, waiting for transfers between devices: 199 us -> 20.4 us  [the longest x8 20.4 us: shift(): lax.ppermute(block, 'box', [(i, (i + distance) % count) for i in range(co...]
    dot_general x19 -> x0, matrix products: 79.9 us -> none  [the longest x4 27.4 us: sweep(): jnp.einsum('fxvw,xu->fuvw', wider_x, matrix, preferred_element_type=jnp.f...]
    reshape x5 -> x7, local copies, waits for them, and re-layouts: 72.4 us -> 5.73 us  [the longest x3 2.01 us: coarse_weights(): cb[:, ::-1].reshape(8, 3, 8, 4, 32).transpose(3, 1, 4, 0, 2)]
    mul x0 -> x10, local copies, waits for them, and re-layouts: none -> 59.8 us  [the longest x4 29.5 us: fine_weights(): placed[:, :, None, :, None]]
    pallas_call x0 -> x3, Pallas kernels: none -> 44.8 us  [the longest x1 35.5 us: passes(): call(main_kernel, (jax.ShapeDtypeStruct((8, 32, 1024), F32), jax.ShapeDty...]
    ppermute x20 -> x10, starting transfers between devices: 50.7 us -> 19.6 us  [the longest x8 15.7 us: shift(): lax.ppermute(block, 'box', [(i, (i + distance) % count) for i in range(co...]
    slice x9 -> x1, local copies, waits for them, and re-layouts: 28.6 us -> 0.84 us  [on_device(): xp_own = shift(own[:4], -16)]
  transfers between devices with their start and end apart: 21 -> 10, of which waited for: 13 -> 4; matrix products, arithmetic and copies ran while one was open for 15% -> 29% of each run, Pallas kernels for 0% -> 0%
where the time goes in v1:
time: 190 us; the launch traced here: 189 us
  local copies, waits for them, and re-layouts  78.1 us (41%)
  Pallas kernels  44.8 us (24%)
  waiting for transfers between devices  20.4 us (11%)
  starting transfers between devices  19.6 us (10%)
  blocking collectives  14.9 us (8%)
  other arithmetic  11.2 us (6%)
    pallas_call x1, Pallas kernels, passes(): call(main_kernel, (jax.ShapeDtypeStruct((8, 32, 1024), F32), jax.ShapeDty...  35.5 us
    mul x4, local copies, waits for them, and re-layouts, fine_weights(): placed[:, :, None, :, None]  29.5 us
    mul x1, local copies, waits for them, and re-layouts, scale_weights(): two_scale.T[:, None, :, None] * lane_eye(32)[None, :, None, :]  23.4 us
    ppermute x8, waiting for transfers between devices, shift(): lax.ppermute(block, 'box', [(i, (i + distance) % count) for i in range(co...  20.4 us
    ppermute x8, starting transfers between devices, shift(): lax.ppermute(block, 'box', [(i, (i + distance) % count) for i in range(co...  15.7 us
    all_to_all x1, blocking collectives, on_device(): mine = lax.all_to_all(total.reshape(groups, 2, 32, 1024), 'term', 0, 0)  14.9 us
    mul x4, local copies, waits for them, and re-layouts, coarse_weights(): cb[:, :, None, :, None, :] * lane_eye(4)[None, None, :, None, :, None]  6.13 us
    mul x1, other arithmetic, scale_weights(): two_scale.T[:, None, :, None] * lane_eye(32)[None, :, None, :]  5.97 us
  transfers between devices with their start and end apart: 10, of which 4 were waited for; matrix products, arithmetic and copies ran while one was open for 29% of the time, Pallas kernels for 0%

profile of v1, /device:TPU:30, one launch (start us, length us, event | category | flops | bytes accessed | tf_op | source)
XLA Modules:
  0.0 189.3 jit_solution(10853735476469318144)
XLA Ops:
  0.0 0.8 copy.15
  1.0 0.8 mul.80.fz
  1.9 6.0 %broadcast_multiply_fusion = bf16[64,32,32,32]{3,2,1,0:T(8,128)(2,1)} fusion(bf16[32,32]{1,0:T(8,128)(2,1)S(1)} %fusion, bf16[64,32]{1,0:T(8,128)(2,1)S(1)} %bitcast.67), kind=kLoop, calls=%fused_computation.2 | loop fusion | flops 2097152 | bytes 4200448 | tf_op jit(solution)/shard_map/mul | solution.py:73
  7.8 23.4 %mul.84.ky = bf16[2048,1024]{1,0:T(8,128)(2,1)} reshape(bf16[64,32,32,32]{3,2,1,0:T(8,128)(2,1)} %broadcast_multiply_fusion) | data formatting | bytes 8388608 | tf_op jit(solution)/shard_map/mul | solution.py:73
  31.2 1.0 constant_dynamic-slice_fusion
  32.2 4.0 %parents.1.par = bf16[32,1024]{1,0:T(8,128)(2,1)} custom-call(bf16[8,32,1024]{2,1,0:T(8,128)(2,1)} %get-tuple-element.17.own, bf16[256,128]{1,0:T(8,128)(2,1)} %mul.80.fz, bf16[2048,1024]{1,0:T(8,128)(2,1)} %mul.84.ky, bf16[32,64]{1,0:T(8,128)(2,1)} %s.1), custom_call_target="tpu_custom_call" | custom-call | tf_op jit(solution)/shard_map/parents/pallas_call | solution.py:94
  36.2 7.0 %collective-permute-start.5 = (bf16[32,1024]{1,0:T(8,128)(2,1)}, bf16[32,1024]{1,0:T(8,128)(2,1)}, u32[]{:S(2)}, u32[]{:S(2)}) collective-permute-start(bf16[32,1024]{1,0:T(8,128)(2,1)} %parents.1.par), channel_id=1, source_target_pairs={{0,252},{4,0},{8,4},{12,8},{16,12},{20,16},{24,20},{28,24},{32,28}... | collective-permute-start | bytes 196616 | tf_op jit(solution)/shard_map/ppermute | solution.py:301
  43.2 0.7 slice_bitcast_fusion.1
  44.2 0.7 slice_bitcast_fusion
  45.0 3.5 %collective-permute-start.1 = (bf16[4,32,1024]{2,1,0:T(8,128)(2,1)}, bf16[4,32,1024]{2,1,0:T(8,128)(2,1)}, u32[]{:S(2)}, u32[]{:S(2)}) collective-permute-start(bf16[4,32,1024]{2,1,0:T(8,128)(2,1)} %slice_bitcast_fusion), channel_id=1, source_target_pairs={{0,255},{1,254},{2,253},{3,252},{4,0},{5,1},{6,2},{7,3},{8,7},{9,6... | collective-permute-start | bytes 786440 | tf_op jit(solution)/shard_map/ppermute | solution.py:315
  48.5 0.8 dynamic-slice_bitcast_fusion.1
  49.6 0.6 gather_fusion
  50.2 0.6 gather_fusion.1
  52.1 0.5 copy.16
  52.6 5.7 %mul.85 = bf16[8,4,4,32,4,2,32]{6,5,4,3,2,1,0:T(2,128)(2,1)} broadcast(bf16[8,4,32,2,32]{4,3,2,1,0:T(2,128)(2,1)S(1)} %copy.16), dimensions={0,1,3,5,6} | broadcast | bytes 2228224 | tf_op jit(solution)/shard_map/mul | solution.py:48
  58.3 21.7 %mul.86 = bf16[8,512,256]{2,1,0:T(8,128)(2,1)} reshape(bf16[8,4,4,32,4,2,32]{6,5,4,3,2,1,0:T(2,128)(2,1)} %mul.85) | data formatting | bytes 4194304 | tf_op jit(solution)/shard_map/mul | solution.py:48
  80.0 0.6 mul.87
  80.7 1.4 mul.88
  82.4 0.9 reshape.94.wx
  83.7 0.8 copy.23.my
  84.5 0.7 rev.7
  85.1 2.5 %mul.91 = bf16[8,3,4,32,4,32]{5,4,3,2,1,0:T(4,128)(2,1)S(1)} broadcast(bf16[8,3,32,32]{3,2,1,0:T(8,128)(2,1)} %copy-done.2), dimensions={0,1,3,5} | broadcast | bytes 835584 | tf_op jit(solution)/shard_map/mul | solution.py:62
  87.6 2.5 %mul.92 = bf16[4,2,384,128]{3,2,1,0:T(8,128)(2,1)} reshape(bf16[8,3,4,32,4,32]{5,4,3,2,1,0:T(4,128)(2,1)S(1)} %mul.91) | data formatting | bytes 1572864 | tf_op jit(solution)/shard_map/mul | solution.py:62
  90.1 1.0 mul.93
  91.3 1.1 copy.31
  92.6 0.7 copy.24.cmy
  93.3 1.7 copy.25.cwx
  95.0 1.8 collective-permute-start.3
  96.8 1.0 slice_dynamic-update-slice_fusion.1
  97.8 1.0 slice_dynamic-update-slice_fusion
  98.8 0.9 bitcast_dynamic-update-slice_fusion.2
  99.7 0.9 bitcast_dynamic-update-slice_fusion
  100.5 1.5 collective-permute-start.6
  102.0 0.6 collective-permute-start.7
  102.6 1.5 broadcast_multiply_fusion.1.wz
  104.2 1.1 copy_bitcast_fusion.cwz
  105.3 8.0 %collective-permute-done.6.xm_far = bf16[7,32,1024]{2,1,0:T(8,128)(2,1)S(1)} collective-permute-done((bf16[7,32,1024]{2,1,0:T(8,128)(2,1)S(1)}, bf16[7,32,1024]{2,1,0:T(8,128)(2,1)S(1)}, u32[]{:S(2)}, u32[]{:S(2)}) %collective-permute-start.6) | collective-permute-done | bytes 458784 | tf_op jit(solution)/shard_map/ppermute | solution.py:301
  113.3 2.4 %collective-permute-done.7.xp_far = bf16[7,32,1024]{2,1,0:T(8,128)(2,1)S(1)} collective-permute-done((bf16[7,32,1024]{2,1,0:T(8,128)(2,1)S(1)}, bf16[7,32,1024]{2,1,0:T(8,128)(2,1)S(1)}, u32[]{:S(2)}, u32[]{:S(2)}) %collective-permute-start.7) | collective-permute-done | bytes 458784 | tf_op jit(solution)/shard_map/ppermute | solution.py:301
  115.7 0.8 copy-done.8
  116.5 35.5 %passes.1 = (f32[8,32,1024]{2,1,0:T(8,128)}, bf16[5,32,1024]{2,1,0:T(8,128)(2,1)}, bf16[5,32,1024]{2,1,0:T(8,128)(2,1)}, f32[32,1024]{1,0:T(8,128)}) custom-call(bf16[8,32,1024]{2,1,0:T(8,128)(2,1)} %get-tuple-element.17.own, bf16[4,32,1024]{2,1,0:T(8,128)(2,1)} %collective-permute-done.zm, bf16[4,32,1024]{2,1,0:T(8,128)(2,1)} %collective-permute-done.1.zp, ...), custom_call_target="tpu_custom_call" | custom-call | tf_op jit(solution)/shard_map/passes/pallas_call | solution.py:241
  152.0 4.6 %collective-permute-start.8 = (bf16[5,32,1024]{2,1,0:T(8,128)(2,1)}, bf16[5,32,1024]{2,1,0:T(8,128)(2,1)S(1)}, u32[]{:S(2)}, u32[]{:S(2)}) collective-permute-start(bf16[5,32,1024]{2,1,0:T(8,128)(2,1)} %get-tuple-element.12), channel_id=1, source_target_pairs={{0,16},{4,20},{8,24},{12,28},{16,32},{20,36},{24,40},{28,44},{32,4... | collective-permute-start | bytes 983048 | tf_op jit(solution)/shard_map/ppermute | solution.py:301
  156.6 0.7 pad_maximum_fusion.1.st2
  157.3 4.2 %collective-permute-done.8.low = bf16[5,32,1024]{2,1,0:T(8,128)(2,1)S(1)} collective-permute-done((bf16[5,32,1024]{2,1,0:T(8,128)(2,1)}, bf16[5,32,1024]{2,1,0:T(8,128)(2,1)S(1)}, u32[]{:S(2)}, u32[]{:S(2)}) %collective-permute-start.8) | collective-permute-done | bytes 327712 | tf_op jit(solution)/shard_map/ppermute | solution.py:301
  161.5 5.7 %collective-permute-done.9.high = bf16[5,32,1024]{2,1,0:T(8,128)(2,1)S(1)} collective-permute-done((bf16[5,32,1024]{2,1,0:T(8,128)(2,1)}, bf16[5,32,1024]{2,1,0:T(8,128)(2,1)S(1)}, u32[]{:S(2)}, u32[]{:S(2)}) %collective-permute-start.9) | collective-permute-done | bytes 327712 | tf_op jit(solution)/shard_map/ppermute | solution.py:301
  167.2 0.8 copy-done.10
  167.9 5.3 %finish.1 = bf16[8,32,1024]{2,1,0:T(8,128)(2,1)} custom-call(f32[8,32,1024]{2,1,0:T(8,128)} %get-tuple-element.10.own, f32[32,1024]{1,0:T(8,128)} %get-tuple-element.11.own_c, bf16[5,32,1024]{2,1,0:T(8,128)(2,1)} %copy-done.9, bf16[5,32,1024]{2,1,0:T(8,128)(2,1)} %copy-done.10, bf16[256,128]{1,0:T(8,128)(2,1)} %mul.80.fz, bf16[2048,1024]{1,0:T(8,128)(2,1)} %mul.84.ky, ...), custom_call_target="tpu_custom_call" | custom-call | tf_op jit(solution)/shard_map/finish/pallas_call | solution.py:291
  173.3 14.9 %all_to_all.5 = bf16[4,2,32,1024]{3,2,1,0:T(8,128)(2,1)S(1)} all-to-all(bf16[4,2,32,1024]{3,2,1,0:T(8,128)(2,1)} %bitcast.59), channel_id=1, replica_groups=mesh['box'=64,'term'=4] {'term'}, dimensions={0} | all-to-all | bytes 1048576 | tf_op jit(solution)/shard_map/all_to_all | solution.py:354
  188.2 1.1 convert_element_type.39
  (57 shorter events, 3.1 us)
Async XLA Ops:
  0.0 49.6 %copy-start = (bf16[16,3,32,32]{3,2,1,0:T(8,128)(2,1)S(1)}, bf16[16,3,32,32]{3,2,1,0:T(8,128)(2,1)}, u32[]{:S(2)}) copy-start(bf16[16,3,32,32]{3,2,1,0:T(8,128)(2,1)} %param.8) | copy-start | bytes 294916
  0.0 80.0 %copy-start.13 = (bf16[4,4]{1,0:T(4,128)(2,1)}, bf16[4,4]{1,0:T(4,128)(2,1)S(1)}, u32[]{:S(2)}) copy-start(bf16[4,4]{1,0:T(4,128)(2,1)S(1)} %fusion.1) | copy-start | bytes 100
  7.8 23.4 %copy-start.4 = (bf16[4,8,32,1024]{3,2,1,0:T(8,128)(2,1)S(1)}, bf16[4,8,32,1024]{3,2,1,0:T(8,128)(2,1)}, u32[]{:S(2)}) copy-start(bf16[4,8,32,1024]{3,2,1,0:T(8,128)(2,1)} %param.7) | copy-start | bytes 6291460
  36.2 13.3 %copy-start.14 = (s32[8]{0:T(128)S(1)}, s32[8]{0:T(128)}, u32[]{:S(2)}) copy-start(s32[8]{0:T(128)} %param.11) | copy-start | bytes 100
  36.2 14.0 %copy-start.12 = (bf16[16,3,32,32]{3,2,1,0:T(8,128)(2,1)S(1)}, bf16[16,3,32,32]{3,2,1,0:T(8,128)(2,1)}, u32[]{:S(2)}) copy-start(bf16[16,3,32,32]{3,2,1,0:T(8,128)(2,1)} %param.9) | copy-start | bytes 294916
  36.2 62.6 %collective-permute-start.4 = (bf16[32,1024]{1,0:T(8,128)(2,1)}, bf16[32,1024]{1,0:T(8,128)(2,1)}, u32[]{:S(2)}, u32[]{:S(2)}) collective-permute-start(bf16[32,1024]{1,0:T(8,128)(2,1)} %parents.1.par), channel_id=1, source_target_pairs={{0,4},{4,8},{8,12},{12,16},{16,20},{20,24},{24,28},{28,32},{32,36}... | collective-permute-start | bytes 196616 | tf_op jit(solution)/shard_map/ppermute | solution.py:301
  36.2 63.4 %collective-permute-start.5 = (bf16[32,1024]{1,0:T(8,128)(2,1)}, bf16[32,1024]{1,0:T(8,128)(2,1)}, u32[]{:S(2)}, u32[]{:S(2)}) collective-permute-start(bf16[32,1024]{1,0:T(8,128)(2,1)} %parents.1.par), channel_id=1, source_target_pairs={{0,252},{4,0},{8,4},{12,8},{16,12},{20,16},{24,20},{28,24},{32,28}... | collective-permute-start | bytes 196616 | tf_op jit(solution)/shard_map/ppermute | solution.py:301
  43.9 51.1 %collective-permute-start = (bf16[4,32,1024]{2,1,0:T(8,128)(2,1)}, bf16[4,32,1024]{2,1,0:T(8,128)(2,1)}, u32[]{:S(2)}, u32[]{:S(2)}) collective-permute-start(bf16[4,32,1024]{2,1,0:T(8,128)(2,1)} %slice_bitcast_fusion.1), channel_id=1, source_target_pairs={{0,4},{1,5},{2,6},{3,7},{4,11},{5,10},{6,9},{7,8},{8,12},{9,13},{1... | collective-permute-start | bytes 786440 | tf_op jit(solution)/shard_map/ppermute | solution.py:315
  45.0 52.8 %collective-permute-start.1 = (bf16[4,32,1024]{2,1,0:T(8,128)(2,1)}, bf16[4,32,1024]{2,1,0:T(8,128)(2,1)}, u32[]{:S(2)}, u32[]{:S(2)}) collective-permute-start(bf16[4,32,1024]{2,1,0:T(8,128)(2,1)} %slice_bitcast_fusion), channel_id=1, source_target_pairs={{0,255},{1,254},{2,253},{3,252},{4,0},{5,1},{6,2},{7,3},{8,7},{9,6... | collective-permute-start | bytes 786440 | tf_op jit(solution)/shard_map/ppermute | solution.py:315
  49.3 55.9 %collective-permute-start.2 = (bf16[4,32,1024]{2,1,0:T(8,128)(2,1)}, bf16[4,32,1024]{2,1,0:T(8,128)(2,1)}, u32[]{:S(2)}, u32[]{:S(2)}) collective-permute-start(bf16[4,32,1024]{2,1,0:T(8,128)(2,1)} %get-tuple-element.15), channel_id=1, source_target_pairs={{0,64},{4,68},{8,72},{12,76},{16,80},{20,84},{24,88},{28,92},{32,9... | collective-permute-start | bytes 786440 | tf_op jit(solution)/shard_map/ppermute | solution.py:301
  50.9 33.6 %copy-start.2 = (bf16[8,3,32,32]{3,2,1,0:T(8,128)(2,1)}, bf16[8,3,32,32]{3,2,1,0:T(8,128)(2,1)S(1)}, u32[]{:S(2)}) copy-start(bf16[8,3,32,32]{3,2,1,0:T(8,128)(2,1)S(1)} %get-tuple-element.35) | copy-start | bytes 147460
  90.1 8.7 %copy-start.6 = (bf16[32,1024]{1,0:T(8,128)(2,1)S(1)}, bf16[32,1024]{1,0:T(8,128)(2,1)}, u32[]{:S(2)}) copy-start(bf16[32,1024]{1,0:T(8,128)(2,1)} %parents.1.par) | copy-start | bytes 196612
  90.1 12.6 %copy-start.1 = (bf16[8,512,256]{2,1,0:T(8,128)(2,1)S(1)}, bf16[8,512,256]{2,1,0:T(8,128)(2,1)}, u32[]{:S(2)}) copy-start(bf16[8,512,256]{2,1,0:T(8,128)(2,1)} %mul.86) | copy-start | bytes 6291460
  90.1 12.6 %copy-start.5 = (bf16[512,256]{1,0:T(8,128)(2,1)S(1)}, bf16[512,256]{1,0:T(8,128)(2,1)}, u32[]{:S(2)}) copy-start(bf16[512,256]{1,0:T(8,128)(2,1)} %mul.88) | copy-start | bytes 786436
  95.0 10.3 %collective-permute-start.3 = (bf16[4,32,1024]{2,1,0:T(8,128)(2,1)}, bf16[4,32,1024]{2,1,0:T(8,128)(2,1)S(1)}, u32[]{:S(2)}, u32[]{:S(2)}) collective-permute-start(bf16[4,32,1024]{2,1,0:T(8,128)(2,1)} %get-tuple-element.14), channel_id=1, source_target_pairs={{0,192},{4,196},{8,200},{12,204},{16,208},{20,212},{24,216},{28,22... | collective-permute-start | bytes 786440 | tf_op jit(solution)/shard_map/ppermute | solution.py:301
  100.5 12.7 %collective-permute-start.6 = (bf16[7,32,1024]{2,1,0:T(8,128)(2,1)S(1)}, bf16[7,32,1024]{2,1,0:T(8,128)(2,1)S(1)}, u32[]{:S(2)}, u32[]{:S(2)}) collective-permute-start(bf16[7,32,1024]{2,1,0:T(8,128)(2,1)S(1)} %get-tuple-element.30), channel_id=1, source_target_pairs={{0,64},{4,68},{8,72},{12,76},{16,80},{20,84},{24,88},{28,92},{32,9... | collective-permute-start | bytes 1376264 | tf_op jit(solution)/shard_map/ppermute | solution.py:301
  102.0 2.1 %copy-start.3 = (bf16[4,2,384,128]{3,2,1,0:T(8,128)(2,1)S(1)}, bf16[4,2,384,128]{3,2,1,0:T(8,128)(2,1)}, u32[]{:S(2)}) copy-start(bf16[4,2,384,128]{3,2,1,0:T(8,128)(2,1)} %mul.92) | copy-start | bytes 2359300
  102.0 13.7 %collective-permute-start.7 = (bf16[7,32,1024]{2,1,0:T(8,128)(2,1)S(1)}, bf16[7,32,1024]{2,1,0:T(8,128)(2,1)S(1)}, u32[]{:S(2)}, u32[]{:S(2)}) collective-permute-start(bf16[7,32,1024]{2,1,0:T(8,128)(2,1)S(1)} %get-tuple-element.29), channel_id=1, source_target_pairs={{0,192},{4,196},{8,200},{12,204},{16,208},{20,212},{24,216},{28,22... | collective-permute-start | bytes 1376264 | tf_op jit(solution)/shard_map/ppermute | solution.py:301
  105.3 10.5 %copy-start.11 = (bf16[4,32,1024]{2,1,0:T(8,128)(2,1)}, bf16[4,32,1024]{2,1,0:T(8,128)(2,1)S(1)}, u32[]{:S(2)}) copy-start(bf16[4,32,1024]{2,1,0:T(8,128)(2,1)S(1)} %collective-permute-done.3.xp_own) | copy-start | bytes 786436
  113.3 2.4 %copy-start.7 = (bf16[7,32,1024]{2,1,0:T(8,128)(2,1)}, bf16[7,32,1024]{2,1,0:T(8,128)(2,1)S(1)}, u32[]{:S(2)}) copy-start(bf16[7,32,1024]{2,1,0:T(8,128)(2,1)S(1)} %collective-permute-done.6.xm_far) | copy-start | bytes 1376260
  115.7 0.8 copy-start.8
  152.0 9.5 %collective-permute-start.8 = (bf16[5,32,1024]{2,1,0:T(8,128)(2,1)}, bf16[5,32,1024]{2,1,0:T(8,128)(2,1)S(1)}, u32[]{:S(2)}, u32[]{:S(2)}) collective-permute-start(bf16[5,32,1024]{2,1,0:T(8,128)(2,1)} %get-tuple-element.12), channel_id=1, source_target_pairs={{0,16},{4,20},{8,24},{12,28},{16,32},{20,36},{24,40},{28,44},{32,4... | collective-permute-start | bytes 983048 | tf_op jit(solution)/shard_map/ppermute | solution.py:301
  156.6 10.6 %collective-permute-start.9 = (bf16[5,32,1024]{2,1,0:T(8,128)(2,1)}, bf16[5,32,1024]{2,1,0:T(8,128)(2,1)S(1)}, u32[]{:S(2)}, u32[]{:S(2)}) collective-permute-start(bf16[5,32,1024]{2,1,0:T(8,128)(2,1)} %get-tuple-element.13), channel_id=1, source_target_pairs={{0,240},{4,244},{8,248},{12,252},{16,0},{20,4},{24,8},{28,12},{32,... | collective-permute-start | bytes 983048 | tf_op jit(solution)/shard_map/ppermute | solution.py:301
  161.5 5.7 %copy-start.9 = (bf16[5,32,1024]{2,1,0:T(8,128)(2,1)}, bf16[5,32,1024]{2,1,0:T(8,128)(2,1)S(1)}, u32[]{:S(2)}) copy-start(bf16[5,32,1024]{2,1,0:T(8,128)(2,1)S(1)} %collective-permute-done.8.low) | copy-start | bytes 983044
  167.2 0.8 copy-start.10

commit v2 on v1

--- a/solution.py
+++ b/solution.py
@@ -5,6 +5,7 @@
 from jax.experimental.pallas import tpu as pltpu
 from jax.sharding import PartitionSpec as P
 
+
 BF = jnp.bfloat16
 F32 = jnp.float32
 INTERPRET = False
@@ -24,58 +25,112 @@
     return hi, (value - hi.astype(F32)).astype(BF)
 
 
-def call(kernel, outs, scratch=(), name=None):
+def call(kernel, outs, scratch=()):
+    return pl.pallas_call(kernel, out_shape=outs, scratch_shapes=list(scratch), interpret=INTERPRET, **PARAMS)
+
+
+def same(rows, columns, test):
+    i = lax.broadcasted_iota(jnp.int32, (rows, columns), 0)
+    j = lax.broadcasted_iota(jnp.int32, (rows, columns), 1)
+    return test(i, j).astype(F32).astype(BF)
+
+
+def weight_kernel(
+    exponents, fine, coarse,
+    wz, wx, my, cwz, cwx, cmy,
+    dense, turned, tall, dense_c, turned_c, tall_c,
+):
+    wz[...] = jnp.zeros(wz.shape, BF)
+    cwz[...] = jnp.zeros(cwz.shape, BF)
+    dense[...] = jnp.zeros(dense.shape, F32)
+    turned[...] = jnp.zeros(turned.shape, F32)
+    eye = same(128, 128, lambda i, j: i == j)
+    by_parity = same(64, 64, lambda i, j: j == 2 * (i % 32) + i // 32)
+    by_four = same(32, 32, lambda i, j: j == 4 * (i % 8) + i // 8)
+
+    def term(t, carry):
+        e = exponents[t]
+        for d in range(3):
+            block = fine[e, d]
+            for child in range(2):
+                source = d + child
+                for y in range(4):
+                    row, column = source * 128 + y * 32, y * 64 + child * 32
+                    wz[t, row : row + 32, column : column + 32] = block
+                wide_block = block.astype(F32)
+                dense[source * 32 : source * 32 + 32, child * 32 : child * 32 + 32] = wide_block
+                target = 2 + child - d
+                turned[child * 32 : child * 32 + 32, target * 32 : target * 32 + 32] = wide_block
+        wx[t] = dot_t(eye[:64, :64], dense[...].astype(BF)).astype(BF)
+        chosen = dot(by_parity, turned[...].astype(BF))
+        for parity in range(2):
+            tall[parity, pl.ds(t * 32, 32), :] = chosen[parity * 32 : parity * 32 + 32]
+        for d in range(3):
+            block = coarse[e, d]
+            dense_c[d * 32 : d * 32 + 32, :] = block.astype(F32)
+            turned_c[:, (2 - d) * 32 : (2 - d) * 32 + 32] = block.astype(F32)
+            for y in range(4):
+                cwz[t, d * 128 + y * 32 : d * 128 + y * 32 + 32, y * 32 : y * 32 + 32] = block
+        cwx[t] = dot_t(eye[:32, :32], dense_c[...].astype(BF)).astype(BF)
+        chosen = dot(by_four, turned_c[...].astype(BF))
+        for parity in range(4):
+            tall_c[parity, pl.ds(t * 8, 8), :] = chosen[parity * 8 : parity * 8 + 8]
+        return carry
+
+    lax.fori_loop(0, 8, term, 0)
+    for parity in range(2):
+        my[parity * 128 : parity * 128 + 128, :] = dot_t(eye, tall[parity].astype(BF)).astype(BF)
+    for parity in range(4):
+        cmy[parity * 96 : parity * 96 + 96, :] = dot_t(eye[:96, :96], tall_c[parity].astype(BF)).astype(BF)
+
+
+def weights(exponents, fine, coarse):
+    whole = pl.BlockSpec(memory_space=pltpu.VMEM)
     return pl.pallas_call(
-        kernel,
-        out_shape=outs,
-        scratch_shapes=list(scratch),
+        weight_kernel,
+        out_shape=(
+            jax.ShapeDtypeStruct((8, 512, 256), BF),
+            jax.ShapeDtypeStruct((8, 64, 128), BF),
+            jax.ShapeDtypeStruct((256, 256), BF),
+            jax.ShapeDtypeStruct((8, 384, 128), BF),
+            jax.ShapeDtypeStruct((8, 32, 96), BF),
+            jax.ShapeDtypeStruct((384, 64), BF),
+        ),
+        in_specs=[pl.BlockSpec(memory_space=pltpu.SMEM), whole, whole],
+        scratch_shapes=[
+            pltpu.VMEM((128, 64), F32),
+            pltpu.VMEM((64, 128), F32),
+            pltpu.VMEM((2, 256, 128), F32),
+            pltpu.VMEM((96, 32), F32),
+            pltpu.VMEM((32, 96), F32),
+            pltpu.VMEM((4, 64, 96), F32),
+        ],
         interpret=INTERPRET,
-        name=name,
+        name="weights",
         **PARAMS,
+    )(exponents, fine, coarse)
+
+
+def parent_kernel(own, s, out, fz, ky, st2, rows, wide):
+    scale = s[...]
+    tiled = lax.dot_general(
+        scale, same(32, 128, lambda i, j: j % 32 == i), (((0,), (0,)), ((), ())), preferred_element_type=F32
     )
-
-
-def lane_eye(count):
-    return jnp.eye(count, dtype=BF)
-
-
-def fine_weights(fb):
-    placed = jnp.stack(
-        [jnp.pad(fb, ((0, 0), (0, 1), (0, 0), (0, 0))), jnp.pad(fb, ((0, 0), (1, 0), (0, 0), (0, 0)))],
-        axis=3,
+    block = same(128, 128, lambda i, j: i // 32 == j // 32).astype(F32)
+    for cz in range(2):
+        part = tiled[cz * 32 : cz * 32 + 32]
+        fz[cz * 128 : cz * 128 + 128, :] = (jnp.concatenate([part] * 4, axis=0) * block).astype(BF)
+    st2[...] = lax.dot_general(
+        scale, same(32, 64, lambda i, j: j % 32 == i), (((0,), (0,)), ((), ())), preferred_element_type=F32
+    ).astype(BF)
+    spread = lax.dot_general(
+        scale, same(32, 1024, lambda i, j: j // 32 == i), (((0,), (0,)), ((), ())), preferred_element_type=F32
     )
-    wz = (
-        placed[:, :, None, :, None] * lane_eye(4)[None, None, :, None, :, None, None]
-    ).reshape(8, 512, 256)
-    wx = placed.transpose(0, 3, 4, 1, 2).reshape(8, 64, 128)
-    flipped = fb[:, ::-1]
-    spread = jnp.stack(
-        [jnp.pad(flipped, ((0, 0), (0, 1), (0, 0), (0, 0))), jnp.pad(flipped, ((0, 0), (1, 0), (0, 0), (0, 0)))],
-        axis=1,
-    )
-    my = spread.reshape(8, 2, 4, 16, 2, 32).transpose(4, 2, 5, 0, 1, 3).reshape(256, 256)
-    return wz, wx, my
-
-
-def coarse_weights(cb):
-    wz = (
-        cb[:, :, None, :, None, :] * lane_eye(4)[None, None, :, None, :, None]
-    ).reshape(4, 2, 384, 128).transpose(0, 2, 1, 3).reshape(4, 384, 256)
-    wx = cb.transpose(0, 3, 1, 2).reshape(8, 32, 96)
-    my = cb[:, ::-1].reshape(8, 3, 8, 4, 32).transpose(3, 1, 4, 0, 2).reshape(384, 64)
-    return wz, wx, my
-
-
-def scale_weights(two_scale):
-    fz = (
-        two_scale.T.reshape(2, 1, 32, 1, 32) * lane_eye(4)[None, :, None, :, None]
-    ).reshape(256, 128)
-    ky = (two_scale.T[:, None, :, None] * lane_eye(32)[None, :, None, :]).reshape(2048, 1024)
-    st2 = jnp.concatenate([two_scale.T, two_scale.T], axis=1)
-    return fz, ky, st2
-
-
-def parent_kernel(own, fz, ky, s, out, rows, wide):
+    lane = lax.broadcasted_iota(jnp.int32, (32, 1024), 1) % 32 == lax.broadcasted_iota(jnp.int32, (32, 1024), 0)
+    for y in range(64):
+        ky[y * 32 : y * 32 + 32, :] = jnp.where(
+            lane, jnp.broadcast_to(spread[y : y + 1], (32, 1024)), 0.0
+        ).astype(BF)
     for yg in range(16):
         cy, g = divmod(yg, 8)
         for cx in range(2):
@@ -87,16 +142,20 @@
     for yg in range(16):
         wide[:, yg * 128 : yg * 128 + 128] = along_z[yg * 64 : yg * 64 + 64]
     along_y = dot(wide[...], ky[...]).astype(BF)
-    out[...] = dot(s[...], along_y).astype(BF)
-
-
-def parents_of(own, fz, ky, s):
+    out[...] = dot(scale, along_y).astype(BF)
+
+
+def parents_of(own, s):
     return call(
         parent_kernel,
-        jax.ShapeDtypeStruct((32, 1024), BF),
+        (
+            jax.ShapeDtypeStruct((32, 1024), BF),
+            jax.ShapeDtypeStruct((256, 128), BF),
+            jax.ShapeDtypeStruct((2048, 1024), BF),
+            jax.ShapeDtypeStruct((64, 64), BF),
+        ),
         [pltpu.VMEM((1024, 256), BF), pltpu.VMEM((64, 2048), BF)],
-        "parents",
-    )(own, fz, ky, s)
+    )(own, s)
 
 
 def main_kernel(
@@ -184,7 +243,8 @@
                 left_c[row : row + 32, zb * 128 : zb * 128 + 128] = sources[xb][zb][:, g * 128 : g * 128 + 128]
 
     def coarse_pair(h, carry):
-        passed = dot(left_c[...], cwz[h]).astype(BF)
+        weight = jnp.concatenate([cwz[2 * h], cwz[2 * h + 1]], axis=1)
+        passed = dot(left_c[...], weight).astype(BF)
         mid_c[...] = passed.reshape(8, 96, 256)
         for i in range(2):
             weight_x = cwx[2 * h + i]
@@ -256,7 +316,6 @@
             pltpu.VMEM((2048, 128), F32),
             pltpu.VMEM((3072, 128), F32),
         ],
-        "passes",
     )(*operands)
 
 
@@ -292,7 +351,6 @@
         final_kernel,
         jax.ShapeDtypeStruct((8, 32, 1024), BF),
         [pltpu.VMEM((512, 128), BF), pltpu.VMEM((128, 1024), BF), pltpu.VMEM((64, 2048), BF)],
-        "finish",
     )(*operands)
 
 
@@ -323,7 +381,7 @@
     return shift_z(layer, step)
 
 
-def on_device(fine_coeffs, fine_blocks, coarse_blocks, two_scale, term_exponent):
+def steps(fine_coeffs, fine_blocks, coarse_blocks, two_scale, term_exponent):
     p = lax.axis_index("box")
     t = lax.axis_index("term")
     zm = z_layer(fine_coeffs, 1, p, t)
@@ -332,8 +390,7 @@
     xm_own = shift(own[4:], 16)
     xp_own = shift(own[:4], -16)
 
-    fz, ky, st2 = scale_weights(two_scale)
-    par = parents_of(own, fz, ky, two_scale)
+    par, fz, ky, st2 = parents_of(own, two_scale)
     czm = shift(par, 1)
     czp = shift(par, -1)
 
@@ -342,11 +399,8 @@
     xm_far = shift(far_up, 16)
     xp_far = shift(far_dn, -16)
 
-    wz, wx, my = fine_weights(jnp.take(fine_blocks, term_exponent, axis=0))
-    cwz, cwx, cmy = coarse_weights(jnp.take(coarse_blocks, term_exponent, axis=0))
-    out, send_up, send_dn, out_c = passes(
-        own, zm, zp, xm_own, xp_own, xm_far, xp_far, par, czm, czp, wz, wx, my, cwz, cwx, cmy
-    )
+    made = weights(term_exponent, fine_blocks, coarse_blocks)
+    out, send_up, send_dn, out_c = passes(own, zm, zp, xm_own, xp_own, xm_far, xp_far, par, czm, czp, *made)
     low = shift(send_up, 4)
     high = shift(send_dn, -4)
     total = finish(out, out_c, low, high, fz, ky, st2)
@@ -358,7 +412,7 @@
 def solution(mesh):
     placed = (P(None, "box", None, None), P(), P(), P(), P())
     return jax.shard_map(
-        on_device,
+        steps,
         mesh=mesh,
         in_specs=placed,
         out_specs=P(None, ("box", "term"), None, None),

time: 190 us -> 117 us (0.62)
  local copies, waits for them, and re-layouts: 78.1 us -> 6.28 us
  other arithmetic: 11.2 us -> 1.09 us
  Pallas kernels: 44.8 us -> 49.7 us
  waiting for transfers between devices: 20.4 us -> 25.3 us
  starting transfers between devices: 19.6 us -> 16.9 us
    mul x10 -> x0, local copies, waits for them, and re-layouts: 59.8 us -> none  [the longest x4 29.5 us: fine_weights(): placed[:, :, None, :, None]]
    ppermute x2, waiting for transfers between devices: 0.01 us -> 8.38 us  [shift_z(): return lax.ppermute(block, ('box', 'term'), route)]
    mul x3 -> x0, other arithmetic: 7.67 us -> none  [the longest x1 5.97 us: scale_weights(): two_scale.T[:, None, :, None] * lane_eye(32)[None, :, None, :]]
    reshape x7 -> x0, local copies, waits for them, and re-layouts: 5.73 us -> none  [the longest x3 2.01 us: coarse_weights(): cb[:, ::-1].reshape(8, 3, 8, 4, 32).transpose(3, 1, 4, 0, 2)]
    pallas_call x1 -> x2, Pallas kernels: 4.01 us -> 8.95 us  [the longest x1 4.98 us: weights(): pl.pallas_call(weight_kernel, out_shape=(jax.ShapeDtypeStruct((8, 512, 25...]
    ppermute x8, starting transfers between devices: 15.7 us -> 11.2 us  [shift(): lax.ppermute(block, 'box', [(i, (i + distance) % count) for i in range(co...]
    ppermute x8, waiting for transfers between devices: 20.4 us -> 16.9 us  [shift(): lax.ppermute(block, 'box', [(i, (i + distance) % count) for i in range(co...]
    unnamed x35 -> x24, local copies, waits for them, and re-layouts: 5.25 us -> 2.85 us
  transfers between devices with their start and end apart: 10 -> 10, of which waited for: 4 -> 5; matrix products, arithmetic and copies ran while one was open for 29% -> 2% of each run, Pallas kernels for 0% -> 8%
where the time goes in v2:
time: 117 us; the launch traced here: 115 us
  Pallas kernels  49.7 us (42%)
  waiting for transfers between devices  25.3 us (22%)
  starting transfers between devices  16.9 us (14%)
  blocking collectives  16.1 us (14%)
  local copies, waits for them, and re-layouts  6.28 us (5%)
    pallas_call x1, Pallas kernels, passes(): call(main_kernel, (jax.ShapeDtypeStruct((8, 32, 1024), F32), jax.ShapeDty...  35.4 us
    ppermute x8, waiting for transfers between devices, shift(): lax.ppermute(block, 'box', [(i, (i + distance) % count) for i in range(co...  16.9 us
    all_to_all x1, blocking collectives, steps(): mine = lax.all_to_all(total.reshape(groups, 2, 32, 1024), 'term', 0, 0)  16.1 us
    ppermute x8, starting transfers between devices, shift(): lax.ppermute(block, 'box', [(i, (i + distance) % count) for i in range(co...  11.2 us
    ppermute x2, waiting for transfers between devices, shift_z(): return lax.ppermute(block, ('box', 'term'), route)  8.38 us
    ppermute x2, starting transfers between devices, shift_z(): return lax.ppermute(block, ('box', 'term'), route)  5.71 us
    pallas_call x1, Pallas kernels, finish(): call(final_kernel, jax.ShapeDtypeStruct((8, 32, 1024), BF), [pltpu.VMEM((...  5.34 us
    pallas_call x1, Pallas kernels, weights(): pl.pallas_call(weight_kernel, out_shape=(jax.ShapeDtypeStruct((8, 512, 25...  4.98 us
  transfers between devices with their start and end apart: 10, of which 5 were waited for; matrix products, arithmetic and copies ran while one was open for 2% of the time, Pallas kernels for 8%

profile of v2, /device:TPU:30, one launch (start us, length us, event | category | flops | bytes accessed | tf_op | source)
XLA Modules:
  0.0 115.5 jit_solution(16342382617862652599)
XLA Ops:
  0.0 2.3 %constant_dynamic-slice_fusion = (bf16[1,8,32,1024]{3,2,1,0:T(8,128)(2,1)S(1)}, bf16[8,32,1024]{2,1,0:T(8,128)(2,1)}, bf16[1,8,32,1024]{3,2,1,0:T(8,128)(2,1)S(1)}) fusion(bf16[4,8,32,1024]{3,2,1,0:T(8,128)(2,1)} %param.5, s32[]{:T(128)S(6)} %select_n.30, s32[]{:T(128)S(6)} %select_n.25, s32[]{:T(128)S(6)} %select_n.28), kind=kLoop, calls=%fused_computation.15 | loop fusion | bytes 3145740 | tf_op jit(solution)/shard_map/jit(dynamic_index_in_dim)/dynamic_slice | solution.py:379
  2.3 0.1 collective-permute-start
  2.5 5.6 %collective-permute-start.1 = (bf16[4,32,1024]{2,1,0:T(8,128)(2,1)S(1)}, bf16[4,32,1024]{2,1,0:T(8,128)(2,1)S(1)}, u32[]{:S(2)}, u32[]{:S(2)}) collective-permute-start(bf16[4,32,1024]{2,1,0:T(8,128)(2,1)S(1)} %slice_bitcast_fusion), channel_id=1, source_target_pairs={{0,255},{1,254},{2,253},{3,252},{4,0},{5,1},{6,2},{7,3},{8,7},{9,6... | collective-permute-start | bytes 786440 | tf_op jit(solution)/shard_map/ppermute | solution.py:373
  8.1 4.0 %shard_map.55 = (bf16[32,1024]{1,0:T(8,128)(2,1)}, bf16[256,128]{1,0:T(8,128)(2,1)}, bf16[2048,1024]{1,0:T(8,128)(2,1)}, bf16[64,64]{1,0:T(8,128)(2,1)}) custom-call(bf16[8,32,1024]{2,1,0:T(8,128)(2,1)} %get-tuple-element.36.own, bf16[32,64]{1,0:T(8,128)(2,1)} %s.1), custom_call_target="tpu_custom_call" | custom-call | tf_op jit(solution)/shard_map/pallas_call | solution.py:149
  12.1 2.4 %collective-permute-start.5 = (bf16[32,1024]{1,0:T(8,128)(2,1)}, bf16[32,1024]{1,0:T(8,128)(2,1)S(1)}, u32[]{:S(2)}, u32[]{:S(2)}) collective-permute-start(bf16[32,1024]{1,0:T(8,128)(2,1)} %get-tuple-element.19.par), channel_id=1, source_target_pairs={{0,252},{4,0},{8,4},{12,8},{16,12},{20,16},{24,20},{28,24},{32,28}... | collective-permute-start | bytes 196616 | tf_op jit(solution)/shard_map/ppermute | solution.py:359
  14.4 0.0 collective-permute-start.4
  14.4 4.9 %collective-permute-done.zm = bf16[4,32,1024]{2,1,0:T(8,128)(2,1)S(1)} collective-permute-done((bf16[4,32,1024]{2,1,0:T(8,128)(2,1)S(1)}, bf16[4,32,1024]{2,1,0:T(8,128)(2,1)S(1)}, u32[]{:S(2)}, u32[]{:S(2)}) %collective-permute-start) | collective-permute-done | bytes 262176 | tf_op jit(solution)/shard_map/ppermute | solution.py:373
  19.4 0.0 copy-start
  19.4 3.4 %collective-permute-done.1.zp = bf16[4,32,1024]{2,1,0:T(8,128)(2,1)S(1)} collective-permute-done((bf16[4,32,1024]{2,1,0:T(8,128)(2,1)S(1)}, bf16[4,32,1024]{2,1,0:T(8,128)(2,1)S(1)}, u32[]{:S(2)}, u32[]{:S(2)}) %collective-permute-start.1) | collective-permute-done | bytes 262176 | tf_op jit(solution)/shard_map/ppermute | solution.py:373
  22.8 0.0 copy-start.1
  22.8 0.9 bitcast_dynamic-update-slice_fusion.4
  23.8 0.0 collective-permute-done.4.czm
  23.8 0.0 copy-start.7
  23.8 0.0 collective-permute-done.5.czp
  23.8 0.0 copy-start.6
  23.9 0.8 collective-permute-start.7
  24.7 2.5 %collective-permute-start.6 = (bf16[7,32,1024]{2,1,0:T(8,128)(2,1)S(1)}, bf16[7,32,1024]{2,1,0:T(8,128)(2,1)S(1)}, u32[]{:S(2)}, u32[]{:S(2)}) collective-permute-start(bf16[7,32,1024]{2,1,0:T(8,128)(2,1)S(1)} %get-tuple-element.43), channel_id=1, source_target_pairs={{0,64},{4,68},{8,72},{12,76},{16,80},{20,84},{24,88},{28,92},{32,9... | collective-permute-start | bytes 1376264 | tf_op jit(solution)/shard_map/ppermute | solution.py:359
  27.2 1.1 dynamic-slice_bitcast_fusion.1
  28.2 0.1 collective-permute-start.3
  28.3 3.2 %collective-permute-start.2 = (bf16[4,32,1024]{2,1,0:T(8,128)(2,1)S(1)}, bf16[4,32,1024]{2,1,0:T(8,128)(2,1)S(1)}, u32[]{:S(2)}, u32[]{:S(2)}) collective-permute-start(bf16[4,32,1024]{2,1,0:T(8,128)(2,1)S(1)} %get-tuple-element.34), channel_id=1, source_target_pairs={{0,64},{4,68},{8,72},{12,76},{16,80},{20,84},{24,88},{28,92},{32,9... | collective-permute-start | bytes 786440 | tf_op jit(solution)/shard_map/ppermute | solution.py:359
  31.6 5.0 %weights.1 = (bf16[8,512,256]{2,1,0:T(8,128)(2,1)}, bf16[8,64,128]{2,1,0:T(8,128)(2,1)}, bf16[256,256]{1,0:T(8,128)(2,1)}, bf16[8,384,128]{2,1,0:T(8,128)(2,1)},...) custom-call(s32[8]{0:T(128)} %exponents.1, bf16[16,3,32,32]{3,2,1,0:T(8,128)(2,1)} %fine.1, ...), custom_call_target="tpu_custom_call" | custom-call | tf_op jit(solution)/shard_map/weights/pallas_call | solution.py:89
  36.5 6.3 %collective-permute-done.3.xp_own = bf16[4,32,1024]{2,1,0:T(8,128)(2,1)S(1)} collective-permute-done((bf16[4,32,1024]{2,1,0:T(8,128)(2,1)S(1)}, bf16[4,32,1024]{2,1,0:T(8,128)(2,1)S(1)}, u32[]{:S(2)}, u32[]{:S(2)}) %collective-permute-start.3) | collective-permute-done | bytes 262176 | tf_op jit(solution)/shard_map/ppermute | solution.py:359
  42.8 0.0 copy-start.8
  42.8 0.0 collective-permute-done.2.xm_own
  42.8 0.0 copy-start.9
  42.8 0.0 collective-permute-done.7.xp_far
  42.8 0.0 copy-start.2
  42.8 0.0 collective-permute-done.6.xm_far
  42.8 0.0 copy-start.3
  42.9 0.0 copy-done
  42.9 0.0 copy-done.1
  42.9 0.0 copy-done.7
  42.9 0.0 copy-done.6
  42.9 0.6 copy-done.8
  43.5 0.1 copy-done.9
  43.6 0.2 copy-done.2
  43.8 0.2 copy-done.3
  44.0 35.4 %shard_map.56 = (f32[8,32,1024]{2,1,0:T(8,128)}, bf16[5,32,1024]{2,1,0:T(8,128)(2,1)}, bf16[5,32,1024]{2,1,0:T(8,128)(2,1)}, f32[32,1024]{1,0:T(8,128)}) custom-call(bf16[8,32,1024]{2,1,0:T(8,128)(2,1)} %get-tuple-element.36.own, bf16[4,32,1024]{2,1,0:T(8,128)(2,1)} %copy-done, bf16[4,32,1024]{2,1,0:T(8,128)(2,1)} %copy-done.1, ...), custom_call_target="tpu_custom_call" | custom-call | tf_op jit(solution)/shard_map/pallas_call | solution.py:301
  79.4 2.2 %collective-permute-start.8 = (bf16[5,32,1024]{2,1,0:T(8,128)(2,1)}, bf16[5,32,1024]{2,1,0:T(8,128)(2,1)S(1)}, u32[]{:S(2)}, u32[]{:S(2)}) collective-permute-start(bf16[5,32,1024]{2,1,0:T(8,128)(2,1)} %get-tuple-element.28), channel_id=1, source_target_pairs={{0,16},{4,20},{8,24},{12,28},{16,32},{20,36},{24,40},{28,44},{32,4... | collective-permute-start | bytes 983048 | tf_op jit(solution)/shard_map/ppermute | solution.py:359
  81.6 0.0 collective-permute-start.9
  81.6 6.9 %collective-permute-done.8.low = bf16[5,32,1024]{2,1,0:T(8,128)(2,1)S(1)} collective-permute-done((bf16[5,32,1024]{2,1,0:T(8,128)(2,1)}, bf16[5,32,1024]{2,1,0:T(8,128)(2,1)S(1)}, u32[]{:S(2)}, u32[]{:S(2)}) %collective-permute-start.8) | collective-permute-done | bytes 327712 | tf_op jit(solution)/shard_map/ppermute | solution.py:359
  88.5 0.0 copy-start.4
  88.5 3.7 %collective-permute-done.9.high = bf16[5,32,1024]{2,1,0:T(8,128)(2,1)S(1)} collective-permute-done((bf16[5,32,1024]{2,1,0:T(8,128)(2,1)}, bf16[5,32,1024]{2,1,0:T(8,128)(2,1)S(1)}, u32[]{:S(2)}, u32[]{:S(2)}) %collective-permute-start.9) | collective-permute-done | bytes 327712 | tf_op jit(solution)/shard_map/ppermute | solution.py:359
  92.2 0.0 copy-done.4
  92.2 0.7 copy-done.5
  93.0 5.3 %shard_map.57 = bf16[8,32,1024]{2,1,0:T(8,128)(2,1)} custom-call(f32[8,32,1024]{2,1,0:T(8,128)} %get-tuple-element.26.own, f32[32,1024]{1,0:T(8,128)} %get-tuple-element.27.own_c, bf16[5,32,1024]{2,1,0:T(8,128)(2,1)} %copy-done.4, bf16[5,32,1024]{2,1,0:T(8,128)(2,1)} %copy-done.5, bf16[256,128]{1,0:T(8,128)(2,1)} %get-tuple-element.30.fz, ...), custom_call_target="tpu_custom_call" | custom-call | tf_op jit(solution)/shard_map/pallas_call | solution.py:350
  98.3 16.1 %all_to_all.5 = bf16[4,2,32,1024]{3,2,1,0:T(8,128)(2,1)S(1)} all-to-all(bf16[4,2,32,1024]{3,2,1,0:T(8,128)(2,1)} %bitcast.26), channel_id=1, replica_groups=mesh['box'=64,'term'=4] {'term'}, dimensions={0} | all-to-all | bytes 1048576 | tf_op jit(solution)/shard_map/all_to_all | solution.py:408
  114.4 1.1 convert_element_type.3
  (7 shorter events, 0.1 us)
Async XLA Ops:
  2.3 17.0 %collective-permute-start = (bf16[4,32,1024]{2,1,0:T(8,128)(2,1)S(1)}, bf16[4,32,1024]{2,1,0:T(8,128)(2,1)S(1)}, u32[]{:S(2)}, u32[]{:S(2)}) collective-permute-start(bf16[4,32,1024]{2,1,0:T(8,128)(2,1)S(1)} %slice_bitcast_fusion.1), channel_id=1, source_target_pairs={{0,4},{1,5},{2,6},{3,7},{4,11},{5,10},{6,9},{7,8},{8,12},{9,13},{1... | collective-permute-start | bytes 786440 | tf_op jit(solution)/shard_map/ppermute | solution.py:373
  2.5 20.4 %collective-permute-start.1 = (bf16[4,32,1024]{2,1,0:T(8,128)(2,1)S(1)}, bf16[4,32,1024]{2,1,0:T(8,128)(2,1)S(1)}, u32[]{:S(2)}, u32[]{:S(2)}) collective-permute-start(bf16[4,32,1024]{2,1,0:T(8,128)(2,1)S(1)} %slice_bitcast_fusion), channel_id=1, source_target_pairs={{0,255},{1,254},{2,253},{3,252},{4,0},{5,1},{6,2},{7,3},{8,7},{9,6... | collective-permute-start | bytes 786440 | tf_op jit(solution)/shard_map/ppermute | solution.py:373
  12.1 11.8 %collective-permute-start.5 = (bf16[32,1024]{1,0:T(8,128)(2,1)}, bf16[32,1024]{1,0:T(8,128)(2,1)S(1)}, u32[]{:S(2)}, u32[]{:S(2)}) collective-permute-start(bf16[32,1024]{1,0:T(8,128)(2,1)} %get-tuple-element.19.par), channel_id=1, source_target_pairs={{0,252},{4,0},{8,4},{12,8},{16,12},{20,16},{24,20},{28,24},{32,28}... | collective-permute-start | bytes 196616 | tf_op jit(solution)/shard_map/ppermute | solution.py:359
  14.4 9.4 %collective-permute-start.4 = (bf16[32,1024]{1,0:T(8,128)(2,1)}, bf16[32,1024]{1,0:T(8,128)(2,1)S(1)}, u32[]{:S(2)}, u32[]{:S(2)}) collective-permute-start(bf16[32,1024]{1,0:T(8,128)(2,1)} %get-tuple-element.19.par), channel_id=1, source_target_pairs={{0,4},{4,8},{8,12},{12,16},{16,20},{20,24},{24,28},{28,32},{32,36}... | collective-permute-start | bytes 196616 | tf_op jit(solution)/shard_map/ppermute | solution.py:359
  19.4 23.5 %copy-start = (bf16[4,32,1024]{2,1,0:T(8,128)(2,1)}, bf16[4,32,1024]{2,1,0:T(8,128)(2,1)S(1)}, u32[]{:S(2)}) copy-start(bf16[4,32,1024]{2,1,0:T(8,128)(2,1)S(1)} %collective-permute-done.zm) | copy-start | bytes 786436
  22.8 20.0 %copy-start.1 = (bf16[4,32,1024]{2,1,0:T(8,128)(2,1)}, bf16[4,32,1024]{2,1,0:T(8,128)(2,1)S(1)}, u32[]{:S(2)}) copy-start(bf16[4,32,1024]{2,1,0:T(8,128)(2,1)S(1)} %collective-permute-done.1.zp) | copy-start | bytes 786436
  23.8 19.1 %copy-start.7 = (bf16[32,1024]{1,0:T(8,128)(2,1)}, bf16[32,1024]{1,0:T(8,128)(2,1)S(1)}, u32[]{:S(2)}) copy-start(bf16[32,1024]{1,0:T(8,128)(2,1)S(1)} %collective-permute-done.4.czm) | copy-start | bytes 196612
  23.8 19.1 %copy-start.6 = (bf16[32,1024]{1,0:T(8,128)(2,1)}, bf16[32,1024]{1,0:T(8,128)(2,1)S(1)}, u32[]{:S(2)}) copy-start(bf16[32,1024]{1,0:T(8,128)(2,1)S(1)} %collective-permute-done.5.czp) | copy-start | bytes 196612
  23.9 19.0 %collective-permute-start.7 = (bf16[7,32,1024]{2,1,0:T(8,128)(2,1)S(1)}, bf16[7,32,1024]{2,1,0:T(8,128)(2,1)S(1)}, u32[]{:S(2)}, u32[]{:S(2)}) collective-permute-start(bf16[7,32,1024]{2,1,0:T(8,128)(2,1)S(1)} %get-tuple-element.42), channel_id=1, source_target_pairs={{0,192},{4,196},{8,200},{12,204},{16,208},{20,212},{24,216},{28,22... | collective-permute-start | bytes 1376264 | tf_op jit(solution)/shard_map/ppermute | solution.py:359
  24.7 18.2 %collective-permute-start.6 = (bf16[7,32,1024]{2,1,0:T(8,128)(2,1)S(1)}, bf16[7,32,1024]{2,1,0:T(8,128)(2,1)S(1)}, u32[]{:S(2)}, u32[]{:S(2)}) collective-permute-start(bf16[7,32,1024]{2,1,0:T(8,128)(2,1)S(1)} %get-tuple-element.43), channel_id=1, source_target_pairs={{0,64},{4,68},{8,72},{12,76},{16,80},{20,84},{24,88},{28,92},{32,9... | collective-permute-start | bytes 1376264 | tf_op jit(solution)/shard_map/ppermute | solution.py:359
  28.2 14.6 %collective-permute-start.3 = (bf16[4,32,1024]{2,1,0:T(8,128)(2,1)S(1)}, bf16[4,32,1024]{2,1,0:T(8,128)(2,1)S(1)}, u32[]{:S(2)}, u32[]{:S(2)}) collective-permute-start(bf16[4,32,1024]{2,1,0:T(8,128)(2,1)S(1)} %get-tuple-element.33), channel_id=1, source_target_pairs={{0,192},{4,196},{8,200},{12,204},{16,208},{20,212},{24,216},{28,22... | collective-permute-start | bytes 786440 | tf_op jit(solution)/shard_map/ppermute | solution.py:359
  28.3 14.5 %collective-permute-start.2 = (bf16[4,32,1024]{2,1,0:T(8,128)(2,1)S(1)}, bf16[4,32,1024]{2,1,0:T(8,128)(2,1)S(1)}, u32[]{:S(2)}, u32[]{:S(2)}) collective-permute-start(bf16[4,32,1024]{2,1,0:T(8,128)(2,1)S(1)} %get-tuple-element.34), channel_id=1, source_target_pairs={{0,64},{4,68},{8,72},{12,76},{16,80},{20,84},{24,88},{28,92},{32,9... | collective-permute-start | bytes 786440 | tf_op jit(solution)/shard_map/ppermute | solution.py:359
  42.8 0.7 copy-start.8
  42.8 0.8 copy-start.9
  42.8 1.0 copy-start.2
  42.8 1.1 copy-start.3
  79.4 9.0 %collective-permute-start.8 = (bf16[5,32,1024]{2,1,0:T(8,128)(2,1)}, bf16[5,32,1024]{2,1,0:T(8,128)(2,1)S(1)}, u32[]{:S(2)}, u32[]{:S(2)}) collective-permute-start(bf16[5,32,1024]{2,1,0:T(8,128)(2,1)} %get-tuple-element.28), channel_id=1, source_target_pairs={{0,16},{4,20},{8,24},{12,28},{16,32},{20,36},{24,40},{28,44},{32,4... | collective-permute-start | bytes 983048 | tf_op jit(solution)/shard_map/ppermute | solution.py:359
  81.6 10.6 %collective-permute-start.9 = (bf16[5,32,1024]{2,1,0:T(8,128)(2,1)}, bf16[5,32,1024]{2,1,0:T(8,128)(2,1)S(1)}, u32[]{:S(2)}, u32[]{:S(2)}) collective-permute-start(bf16[5,32,1024]{2,1,0:T(8,128)(2,1)} %get-tuple-element.29), channel_id=1, source_target_pairs={{0,240},{4,244},{8,248},{12,252},{16,0},{20,4},{24,8},{28,12},{32,... | collective-permute-start | bytes 983048 | tf_op jit(solution)/shard_map/ppermute | solution.py:359
  88.5 3.7 %copy-start.4 = (bf16[5,32,1024]{2,1,0:T(8,128)(2,1)}, bf16[5,32,1024]{2,1,0:T(8,128)(2,1)S(1)}, u32[]{:S(2)}) copy-start(bf16[5,32,1024]{2,1,0:T(8,128)(2,1)S(1)} %collective-permute-done.8.low) | copy-start | bytes 983044
  92.2 0.7 copy-start.5

commit v3 on v2

--- a/solution.py
+++ b/solution.py
@@ -9,7 +9,7 @@
 BF = jnp.bfloat16
 F32 = jnp.float32
 INTERPRET = False
-PARAMS = dict(compiler_params=pltpu.CompilerParams(vmem_limit_bytes=56 * 1024 * 1024))
+PARAMS = dict(compiler_params=pltpu.CompilerParams(vmem_limit_bytes=40 * 1024 * 1024))
 
 
 def dot(a, b):
@@ -158,11 +158,16 @@
     )(own, s)
 
 
-def main_kernel(
-    own, zm, zp, xm_own, xp_own, xm_far, xp_far, par, czm, czp,
-    wz, wx, my, cwz, cwx, cmy,
-    out, send_up, send_dn, out_c,
-    left, mid, wide, done, left_c, mid_c, wide_c, done_c,
+PITCH_U = 68
+PITCH_V = 132
+PITCH_CU = 36
+PITCH_CV = 100
+
+
+def fine_kernel(
+    own, zm, zp, xm_own, xp_own, xm_far, xp_far, wz, wx, my,
+    out, send_up, send_dn,
+    left, mid, wide, done,
 ):
     for cy in range(2):
         sources = [
@@ -178,47 +183,47 @@
                     row = (cy * 8 + g) * 128 + xb * 32
                     left[row : row + 32, zb * 128 : zb * 128 + 128] = box[:, g * 128 : g * 128 + 128]
 
-    def fine_term(t, carry):
+    def term(t, carry):
         weight = wz[t]
         for m in range(4):
             passed = dot(left[m * 512 : m * 512 + 512, :], weight).astype(BF)
             mid[m * 4 : m * 4 + 4] = passed.reshape(4, 128, 256)
         weight_x = wx[t]
+        start = pl.multiple_of(t * (32 * PITCH_U), 8)
         for yg in range(16):
             passed = dot(weight_x, mid[yg])
-            base = (t * 32 + 2 * yg) * 64
-            wide[pl.ds(base, 64), :] = passed[:, :128]
-            wide[pl.ds(base + 64, 64), :] = passed[:, 128:]
-        return carry
-
-    lax.fori_loop(0, 8, fine_term, 0)
-
-    def fine_rows(k, carry):
+            wide[pl.ds(start + 2 * yg * PITCH_U, 64), :] = passed[:, :128]
+            wide[pl.ds(start + (2 * yg + 1) * PITCH_U, 64), :] = passed[:, 128:]
+        return carry
+
+    lax.fori_loop(0, 8, term, 0)
+
+    def rows(k, carry):
         u = 2 * k
         data = jnp.concatenate(
-            [wide[pl.ds(u, 256, stride=64), :].astype(BF), wide[pl.ds(u + 1, 256, stride=64), :].astype(BF)], axis=1
+            [wide[pl.ds(u + i, 256, stride=PITCH_U), :].astype(BF) for i in range(2)], axis=1
         )
         passed = dot(my[...], data)
+        start = pl.multiple_of(k * (2 * PITCH_V), 8)
         for i in range(2):
             lanes = passed[:, i * 128 : i * 128 + 128]
-            base = pl.multiple_of((u + i) * 128, 128)
-            done[pl.ds(base, 128), :] = lanes[:128] + pltpu.roll(lanes[128:], 64, 1)
-        return carry
-
-    lax.fori_loop(0, 32, fine_rows, 0)
-
-    lane64 = lax.broadcasted_iota(jnp.int32, (64, 128), 1) // 32
-
-    def fine_lanes(g, carry):
+            done[pl.ds(start + i * PITCH_V, 128), :] = lanes[:128] + pltpu.roll(lanes[128:], 64, 1)
+        return carry
+
+    lax.fori_loop(0, 32, rows, 0)
+
+    lane = lax.broadcasted_iota(jnp.int32, (64, 128), 1) // 32
+
+    def relay(g, carry):
         at = pl.multiple_of(g * 128, 128)
         for vb in range(4):
-            parts = [done[pl.ds(vb * 32 + 4 * g + j, 64, stride=128), :] for j in range(4)]
+            parts = [done[pl.ds(vb * 32 + 4 * g + j, 64, stride=PITCH_V), :] for j in range(4)]
             for cz in range(2):
                 block = parts[0] if cz == 0 else pltpu.roll(parts[0], 96, 1)
                 for j in range(1, 4):
                     turn = (32 * (j - cz)) % 128
                     moved = pltpu.roll(parts[j], turn, 1) if turn else parts[j]
-                    block = jnp.where(lane64 == j, moved, block)
+                    block = jnp.where(lane == j, moved, block)
                 for cx in range(2):
                     piece = block[cx * 32 : cx * 32 + 32]
                     if vb == 0:
@@ -229,98 +234,111 @@
                         out[4 * cx + 2 * (vb - 1) + cz, :, pl.ds(at, 128)] = piece
         return carry
 
-    lax.fori_loop(0, 8, fine_lanes, 0)
-
+    lax.fori_loop(0, 8, relay, 0)
+
+
+def fine_passes(*operands):
+    return call(
+        fine_kernel,
+        (
+            jax.ShapeDtypeStruct((8, 32, 1024), F32),
+            jax.ShapeDtypeStruct((4, 32, 1024), BF),
+            jax.ShapeDtypeStruct((4, 32, 1024), BF),
+        ),
+        [
+            pltpu.VMEM((2048, 512), BF),
+            pltpu.VMEM((16, 128, 256), BF),
+            pltpu.VMEM((256 * PITCH_U, 128), F32),
+            pltpu.VMEM((64 * PITCH_V, 128), F32),
+        ],
+    )(*operands)
+
+
+def coarse_kernel(par, zm, zp, xm, xp, wz, wx, my, out, send_up, send_dn, left, mid, wide, done):
     sources = [
-        [xm_far[5], xm_far[4], xm_far[6]],
-        [czm[...], par[...], czp[...]],
-        [xp_far[5], xp_far[4], xp_far[6]],
+        [xm[1], xm[0], xm[2]],
+        [zm[...], par[...], zp[...]],
+        [xp[1], xp[0], xp[2]],
     ]
     for xb in range(3):
         for zb in range(3):
             for g in range(8):
                 row = g * 96 + xb * 32
-                left_c[row : row + 32, zb * 128 : zb * 128 + 128] = sources[xb][zb][:, g * 128 : g * 128 + 128]
-
-    def coarse_pair(h, carry):
-        weight = jnp.concatenate([cwz[2 * h], cwz[2 * h + 1]], axis=1)
-        passed = dot(left_c[...], weight).astype(BF)
-        mid_c[...] = passed.reshape(8, 96, 256)
+                left[row : row + 32, zb * 128 : zb * 128 + 128] = sources[xb][zb][:, g * 128 : g * 128 + 128]
+
+    def pair(h, carry):
+        weight = jnp.concatenate([wz[2 * h], wz[2 * h + 1]], axis=1)
+        mid[...] = dot(left[...], weight).astype(BF).reshape(8, 96, 256)
+        start = pl.multiple_of(h * (16 * PITCH_CU), 8)
         for i in range(2):
-            weight_x = cwx[2 * h + i]
+            weight_x = wx[2 * h + i]
             for g in range(0, 8, 2):
                 data = jnp.concatenate(
-                    [mid_c[g, :, i * 128 : i * 128 + 128], mid_c[g + 1, :, i * 128 : i * 128 + 128]], axis=1
+                    [mid[g, :, i * 128 : i * 128 + 128], mid[g + 1, :, i * 128 : i * 128 + 128]], axis=1
                 )
                 moved = dot(weight_x, data)
-                base = ((2 * h + i) * 8 + g) * 32
-                wide_c[pl.ds(base, 32), :] = moved[:, :128]
-                wide_c[pl.ds(base + 32, 32), :] = moved[:, 128:]
-        return carry
-
-    lax.fori_loop(0, 4, coarse_pair, 0)
-
-    def coarse_rows(k, carry):
+                wide[pl.ds(start + (i * 8 + g) * PITCH_CU, 32), :] = moved[:, :128]
+                wide[pl.ds(start + (i * 8 + g + 1) * PITCH_CU, 32), :] = moved[:, 128:]
+        return carry
+
+    lax.fori_loop(0, 4, pair, 0)
+
+    def rows(k, carry):
         u = 2 * k
         data = jnp.concatenate(
-            [wide_c[pl.ds(u, 64, stride=32), :].astype(BF), wide_c[pl.ds(u + 1, 64, stride=32), :].astype(BF)], axis=1
+            [wide[pl.ds(u + i, 64, stride=PITCH_CU), :].astype(BF) for i in range(2)], axis=1
         )
-        passed = dot(cmy[...], data)
+        passed = dot(my[...], data)
+        start = pl.multiple_of(k * (2 * PITCH_CV), 8)
         for i in range(2):
             lanes = passed[:, i * 128 : i * 128 + 128]
             total = lanes[:96]
             for j in range(1, 4):
                 total = total + pltpu.roll(lanes[j * 96 : j * 96 + 96], 128 - 32 * j, 1)
-            base = pl.multiple_of((u + i) * 96, 32)
-            done_c[pl.ds(base, 96), :] = total
-        return carry
-
-    lax.fori_loop(0, 16, coarse_rows, 0)
-
-    lane32 = lax.broadcasted_iota(jnp.int32, (32, 128), 1) // 32
-
-    def coarse_lanes(g, carry):
+            done[pl.ds(start + i * PITCH_CV, 96), :] = total
+        return carry
+
+    lax.fori_loop(0, 16, rows, 0)
+
+    lane = lax.broadcasted_iota(jnp.int32, (32, 128), 1) // 32
+
+    def relay(g, carry):
         at = pl.multiple_of(g * 128, 128)
         for vb in range(3):
-            block = done_c[pl.ds(vb * 32 + 4 * g, 32, stride=96), :]
+            block = done[pl.ds(vb * 32 + 4 * g, 32, stride=PITCH_CV), :]
             for j in range(1, 4):
-                part = done_c[pl.ds(vb * 32 + 4 * g + j, 32, stride=96), :]
-                block = jnp.where(lane32 == j, pltpu.roll(part, 32 * j, 1), block)
+                part = done[pl.ds(vb * 32 + 4 * g + j, 32, stride=PITCH_CV), :]
+                block = jnp.where(lane == j, pltpu.roll(part, 32 * j, 1), block)
             if vb == 0:
-                send_dn[4, :, pl.ds(at, 128)] = block.astype(BF)
+                send_dn[:, pl.ds(at, 128)] = block.astype(BF)
             elif vb == 2:
-                send_up[4, :, pl.ds(at, 128)] = block.astype(BF)
+                send_up[:, pl.ds(at, 128)] = block.astype(BF)
             else:
-                out_c[:, pl.ds(at, 128)] = block
-        return carry
-
-    lax.fori_loop(0, 8, coarse_lanes, 0)
-
-
-def passes(*operands):
+                out[:, pl.ds(at, 128)] = block
+        return carry
+
+    lax.fori_loop(0, 8, relay, 0)
+
+
+def coarse_passes(*operands):
     return call(
-        main_kernel,
+        coarse_kernel,
         (
-            jax.ShapeDtypeStruct((8, 32, 1024), F32),
-            jax.ShapeDtypeStruct((5, 32, 1024), BF),
-            jax.ShapeDtypeStruct((5, 32, 1024), BF),
             jax.ShapeDtypeStruct((32, 1024), F32),
+            jax.ShapeDtypeStruct((32, 1024), BF),
+            jax.ShapeDtypeStruct((32, 1024), BF),
         ),
         [
-            pltpu.VMEM((2048, 512), BF),
-            pltpu.VMEM((16, 128, 256), BF),
-            pltpu.VMEM((16384, 128), F32),
-            pltpu.VMEM((8192, 128), F32),
             pltpu.VMEM((768, 384), BF),
             pltpu.VMEM((8, 96, 256), BF),
-            pltpu.VMEM((2048, 128), F32),
-            pltpu.VMEM((3072, 128), F32),
+            pltpu.VMEM((64 * PITCH_CU, 128), F32),
+            pltpu.VMEM((32 * PITCH_CV, 128), F32),
         ],
     )(*operands)
 
 
-def final_kernel(own, own_c, low, high, fz, ky, st2, out, rows, mixed, deep):
-    total = own_c[...] + low[4].astype(F32) + high[4].astype(F32)
+def final_kernel(own, own_c, low, high, low_c, high_c, fz, ky, st2, out, rows, mixed, deep):
+    total = own_c[...] + low_c[...].astype(F32) + high_c[...].astype(F32)
     hi, lo = split(total)
     for g in range(8):
         rows[g * 64 : g * 64 + 32, :] = hi[:, g * 128 : g * 128 + 128]
@@ -394,16 +412,20 @@
     czm = shift(par, 1)
     czp = shift(par, -1)
 
-    far_up = jnp.concatenate([zm[2:], zp[2:], par[None], czm[None], czp[None]], axis=0)
-    far_dn = jnp.concatenate([zm[:2], zp[:2], par[None], czm[None], czp[None]], axis=0)
-    xm_far = shift(far_up, 16)
-    xp_far = shift(far_dn, -16)
-
-    made = weights(term_exponent, fine_blocks, coarse_blocks)
-    out, send_up, send_dn, out_c = passes(own, zm, zp, xm_own, xp_own, xm_far, xp_far, par, czm, czp, *made)
+    xm_far = shift(jnp.concatenate([zm[2:], zp[2:]], axis=0), 16)
+    xp_far = shift(jnp.concatenate([zm[:2], zp[:2]], axis=0), -16)
+    wz, wx, my, cwz, cwx, cmy = weights(term_exponent, fine_blocks, coarse_blocks)
+    planes = jnp.stack([par, czm, czp])
+    cxm = shift(planes, 16)
+    cxp = shift(planes, -16)
+
+    out, send_up, send_dn = fine_passes(own, zm, zp, xm_own, xp_own, xm_far, xp_far, wz, wx, my)
     low = shift(send_up, 4)
     high = shift(send_dn, -4)
-    total = finish(out, out_c, low, high, fz, ky, st2)
+    out_c, send_up_c, send_dn_c = coarse_passes(par, czm, czp, cxm, cxp, cwz, cwx, cmy)
+    low_c = shift(send_up_c, 4)
+    high_c = shift(send_dn_c, -4)
+    total = finish(out, out_c, low, high, low_c, high_c, fz, ky, st2)
     groups = lax.axis_size("term")
     mine = lax.all_to_all(total.reshape(groups, 2, 32, 1024), "term", 0, 0)
     return mine.astype(F32)

time: 117 us -> 103 us (0.88)
  Pallas kernels: 49.7 us -> 32 us
  starting transfers between devices: 16.9 us -> 31.2 us
  local copies, waits for them, and re-layouts: 6.28 us -> 2.75 us
  blocking collectives: 16.1 us -> 12.9 us
  waiting for transfers between devices: 25.3 us -> 22.2 us
    ppermute x8 -> x12, starting transfers between devices: 11.2 us -> 25.5 us  [shift(): lax.ppermute(block, 'box', [(i, (i + distance) % count) for i in range(co...]
    pallas_call x1 -> x2, Pallas kernels: 35.4 us -> 25.4 us  [the longest x1 17.5 us: fine_passes(): call(fine_kernel, (jax.ShapeDtypeStruct((8, 32, 1024), F32), jax.ShapeDty...]
    pallas_call x1, Pallas kernels: 5.34 us -> 1.8 us  [finish(): call(final_kernel, jax.ShapeDtypeStruct((8, 32, 1024), BF), [pltpu.VMEM((...]
    all_to_all x1, blocking collectives: 16.1 us -> 12.9 us  [steps(): mine = lax.all_to_all(total.reshape(groups, 2, 32, 1024), 'term', 0, 0)]
    unnamed x24 -> x8, local copies, waits for them, and re-layouts: 2.85 us -> 0.03 us
    pallas_call x1, Pallas kernels: 3.97 us -> 1.79 us  [parents_of(): call(parent_kernel, (jax.ShapeDtypeStruct((32, 1024), BF), jax.ShapeDtype...]
    ppermute x8 -> x12, waiting for transfers between devices: 16.9 us -> 14.8 us  [shift(): lax.ppermute(block, 'box', [(i, (i + distance) % count) for i in range(co...]
    pallas_call x1, Pallas kernels: 4.98 us -> 2.97 us  [weights(): pl.pallas_call(weight_kernel, out_shape=(jax.ShapeDtypeStruct((8, 512, 25...]
  transfers between devices with their start and end apart: 10 -> 14, of which waited for: 5 -> 6; matrix products, arithmetic and copies ran while one was open for 2% -> 1% of each run, Pallas kernels for 8% -> 29%
where the time goes in v3:
time: 103 us; the launch traced here: 102 us
  Pallas kernels  32 us (31%)
  starting transfers between devices  31.2 us (30%)
  waiting for transfers between devices  22.2 us (22%)
  blocking collectives  12.9 us (13%)
  local copies, waits for them, and re-layouts  2.75 us (3%)
  other arithmetic  1.17 us (1%)
    ppermute x12, starting transfers between devices, shift(): lax.ppermute(block, 'box', [(i, (i + distance) % count) for i in range(co...  25.5 us
    pallas_call x1, Pallas kernels, fine_passes(): call(fine_kernel, (jax.ShapeDtypeStruct((8, 32, 1024), F32), jax.ShapeDty...  17.5 us
    ppermute x12, waiting for transfers between devices, shift(): lax.ppermute(block, 'box', [(i, (i + distance) % count) for i in range(co...  14.8 us
    all_to_all x1, blocking collectives, steps(): mine = lax.all_to_all(total.reshape(groups, 2, 32, 1024), 'term', 0, 0)  12.9 us
    pallas_call x1, Pallas kernels, coarse_passes(): call(coarse_kernel, (jax.ShapeDtypeStruct((32, 1024), F32), jax.ShapeDtyp...  7.92 us
    ppermute x2, waiting for transfers between devices, shift_z(): return lax.ppermute(block, ('box', 'term'), route)  7.47 us
    ppermute x2, starting transfers between devices, shift_z(): return lax.ppermute(block, ('box', 'term'), route)  5.65 us
    pallas_call x1, Pallas kernels, weights(): pl.pallas_call(weight_kernel, out_shape=(jax.ShapeDtypeStruct((8, 512, 25...  2.97 us
  transfers between devices with their start and end apart: 14, of which 6 were waited for; matrix products, arithmetic and copies ran while one was open for 1% of the time, Pallas kernels for 29%

profile of v3, /device:TPU:30, one launch (start us, length us, event | category | flops | bytes accessed | tf_op | source)
XLA Modules:
  0.0 102.4 jit_solution(8482456097053145484)
XLA Ops:
  0.0 1.6 %constant_dynamic-slice_fusion = (bf16[1,8,32,1024]{3,2,1,0:T(8,128)(2,1)S(1)}, bf16[8,32,1024]{2,1,0:T(8,128)(2,1)S(1)}, bf16[1,8,32,1024]{3,2,1,0:T(8,128)(2,1)S(1)}) fusion(bf16[4,8,32,1024]{3,2,1,0:T(8,128)(2,1)} %param.5, s32[]{:T(128)S(6)} %select_n.30, s32[]{:T(128)S(6)} %select_n.25, s32[]{:T(128)S(6)} %select_n.28), kind=kLoop, calls=%fused_computation.8 | loop fusion | bytes 3145740 | tf_op jit(solution)/shard_map/jit(dynamic_index_in_dim)/dynamic_slice | solution.py:397
  1.6 0.0 copy-start.2
  1.6 0.1 collective-permute-start
  1.7 0.0 copy-start
  1.7 0.0 copy-start.1
  1.7 0.0 copy-start.3
  1.8 5.6 %collective-permute-start.1 = (bf16[4,32,1024]{2,1,0:T(8,128)(2,1)S(1)}, bf16[4,32,1024]{2,1,0:T(8,128)(2,1)S(1)}, u32[]{:S(2)}, u32[]{:S(2)}) collective-permute-start(bf16[4,32,1024]{2,1,0:T(8,128)(2,1)S(1)} %slice_bitcast_fusion), channel_id=1, source_target_pairs={{0,255},{1,254},{2,253},{3,252},{4,0},{5,1},{6,2},{7,3},{8,7},{9,6... | collective-permute-start | bytes 786440 | tf_op jit(solution)/shard_map/ppermute | solution.py:391
  7.3 1.1 %dynamic-slice_bitcast_fusion.1 = (bf16[4,32,1024]{2,1,0:T(8,128)(2,1)S(1)}, bf16[4,32,1024]{2,1,0:T(8,128)(2,1)S(1)}) fusion(bf16[4,8,32,1024]{3,2,1,0:T(8,128)(2,1)} %param.5, s32[]{:T(128)S(6)} %select_n.25, s32[]{:T(128)S(6)} %add.19), kind=kLoop, calls=%fused_computation.1 | loop fusion | bytes 1048584 | tf_op jit(solution)/shard_map/slice | solution.py:409
  8.4 0.8 collective-permute-start.3
  9.2 2.5 %collective-permute-start.2 = (bf16[4,32,1024]{2,1,0:T(8,128)(2,1)S(1)}, bf16[4,32,1024]{2,1,0:T(8,128)(2,1)S(1)}, u32[]{:S(2)}, u32[]{:S(2)}) collective-permute-start(bf16[4,32,1024]{2,1,0:T(8,128)(2,1)S(1)} %get-tuple-element.38), channel_id=1, source_target_pairs={{0,64},{4,68},{8,72},{12,76},{16,80},{20,84},{24,88},{28,92},{32,9... | collective-permute-start | bytes 786440 | tf_op jit(solution)/shard_map/ppermute | solution.py:377
  11.7 6.8 %collective-permute-done.zm = bf16[4,32,1024]{2,1,0:T(8,128)(2,1)S(1)} collective-permute-done((bf16[4,32,1024]{2,1,0:T(8,128)(2,1)S(1)}, bf16[4,32,1024]{2,1,0:T(8,128)(2,1)S(1)}, u32[]{:S(2)}, u32[]{:S(2)}) %collective-permute-start) | collective-permute-done | bytes 262176 | tf_op jit(solution)/shard_map/ppermute | solution.py:391
  18.6 0.6 collective-permute-done.1.zp
  19.3 0.3 collective-permute-start.4
  19.6 1.9 %collective-permute-start.5 = (bf16[4,32,1024]{2,1,0:T(8,128)(2,1)S(1)}, bf16[4,32,1024]{2,1,0:T(8,128)(2,1)S(1)}, u32[]{:S(2)}, u32[]{:S(2)}) collective-permute-start(bf16[4,32,1024]{2,1,0:T(8,128)(2,1)S(1)} %pad_maximum_fusion.1), channel_id=1, source_target_pairs={{0,192},{4,196},{8,200},{12,204},{16,208},{20,212},{24,216},{28,22... | collective-permute-start | bytes 786440 | tf_op jit(solution)/shard_map/ppermute | solution.py:377
  21.5 0.0 copy-done.2
  21.5 1.8 %shard_map.56 = (bf16[32,1024]{1,0:T(8,128)(2,1)S(1)}, bf16[256,128]{1,0:T(8,128)(2,1)S(1)}, bf16[2048,1024]{1,0:T(8,128)(2,1)S(1)}, bf16[64,64]{1,0:T(8,128)(2,1)S(1)}) custom-call(bf16[8,32,1024]{2,1,0:T(8,128)(2,1)S(1)} %get-tuple-element.40.own, bf16[32,64]{1,0:T(8,128)(2,1)S(1)} %copy-done.2), custom_call_target="tpu_custom_call" | custom-call | tf_op jit(solution)/shard_map/pallas_call | solution.py:149
  23.3 4.9 %collective-permute-start.7 = (bf16[32,1024]{1,0:T(8,128)(2,1)S(1)}, bf16[32,1024]{1,0:T(8,128)(2,1)S(1)}, u32[]{:S(2)}, u32[]{:S(2)}) collective-permute-start(bf16[32,1024]{1,0:T(8,128)(2,1)S(1)} %get-tuple-element.25.par), channel_id=1, source_target_pairs={{0,252},{4,0},{8,4},{12,8},{16,12},{20,16},{24,20},{28,24},{32,28}... | collective-permute-start | bytes 196616 | tf_op jit(solution)/shard_map/ppermute | solution.py:377
  28.2 1.9 %collective-permute-done.7.zp = bf16[32,1024]{1,0:T(8,128)(2,1)S(1)} collective-permute-done((bf16[32,1024]{1,0:T(8,128)(2,1)S(1)}, bf16[32,1024]{1,0:T(8,128)(2,1)S(1)}, u32[]{:S(2)}, u32[]{:S(2)}) %collective-permute-start.7) | collective-permute-done | bytes 65568 | tf_op jit(solution)/shard_map/ppermute | solution.py:377
  30.1 0.3 collective-permute-start.6
  30.4 0.0 copy-done
  30.4 0.0 copy-done.1
  30.4 0.0 copy-done.3
  30.4 3.0 %weights.1 = (bf16[8,512,256]{2,1,0:T(8,128)(2,1)S(1)}, bf16[8,64,128]{2,1,0:T(8,128)(2,1)S(1)}, bf16[256,256]{1,0:T(8,128)(2,1)S(1)}, bf16[8,384,128]{2,1,0:T(8...) custom-call(s32[8]{0:T(128)S(1)} %copy-done.3, bf16[16,3,32,32]{3,2,1,0:T(8,128)(2,1)S(1)} %copy-done, ...), custom_call_target="tpu_custom_call" | custom-call | tf_op jit(solution)/shard_map/weights/pallas_call | solution.py:89
  33.4 5.3 %collective-permute-done.6.zm = bf16[32,1024]{1,0:T(8,128)(2,1)S(1)} collective-permute-done((bf16[32,1024]{1,0:T(8,128)(2,1)S(1)}, bf16[32,1024]{1,0:T(8,128)(2,1)S(1)}, u32[]{:S(2)}, u32[]{:S(2)}) %collective-permute-start.6) | collective-permute-done | bytes 65568 | tf_op jit(solution)/shard_map/ppermute | solution.py:377
  38.7 0.8 collective-permute-start.9
  39.5 0.0 collective-permute-done.3.xp_own
  39.5 2.5 %collective-permute-start.8 = (bf16[3,32,1024]{2,1,0:T(8,128)(2,1)S(1)}, bf16[3,32,1024]{2,1,0:T(8,128)(2,1)S(1)}, u32[]{:S(2)}, u32[]{:S(2)}) collective-permute-start(bf16[3,32,1024]{2,1,0:T(8,128)(2,1)S(1)} %pad_maximum_fusion.2), channel_id=1, source_target_pairs={{0,64},{4,68},{8,72},{12,76},{16,80},{20,84},{24,88},{28,92},{32,9... | collective-permute-start | bytes 589832 | tf_op jit(solution)/shard_map/ppermute | solution.py:377
  42.0 0.0 collective-permute-done.2.xm_own
  42.0 0.0 collective-permute-done.4.xm_far
  42.0 0.0 collective-permute-done.5.xp_far
  42.0 17.5 %shard_map.55 = (f32[8,32,1024]{2,1,0:T(8,128)S(1)}, bf16[4,32,1024]{2,1,0:T(8,128)(2,1)S(1)}, bf16[4,32,1024]{2,1,0:T(8,128)(2,1)S(1)}) custom-call(bf16[8,32,1024]{2,1,0:T(8,128)(2,1)S(1)} %get-tuple-element.40.own, bf16[4,32,1024]{2,1,0:T(8,128)(2,1)S(1)} %collective-permute-done.zm, bf16[4,32,1024]{2,1,0:T(8,128)(2,1)S(1)} %collective-permute-done.1.zp, ...), custom_call_target="tpu_custom_call" | custom-call | tf_op jit(solution)/shard_map/pallas_call | solution.py:241
  59.5 6.1 %collective-permute-start.10 = (bf16[4,32,1024]{2,1,0:T(8,128)(2,1)S(1)}, bf16[4,32,1024]{2,1,0:T(8,128)(2,1)S(1)}, u32[]{:S(2)}, u32[]{:S(2)}) collective-permute-start(bf16[4,32,1024]{2,1,0:T(8,128)(2,1)S(1)} %get-tuple-element.30), channel_id=1, source_target_pairs={{0,16},{4,20},{8,24},{12,28},{16,32},{20,36},{24,40},{28,44},{32,4... | collective-permute-start | bytes 786440 | tf_op jit(solution)/shard_map/ppermute | solution.py:377
  65.6 0.0 collective-permute-start.11
  65.6 0.0 collective-permute-done.9.xp
  65.6 0.0 collective-permute-done.8.xm
  65.7 7.9 %shard_map.57 = (f32[32,1024]{1,0:T(8,128)S(1)}, bf16[32,1024]{1,0:T(8,128)(2,1)S(1)}, bf16[32,1024]{1,0:T(8,128)(2,1)S(1)}) custom-call(bf16[32,1024]{1,0:T(8,128)(2,1)S(1)} %get-tuple-element.25.par, bf16[32,1024]{1,0:T(8,128)(2,1)S(1)} %collective-permute-done.6.zm, bf16[32,1024]{1,0:T(8,128)(2,1)S(1)} %collective-permute-done.7.zp, ...), custom_call_target="tpu_custom_call" | custom-call | tf_op jit(solution)/shard_map/pallas_call | solution.py:324
  73.6 5.4 %collective-permute-start.12 = (bf16[32,1024]{1,0:T(8,128)(2,1)S(1)}, bf16[32,1024]{1,0:T(8,128)(2,1)S(1)}, u32[]{:S(2)}, u32[]{:S(2)}) collective-permute-start(bf16[32,1024]{1,0:T(8,128)(2,1)S(1)} %get-tuple-element.32), channel_id=1, source_target_pairs={{0,16},{4,20},{8,24},{12,28},{16,32},{20,36},{24,40},{28,44},{32,4... | collective-permute-start | bytes 196616 | tf_op jit(solution)/shard_map/ppermute | solution.py:377
  79.0 0.0 collective-permute-start.13
  79.0 1.9 %collective-permute-done.12.low_c = bf16[32,1024]{1,0:T(8,128)(2,1)S(1)} collective-permute-done((bf16[32,1024]{1,0:T(8,128)(2,1)S(1)}, bf16[32,1024]{1,0:T(8,128)(2,1)S(1)}, u32[]{:S(2)}, u32[]{:S(2)}) %collective-permute-start.12) | collective-permute-done | bytes 65568 | tf_op jit(solution)/shard_map/ppermute | solution.py:377
  80.9 5.7 %collective-permute-done.13.high_c = bf16[32,1024]{1,0:T(8,128)(2,1)S(1)} collective-permute-done((bf16[32,1024]{1,0:T(8,128)(2,1)S(1)}, bf16[32,1024]{1,0:T(8,128)(2,1)S(1)}, u32[]{:S(2)}, u32[]{:S(2)}) %collective-permute-start.13) | collective-permute-done | bytes 65568 | tf_op jit(solution)/shard_map/ppermute | solution.py:377
  86.6 0.0 collective-permute-done.10.low
  86.6 0.0 collective-permute-done.11.high
  86.6 1.8 %shard_map.58 = bf16[8,32,1024]{2,1,0:T(8,128)(2,1)S(1)} custom-call(f32[8,32,1024]{2,1,0:T(8,128)S(1)} %get-tuple-element.24.own, f32[32,1024]{1,0:T(8,128)S(1)} %get-tuple-element.29.own_c, bf16[4,32,1024]{2,1,0:T(8,128)(2,1)S(1)} %collective-permute-done.10.low, bf16[4,32,1024]{2,1,0:T(8,128)(2,1)S(1)} %collective-permute-done.11.high, ...), custom_call_target="tpu_custom_call" | custom-call | tf_op jit(solution)/shard_map/pallas_call | solution.py:368
  88.4 12.9 %all_to_all.5 = bf16[4,2,32,1024]{3,2,1,0:T(8,128)(2,1)S(1)} all-to-all(bf16[4,2,32,1024]{3,2,1,0:T(8,128)(2,1)S(1)} %bitcast.20), channel_id=1, replica_groups=mesh['box'=64,'term'=4] {'term'}, dimensions={0} | all-to-all | bytes 1048576 | tf_op jit(solution)/shard_map/all_to_all | solution.py:430
  101.3 1.1 %convert_element_type.3 = f32[4,2,32,1024]{3,2,1,0:T(8,128)} convert(bf16[4,2,32,1024]{3,2,1,0:T(8,128)(2,1)S(1)} %all_to_all.5) | non-fusion elementwise | flops 262144 | bytes 1572864 | tf_op jit(solution)/shard_map/convert_element_type | solution.py:431
  (7 shorter events, 0.1 us)
Async XLA Ops:
  1.6 19.9 %copy-start.2 = (bf16[32,64]{1,0:T(8,128)(2,1)S(1)}, bf16[32,64]{1,0:T(8,128)(2,1)}, u32[]{:S(2)}) copy-start(bf16[32,64]{1,0:T(8,128)(2,1)} %s.1) | copy-start | bytes 12292
  1.6 17.0 %collective-permute-start = (bf16[4,32,1024]{2,1,0:T(8,128)(2,1)S(1)}, bf16[4,32,1024]{2,1,0:T(8,128)(2,1)S(1)}, u32[]{:S(2)}, u32[]{:S(2)}) collective-permute-start(bf16[4,32,1024]{2,1,0:T(8,128)(2,1)S(1)} %slice_bitcast_fusion.1), channel_id=1, source_target_pairs={{0,4},{1,5},{2,6},{3,7},{4,11},{5,10},{6,9},{7,8},{8,12},{9,13},{1... | collective-permute-start | bytes 786440 | tf_op jit(solution)/shard_map/ppermute | solution.py:391
  1.7 28.7 %copy-start = (bf16[16,3,32,32]{3,2,1,0:T(8,128)(2,1)S(1)}, bf16[16,3,32,32]{3,2,1,0:T(8,128)(2,1)}, u32[]{:S(2)}) copy-start(bf16[16,3,32,32]{3,2,1,0:T(8,128)(2,1)} %fine.1) | copy-start | bytes 294916
  1.7 28.7 %copy-start.1 = (bf16[16,3,32,32]{3,2,1,0:T(8,128)(2,1)S(1)}, bf16[16,3,32,32]{3,2,1,0:T(8,128)(2,1)}, u32[]{:S(2)}) copy-start(bf16[16,3,32,32]{3,2,1,0:T(8,128)(2,1)} %coarse.1) | copy-start | bytes 294916
  1.7 28.7 %copy-start.3 = (s32[8]{0:T(128)S(1)}, s32[8]{0:T(128)}, u32[]{:S(2)}) copy-start(s32[8]{0:T(128)} %exponents.1) | copy-start | bytes 100
  1.8 17.5 %collective-permute-start.1 = (bf16[4,32,1024]{2,1,0:T(8,128)(2,1)S(1)}, bf16[4,32,1024]{2,1,0:T(8,128)(2,1)S(1)}, u32[]{:S(2)}, u32[]{:S(2)}) collective-permute-start(bf16[4,32,1024]{2,1,0:T(8,128)(2,1)S(1)} %slice_bitcast_fusion), channel_id=1, source_target_pairs={{0,255},{1,254},{2,253},{3,252},{4,0},{5,1},{6,2},{7,3},{8,7},{9,6... | collective-permute-start | bytes 786440 | tf_op jit(solution)/shard_map/ppermute | solution.py:391
  8.4 31.1 %collective-permute-start.3 = (bf16[4,32,1024]{2,1,0:T(8,128)(2,1)S(1)}, bf16[4,32,1024]{2,1,0:T(8,128)(2,1)S(1)}, u32[]{:S(2)}, u32[]{:S(2)}) collective-permute-start(bf16[4,32,1024]{2,1,0:T(8,128)(2,1)S(1)} %get-tuple-element.37), channel_id=1, source_target_pairs={{0,192},{4,196},{8,200},{12,204},{16,208},{20,212},{24,216},{28,22... | collective-permute-start | bytes 786440 | tf_op jit(solution)/shard_map/ppermute | solution.py:377
  9.2 32.8 %collective-permute-start.2 = (bf16[4,32,1024]{2,1,0:T(8,128)(2,1)S(1)}, bf16[4,32,1024]{2,1,0:T(8,128)(2,1)S(1)}, u32[]{:S(2)}, u32[]{:S(2)}) collective-permute-start(bf16[4,32,1024]{2,1,0:T(8,128)(2,1)S(1)} %get-tuple-element.38), channel_id=1, source_target_pairs={{0,64},{4,68},{8,72},{12,76},{16,80},{20,84},{24,88},{28,92},{32,9... | collective-permute-start | bytes 786440 | tf_op jit(solution)/shard_map/ppermute | solution.py:377
  19.3 22.7 %collective-permute-start.4 = (bf16[4,32,1024]{2,1,0:T(8,128)(2,1)S(1)}, bf16[4,32,1024]{2,1,0:T(8,128)(2,1)S(1)}, u32[]{:S(2)}, u32[]{:S(2)}) collective-permute-start(bf16[4,32,1024]{2,1,0:T(8,128)(2,1)S(1)} %pad_maximum_fusion), channel_id=1, source_target_pairs={{0,64},{4,68},{8,72},{12,76},{16,80},{20,84},{24,88},{28,92},{32,9... | collective-permute-start | bytes 786440 | tf_op jit(solution)/shard_map/ppermute | solution.py:377
  19.6 22.4 %collective-permute-start.5 = (bf16[4,32,1024]{2,1,0:T(8,128)(2,1)S(1)}, bf16[4,32,1024]{2,1,0:T(8,128)(2,1)S(1)}, u32[]{:S(2)}, u32[]{:S(2)}) collective-permute-start(bf16[4,32,1024]{2,1,0:T(8,128)(2,1)S(1)} %pad_maximum_fusion.1), channel_id=1, source_target_pairs={{0,192},{4,196},{8,200},{12,204},{16,208},{20,212},{24,216},{28,22... | collective-permute-start | bytes 786440 | tf_op jit(solution)/shard_map/ppermute | solution.py:377
  23.3 6.8 %collective-permute-start.7 = (bf16[32,1024]{1,0:T(8,128)(2,1)S(1)}, bf16[32,1024]{1,0:T(8,128)(2,1)S(1)}, u32[]{:S(2)}, u32[]{:S(2)}) collective-permute-start(bf16[32,1024]{1,0:T(8,128)(2,1)S(1)} %get-tuple-element.25.par), channel_id=1, source_target_pairs={{0,252},{4,0},{8,4},{12,8},{16,12},{20,16},{24,20},{28,24},{32,28}... | collective-permute-start | bytes 196616 | tf_op jit(solution)/shard_map/ppermute | solution.py:377
  30.1 8.5 %collective-permute-start.6 = (bf16[32,1024]{1,0:T(8,128)(2,1)S(1)}, bf16[32,1024]{1,0:T(8,128)(2,1)S(1)}, u32[]{:S(2)}, u32[]{:S(2)}) collective-permute-start(bf16[32,1024]{1,0:T(8,128)(2,1)S(1)} %get-tuple-element.25.par), channel_id=1, source_target_pairs={{0,4},{4,8},{8,12},{12,16},{16,20},{20,24},{24,28},{28,32},{32,36}... | collective-permute-start | bytes 196616 | tf_op jit(solution)/shard_map/ppermute | solution.py:377
  38.7 26.9 %collective-permute-start.9 = (bf16[3,32,1024]{2,1,0:T(8,128)(2,1)S(1)}, bf16[3,32,1024]{2,1,0:T(8,128)(2,1)S(1)}, u32[]{:S(2)}, u32[]{:S(2)}) collective-permute-start(bf16[3,32,1024]{2,1,0:T(8,128)(2,1)S(1)} %pad_maximum_fusion.2), channel_id=1, source_target_pairs={{0,192},{4,196},{8,200},{12,204},{16,208},{20,212},{24,216},{28,22... | collective-permute-start | bytes 589832 | tf_op jit(solution)/shard_map/ppermute | solution.py:377
  39.5 26.1 %collective-permute-start.8 = (bf16[3,32,1024]{2,1,0:T(8,128)(2,1)S(1)}, bf16[3,32,1024]{2,1,0:T(8,128)(2,1)S(1)}, u32[]{:S(2)}, u32[]{:S(2)}) collective-permute-start(bf16[3,32,1024]{2,1,0:T(8,128)(2,1)S(1)} %pad_maximum_fusion.2), channel_id=1, source_target_pairs={{0,64},{4,68},{8,72},{12,76},{16,80},{20,84},{24,88},{28,92},{32,9... | collective-permute-start | bytes 589832 | tf_op jit(solution)/shard_map/ppermute | solution.py:377
  59.5 27.0 %collective-permute-start.10 = (bf16[4,32,1024]{2,1,0:T(8,128)(2,1)S(1)}, bf16[4,32,1024]{2,1,0:T(8,128)(2,1)S(1)}, u32[]{:S(2)}, u32[]{:S(2)}) collective-permute-start(bf16[4,32,1024]{2,1,0:T(8,128)(2,1)S(1)} %get-tuple-element.30), channel_id=1, source_target_pairs={{0,16},{4,20},{8,24},{12,28},{16,32},{20,36},{24,40},{28,44},{32,4... | collective-permute-start | bytes 786440 | tf_op jit(solution)/shard_map/ppermute | solution.py:377
  65.6 20.9 %collective-permute-start.11 = (bf16[4,32,1024]{2,1,0:T(8,128)(2,1)S(1)}, bf16[4,32,1024]{2,1,0:T(8,128)(2,1)S(1)}, u32[]{:S(2)}, u32[]{:S(2)}) collective-permute-start(bf16[4,32,1024]{2,1,0:T(8,128)(2,1)S(1)} %get-tuple-element.31), channel_id=1, source_target_pairs={{0,240},{4,244},{8,248},{12,252},{16,0},{20,4},{24,8},{28,12},{32,... | collective-permute-start | bytes 786440 | tf_op jit(solution)/shard_map/ppermute | solution.py:377
  73.6 7.3 %collective-permute-start.12 = (bf16[32,1024]{1,0:T(8,128)(2,1)S(1)}, bf16[32,1024]{1,0:T(8,128)(2,1)S(1)}, u32[]{:S(2)}, u32[]{:S(2)}) collective-permute-start(bf16[32,1024]{1,0:T(8,128)(2,1)S(1)} %get-tuple-element.32), channel_id=1, source_target_pairs={{0,16},{4,20},{8,24},{12,28},{16,32},{20,36},{24,40},{28,44},{32,4... | collective-permute-start | bytes 196616 | tf_op jit(solution)/shard_map/ppermute | solution.py:377
  79.0 7.6 %collective-permute-start.13 = (bf16[32,1024]{1,0:T(8,128)(2,1)S(1)}, bf16[32,1024]{1,0:T(8,128)(2,1)S(1)}, u32[]{:S(2)}, u32[]{:S(2)}) collective-permute-start(bf16[32,1024]{1,0:T(8,128)(2,1)S(1)} %get-tuple-element.33), channel_id=1, source_target_pairs={{0,240},{4,244},{8,248},{12,252},{16,0},{20,4},{24,8},{28,12},{32,... | collective-permute-start | bytes 196616 | tf_op jit(solution)/shard_map/ppermute | solution.py:377

commit v4 on v3

--- a/solution.py
+++ b/solution.py
@@ -79,7 +79,10 @@
 
     lax.fori_loop(0, 8, term, 0)
     for parity in range(2):
-        my[parity * 128 : parity * 128 + 128, :] = dot_t(eye, tall[parity].astype(BF)).astype(BF)
+        moved = dot_t(eye, tall[parity].astype(BF)).astype(BF)
+        my[0, parity * 64 : parity * 64 + 32, :] = moved[:32]
+        my[0, parity * 64 + 32 : parity * 64 + 64, :] = moved[96:]
+        my[1, parity * 64 : parity * 64 + 64, :] = moved[32:96]
     for parity in range(4):
         cmy[parity * 96 : parity * 96 + 96, :] = dot_t(eye[:96, :96], tall_c[parity].astype(BF)).astype(BF)
 
@@ -91,7 +94,7 @@
         out_shape=(
             jax.ShapeDtypeStruct((8, 512, 256), BF),
             jax.ShapeDtypeStruct((8, 64, 128), BF),
-            jax.ShapeDtypeStruct((256, 256), BF),
+            jax.ShapeDtypeStruct((2, 128, 256), BF),
             jax.ShapeDtypeStruct((8, 384, 128), BF),
             jax.ShapeDtypeStruct((8, 32, 96), BF),
             jax.ShapeDtypeStruct((384, 64), BF),
@@ -111,87 +114,153 @@
     )(exponents, fine, coarse)
 
 
-def parent_kernel(own, s, out, fz, ky, st2, rows, wide):
+def parent_kernel(where, boxes, s, out, up, dn, fz, ky, st2, rows, wide):
+    step = pl.program_id(0)
     scale = s[...]
-    tiled = lax.dot_general(
-        scale, same(32, 128, lambda i, j: j % 32 == i), (((0,), (0,)), ((), ())), preferred_element_type=F32
-    )
-    block = same(128, 128, lambda i, j: i // 32 == j // 32).astype(F32)
-    for cz in range(2):
-        part = tiled[cz * 32 : cz * 32 + 32]
-        fz[cz * 128 : cz * 128 + 128, :] = (jnp.concatenate([part] * 4, axis=0) * block).astype(BF)
-    st2[...] = lax.dot_general(
-        scale, same(32, 64, lambda i, j: j % 32 == i), (((0,), (0,)), ((), ())), preferred_element_type=F32
-    ).astype(BF)
-    spread = lax.dot_general(
-        scale, same(32, 1024, lambda i, j: j // 32 == i), (((0,), (0,)), ((), ())), preferred_element_type=F32
-    )
-    lane = lax.broadcasted_iota(jnp.int32, (32, 1024), 1) % 32 == lax.broadcasted_iota(jnp.int32, (32, 1024), 0)
-    for y in range(64):
-        ky[y * 32 : y * 32 + 32, :] = jnp.where(
-            lane, jnp.broadcast_to(spread[y : y + 1], (32, 1024)), 0.0
+
+    @pl.when(step == 0)
+    def _():
+        tiled = lax.dot_general(
+            scale, same(32, 128, lambda i, j: j % 32 == i), (((0,), (0,)), ((), ())), preferred_element_type=F32
+        )
+        block = same(128, 128, lambda i, j: i // 32 == j // 32).astype(F32)
+        for cz in range(2):
+            part = tiled[cz * 32 : cz * 32 + 32]
+            fz[cz * 128 : cz * 128 + 128, :] = (jnp.concatenate([part] * 4, axis=0) * block).astype(BF)
+        st2[...] = lax.dot_general(
+            scale, same(32, 64, lambda i, j: j % 32 == i), (((0,), (0,)), ((), ())), preferred_element_type=F32
         ).astype(BF)
+        spread = lax.dot_general(
+            scale, same(32, 1024, lambda i, j: j // 32 == i), (((0,), (0,)), ((), ())), preferred_element_type=F32
+        )
+        lane = lax.broadcasted_iota(jnp.int32, (32, 1024), 1) % 32 == lax.broadcasted_iota(jnp.int32, (32, 1024), 0)
+        for y in range(64):
+            ky[y * 32 : y * 32 + 32, :] = jnp.where(
+                lane, jnp.broadcast_to(spread[y : y + 1], (32, 1024)), 0.0
+            ).astype(BF)
+
     for yg in range(16):
         cy, g = divmod(yg, 8)
         for cx in range(2):
             for cz in range(2):
-                rows[yg * 64 + cx * 32 : yg * 64 + cx * 32 + 32, cz * 128 : cz * 128 + 128] = own[
-                    4 * cx + 2 * cy + cz, :, g * 128 : g * 128 + 128
+                rows[yg * 64 + cx * 32 : yg * 64 + cx * 32 + 32, cz * 128 : cz * 128 + 128] = boxes[
+                    0, 4 * cx + 2 * cy + cz, :, g * 128 : g * 128 + 128
                 ]
     along_z = dot(rows[...], fz[...]).astype(BF)
     for yg in range(16):
         wide[:, yg * 128 : yg * 128 + 128] = along_z[yg * 64 : yg * 64 + 64]
     along_y = dot(wide[...], ky[...]).astype(BF)
-    out[...] = dot(scale, along_y).astype(BF)
-
-
-def parents_of(own, s):
-    return call(
+    parent = dot(scale, along_y).astype(BF)
+
+    @pl.when(step == 0)
+    def _():
+        out[...] = parent
+
+    @pl.when(step == where[2])
+    def _():
+        up[...] = parent
+
+    @pl.when(step != where[2])
+    def _():
+        dn[...] = parent
+
+
+def parents_of(where, fine_coeffs, s):
+    def whole(*shape):
+        return pl.BlockSpec(shape, lambda i, w: (0,) * len(shape))
+
+    return pl.pallas_call(
         parent_kernel,
-        (
+        out_shape=(
+            jax.ShapeDtypeStruct((32, 1024), BF),
+            jax.ShapeDtypeStruct((32, 1024), BF),
             jax.ShapeDtypeStruct((32, 1024), BF),
             jax.ShapeDtypeStruct((256, 128), BF),
             jax.ShapeDtypeStruct((2048, 1024), BF),
             jax.ShapeDtypeStruct((64, 64), BF),
         ),
-        [pltpu.VMEM((1024, 256), BF), pltpu.VMEM((64, 2048), BF)],
-    )(own, s)
+        grid_spec=pltpu.PrefetchScalarGridSpec(
+            num_scalar_prefetch=1,
+            grid=(2,),
+            in_specs=[pl.BlockSpec((1, 8, 32, 1024), lambda i, w: (w[i], 0, 0, 0)), whole(32, 64)],
+            out_specs=[
+                whole(32, 1024), whole(32, 1024), whole(32, 1024), whole(256, 128), whole(2048, 1024), whole(64, 64),
+            ],
+            scratch_shapes=[pltpu.VMEM((1024, 256), BF), pltpu.VMEM((64, 2048), BF)],
+        ),
+        interpret=INTERPRET,
+        name="parents",
+        **PARAMS,
+    )(where, fine_coeffs, s)
 
 
 PITCH_U = 68
-PITCH_V = 132
 PITCH_CU = 36
 PITCH_CV = 100
 
 
-def fine_kernel(
-    own, zm, zp, xm_own, xp_own, xm_far, xp_far, wz, wx, my,
-    out, send_up, send_dn,
+def fill_left(left, sources, row):
+    for zb in range(4):
+        for g in range(8):
+            left[row + g * 64 : row + g * 64 + 32, zb * 128 : zb * 128 + 128] = sources[zb][:, g * 128 : g * 128 + 128]
+
+
+def inner_kernel(own, zm, zp, wz, mid, left):
+    for cy in range(2):
+        for cx in range(2):
+            at = 4 * cx + 2 * cy
+            fill_left(left, [zm[2 * cx + cy], own[at], own[at + 1], zp[2 * cx + cy]], cy * 512 + cx * 32)
+
+    def term(t, carry):
+        weight = wz[t]
+        for m in range(2):
+            passed = dot(left[m * 512 : m * 512 + 512, :], weight).astype(BF)
+            mid[t, m * 8 : m * 8 + 8] = passed.reshape(8, 64, 256)
+        return carry
+
+    lax.fori_loop(0, 8, term, 0)
+
+
+def inner_pass(*operands):
+    return call(inner_kernel, jax.ShapeDtypeStruct((8, 16, 64, 256), BF), [pltpu.VMEM((1024, 512), BF)])(*operands)
+
+
+def fold_rows(passed, done, start, pitch):
+    for i in range(4):
+        lanes = passed[:, i * 128 : i * 128 + 128]
+        done[pl.ds(start + i * pitch, 64), :] = lanes[:64] + pltpu.roll(lanes[64:], 64, 1)
+
+
+def gather_lanes(done, first, g, cz, lane):
+    block = None
+    for j in range(4):
+        part = done[pl.ds(first + 4 * g + j, 64, stride=PITCH_U), :]
+        turn = (32 * (j - cz)) % 128
+        moved = pltpu.roll(part, turn, 1) if turn else part
+        block = moved if block is None else jnp.where(lane == j, moved, block)
+    return block
+
+
+def outer_kernel(
+    inner, xm_own, xp_own, xm_far, xp_far, wz, wx, my,
+    send_up, send_dn, packed,
     left, mid, wide, done,
 ):
     for cy in range(2):
-        sources = [
-            [xm_far[cy], xm_own[2 * cy], xm_own[2 * cy + 1], xm_far[2 + cy]],
-            [zm[cy], own[2 * cy], own[2 * cy + 1], zp[cy]],
-            [zm[2 + cy], own[4 + 2 * cy], own[5 + 2 * cy], zp[2 + cy]],
-            [xp_far[cy], xp_own[2 * cy], xp_own[2 * cy + 1], xp_far[2 + cy]],
-        ]
-        for xb in range(4):
-            for zb in range(4):
-                box = sources[xb][zb]
-                for g in range(8):
-                    row = (cy * 8 + g) * 128 + xb * 32
-                    left[row : row + 32, zb * 128 : zb * 128 + 128] = box[:, g * 128 : g * 128 + 128]
+        own = 2 * cy
+        fill_left(left, [xm_far[cy], xm_own[own], xm_own[own + 1], xm_far[2 + cy]], cy * 512)
+        fill_left(left, [xp_far[cy], xp_own[own], xp_own[own + 1], xp_far[2 + cy]], cy * 512 + 32)
 
     def term(t, carry):
         weight = wz[t]
-        for m in range(4):
+        for m in range(2):
             passed = dot(left[m * 512 : m * 512 + 512, :], weight).astype(BF)
-            mid[m * 4 : m * 4 + 4] = passed.reshape(4, 128, 256)
+            mid[m * 8 : m * 8 + 8] = passed.reshape(8, 64, 256)
         weight_x = wx[t]
         start = pl.multiple_of(t * (32 * PITCH_U), 8)
         for yg in range(16):
-            passed = dot(weight_x, mid[yg])
+            data = jnp.concatenate([mid[yg, :32], inner[t, yg], mid[yg, 32:]], axis=0)
+            passed = dot(weight_x, data)
             wide[pl.ds(start + 2 * yg * PITCH_U, 64), :] = passed[:, :128]
             wide[pl.ds(start + (2 * yg + 1) * PITCH_U, 64), :] = passed[:, 128:]
         return carry
@@ -199,59 +268,70 @@
     lax.fori_loop(0, 8, term, 0)
 
     def rows(k, carry):
-        u = 2 * k
         data = jnp.concatenate(
-            [wide[pl.ds(u + i, 256, stride=PITCH_U), :].astype(BF) for i in range(2)], axis=1
+            [wide[pl.ds(4 * k + i, 256, stride=PITCH_U), :].astype(BF) for i in range(4)], axis=1
         )
-        passed = dot(my[...], data)
-        start = pl.multiple_of(k * (2 * PITCH_V), 8)
-        for i in range(2):
-            lanes = passed[:, i * 128 : i * 128 + 128]
-            done[pl.ds(start + i * PITCH_V, 128), :] = lanes[:128] + pltpu.roll(lanes[128:], 64, 1)
-        return carry
-
-    lax.fori_loop(0, 32, rows, 0)
+        packed[k] = data
+        fold_rows(dot(my[0], data), done, pl.multiple_of(k * (4 * PITCH_U), 8), PITCH_U)
+        return carry
+
+    lax.fori_loop(0, 16, rows, 0)
 
     lane = lax.broadcasted_iota(jnp.int32, (64, 128), 1) // 32
 
     def relay(g, carry):
         at = pl.multiple_of(g * 128, 128)
-        for vb in range(4):
-            parts = [done[pl.ds(vb * 32 + 4 * g + j, 64, stride=PITCH_V), :] for j in range(4)]
+        for side in range(2):
+            target = send_up if side else send_dn
             for cz in range(2):
-                block = parts[0] if cz == 0 else pltpu.roll(parts[0], 96, 1)
-                for j in range(1, 4):
-                    turn = (32 * (j - cz)) % 128
-                    moved = pltpu.roll(parts[j], turn, 1) if turn else parts[j]
-                    block = jnp.where(lane == j, moved, block)
+                block = gather_lanes(done, side * 32, g, cz, lane).astype(BF)
                 for cx in range(2):
-                    piece = block[cx * 32 : cx * 32 + 32]
-                    if vb == 0:
-                        send_dn[2 * cx + cz, :, pl.ds(at, 128)] = piece.astype(BF)
-                    elif vb == 3:
-                        send_up[2 * cx + cz, :, pl.ds(at, 128)] = piece.astype(BF)
-                    else:
-                        out[4 * cx + 2 * (vb - 1) + cz, :, pl.ds(at, 128)] = piece
+                    target[2 * cx + cz, :, pl.ds(at, 128)] = block[cx * 32 : cx * 32 + 32]
         return carry
 
     lax.fori_loop(0, 8, relay, 0)
 
 
-def fine_passes(*operands):
+def outer_passes(*operands):
     return call(
-        fine_kernel,
+        outer_kernel,
         (
-            jax.ShapeDtypeStruct((8, 32, 1024), F32),
             jax.ShapeDtypeStruct((4, 32, 1024), BF),
             jax.ShapeDtypeStruct((4, 32, 1024), BF),
+            jax.ShapeDtypeStruct((16, 256, 512), BF),
         ),
         [
-            pltpu.VMEM((2048, 512), BF),
-            pltpu.VMEM((16, 128, 256), BF),
+            pltpu.VMEM((1024, 512), BF),
+            pltpu.VMEM((16, 64, 256), BF),
             pltpu.VMEM((256 * PITCH_U, 128), F32),
-            pltpu.VMEM((64 * PITCH_V, 128), F32),
+            pltpu.VMEM((64 * PITCH_U, 128), F32),
         ],
     )(*operands)
+
+
+def own_kernel(packed, my, out, done):
+    def rows(k, carry):
+        fold_rows(dot(my[1], packed[k]), done, pl.multiple_of(k * (4 * PITCH_U), 8), PITCH_U)
+        return carry
+
+    lax.fori_loop(0, 16, rows, 0)
+
+    lane = lax.broadcasted_iota(jnp.int32, (64, 128), 1) // 32
+
+    def relay(g, carry):
+        at = pl.multiple_of(g * 128, 128)
+        for cy in range(2):
+            for cz in range(2):
+                block = gather_lanes(done, cy * 32, g, cz, lane)
+                for cx in range(2):
+                    out[4 * cx + 2 * cy + cz, :, pl.ds(at, 128)] = block[cx * 32 : cx * 32 + 32]
+        return carry
+
+    lax.fori_loop(0, 8, relay, 0)
+
+
+def own_rows(*operands):
+    return call(own_kernel, jax.ShapeDtypeStruct((8, 32, 1024), F32), [pltpu.VMEM((64 * PITCH_U, 128), F32)])(*operands)
 
 
 def coarse_kernel(par, zm, zp, xm, xp, wz, wx, my, out, send_up, send_dn, left, mid, wide, done):
@@ -284,13 +364,12 @@
     lax.fori_loop(0, 4, pair, 0)
 
     def rows(k, carry):
-        u = 2 * k
         data = jnp.concatenate(
-            [wide[pl.ds(u + i, 64, stride=PITCH_CU), :].astype(BF) for i in range(2)], axis=1
+            [wide[pl.ds(4 * k + i, 64, stride=PITCH_CU), :].astype(BF) for i in range(4)], axis=1
         )
         passed = dot(my[...], data)
-        start = pl.multiple_of(k * (2 * PITCH_CV), 8)
-        for i in range(2):
+        start = pl.multiple_of(k * (4 * PITCH_CV), 8)
+        for i in range(4):
             lanes = passed[:, i * 128 : i * 128 + 128]
             total = lanes[:96]
             for j in range(1, 4):
@@ -298,7 +377,7 @@
             done[pl.ds(start + i * PITCH_CV, 96), :] = total
         return carry
 
-    lax.fori_loop(0, 16, rows, 0)
+    lax.fori_loop(0, 8, rows, 0)
 
     lane = lax.broadcasted_iota(jnp.int32, (32, 128), 1) // 32
 
@@ -408,23 +487,26 @@
     xm_own = shift(own[4:], 16)
     xp_own = shift(own[:4], -16)
 
-    par, fz, ky, st2 = parents_of(own, two_scale)
-    czm = shift(par, 1)
-    czp = shift(par, -1)
-
+    other = lax.axis_size("term") - 1 - t
+    where = jnp.stack([t, other, p % 2]).astype(jnp.int32)
+    par, par_up, par_dn, fz, ky, st2 = parents_of(where, fine_coeffs, two_scale)
+    wz, wx, my, cwz, cwx, cmy = weights(term_exponent, fine_blocks, coarse_blocks)
     xm_far = shift(jnp.concatenate([zm[2:], zp[2:]], axis=0), 16)
     xp_far = shift(jnp.concatenate([zm[:2], zp[:2]], axis=0), -16)
-    wz, wx, my, cwz, cwx, cmy = weights(term_exponent, fine_blocks, coarse_blocks)
+    czm = shift_z(par_up, 1)
+    czp = shift_z(par_dn, -1)
+    mid = inner_pass(own, zm, zp, wz)
     planes = jnp.stack([par, czm, czp])
     cxm = shift(planes, 16)
     cxp = shift(planes, -16)
 
-    out, send_up, send_dn = fine_passes(own, zm, zp, xm_own, xp_own, xm_far, xp_far, wz, wx, my)
+    send_up, send_dn, packed = outer_passes(mid, xm_own, xp_own, xm_far, xp_far, wz, wx, my)
     low = shift(send_up, 4)
     high = shift(send_dn, -4)
     out_c, send_up_c, send_dn_c = coarse_passes(par, czm, czp, cxm, cxp, cwz, cwx, cmy)
     low_c = shift(send_up_c, 4)
     high_c = shift(send_dn_c, -4)
+    out = own_rows(packed, my)
     total = finish(out, out_c, low, high, low_c, high_c, fz, ky, st2)
     groups = lax.axis_size("term")
     mine = lax.all_to_all(total.reshape(groups, 2, 32, 1024), "term", 0, 0)

time: 103 us -> 103 us (level)
  the two profiles are of different devices: /device:TPU:30 before, /device:TPU:1 now
where the time goes in v4:
time: 103 us
  starting transfers between devices  35.1 us (34%)
  Pallas kernels  34.9 us (34%)
  blocking collectives  16.8 us (16%)
  waiting for transfers between devices  12.2 us (12%)
  local copies, waits for them, and re-layouts  2.51 us (2%)
  other arithmetic  1.24 us (1%)
    ppermute x4, starting transfers between devices, shift_z(): return lax.ppermute(block, ('box', 'term'), route)  18 us
    ppermute x10, starting transfers between devices, shift(): lax.ppermute(block, 'box', [(i, (i + distance) % count) for i in range(co...  17 us
    all_to_all x1, blocking collectives, steps(): mine = lax.all_to_all(total.reshape(groups, 2, 32, 1024), 'term', 0, 0)  16.8 us
    ppermute x4, waiting for transfers between devices, shift_z(): return lax.ppermute(block, ('box', 'term'), route)  12.1 us
    pallas_call x1, Pallas kernels, outer_passes(): call(outer_kernel, (jax.ShapeDtypeStruct((4, 32, 1024), BF), jax.ShapeDty...  10.8 us
    pallas_call x1, Pallas kernels, coarse_passes(): call(coarse_kernel, (jax.ShapeDtypeStruct((32, 1024), F32), jax.ShapeDtyp...  6.49 us
    pallas_call x1, Pallas kernels, own_rows(): call(own_kernel, jax.ShapeDtypeStruct((8, 32, 1024), F32), [pltpu.VMEM((6...  5.79 us
    pallas_call x1, Pallas kernels, inner_pass(): call(inner_kernel, jax.ShapeDtypeStruct((8, 16, 64, 256), BF), [pltpu.VME...  3.66 us
  transfers between devices with their start and end apart: 14, of which 3 were waited for; matrix products, arithmetic and copies ran while one was open for 0% of the time, Pallas kernels for 32%

profile of v4, /device:TPU:1, one launch (start us, length us, event | category | flops | bytes accessed | tf_op | source)
XLA Modules:
  0.0 102.9 jit_solution(4788648811427203875)
XLA Ops:
  0.0 0.0 copy-start
  0.0 1.7 %constant_dynamic-slice_fusion = (bf16[1,8,32,1024]{3,2,1,0:T(8,128)(2,1)S(1)}, bf16[1,8,32,1024]{3,2,1,0:T(8,128)(2,1)S(1)}, bf16[8,32,1024]{2,1,0:T(8,128)(2,1)S(1)}) fusion(bf16[4,8,32,1024]{3,2,1,0:T(8,128)(2,1)} %boxes.1, s32[]{:T(128)S(6)} %select_n.32, s32[]{:T(128)S(6)} %select_n.30, s32[]{:T(128)S(6)} %select_n.27), kind=kLoop, calls=%fused_computation.8 | loop fusion | bytes 3145740 | tf_op jit(solution)/shard_map/jit(dynamic_index_in_dim)/dynamic_slice | solution.py:476
  1.7 0.0 copy-start.3
  1.7 0.7 slice_bitcast_fusion.1
  2.4 7.0 %collective-permute-start = (bf16[4,32,1024]{2,1,0:T(8,128)(2,1)}, bf16[4,32,1024]{2,1,0:T(8,128)(2,1)S(1)}, u32[]{:S(2)}, u32[]{:S(2)}) collective-permute-start(bf16[4,32,1024]{2,1,0:T(8,128)(2,1)} %slice_bitcast_fusion.1), channel_id=1, source_target_pairs={{0,4},{1,5},{2,6},{3,7},{4,11},{5,10},{6,9},{7,8},{8,12},{9,13},{1... | collective-permute-start | bytes 786440 | tf_op jit(solution)/shard_map/ppermute | solution.py:470
  9.4 0.1 collective-permute-start.1
  9.5 0.0 copy-done
  9.5 0.1 dynamic-slice_bitcast_fusion.1
  9.5 2.8 %collective-permute-start.3 = (bf16[4,32,1024]{2,1,0:T(8,128)(2,1)S(1)}, bf16[4,32,1024]{2,1,0:T(8,128)(2,1)S(1)}, u32[]{:S(2)}, u32[]{:S(2)}) collective-permute-start(bf16[4,32,1024]{2,1,0:T(8,128)(2,1)S(1)} %get-tuple-element.41), channel_id=1, source_target_pairs={{0,192},{4,196},{8,200},{12,204},{16,208},{20,212},{24,216},{28,22... | collective-permute-start | bytes 786440 | tf_op jit(solution)/shard_map/ppermute | solution.py:456
  12.4 0.0 collective-permute-start.2
  12.4 7.2 %collective-permute-done.zm = bf16[4,32,1024]{2,1,0:T(8,128)(2,1)S(1)} collective-permute-done((bf16[4,32,1024]{2,1,0:T(8,128)(2,1)}, bf16[4,32,1024]{2,1,0:T(8,128)(2,1)S(1)}, u32[]{:S(2)}, u32[]{:S(2)}) %collective-permute-start) | collective-permute-done | bytes 262176 | tf_op jit(solution)/shard_map/ppermute | solution.py:470
  19.6 1.9 %collective-permute-done.1.zp = bf16[4,32,1024]{2,1,0:T(8,128)(2,1)S(1)} collective-permute-done((bf16[4,32,1024]{2,1,0:T(8,128)(2,1)S(1)}, bf16[4,32,1024]{2,1,0:T(8,128)(2,1)S(1)}, u32[]{:S(2)}, u32[]{:S(2)}) %collective-permute-start.1) | collective-permute-done | bytes 262176 | tf_op jit(solution)/shard_map/ppermute | solution.py:470
  21.5 1.4 %collective-permute-start.4 = (bf16[4,32,1024]{2,1,0:T(8,128)(2,1)S(1)}, bf16[4,32,1024]{2,1,0:T(8,128)(2,1)S(1)}, u32[]{:S(2)}, u32[]{:S(2)}) collective-permute-start(bf16[4,32,1024]{2,1,0:T(8,128)(2,1)S(1)} %pad_maximum_fusion), channel_id=1, source_target_pairs={{0,64},{4,68},{8,72},{12,76},{16,80},{20,84},{24,88},{28,92},{32,9... | collective-permute-start | bytes 786440 | tf_op jit(solution)/shard_map/ppermute | solution.py:456
  22.9 1.5 %collective-permute-start.5 = (bf16[4,32,1024]{2,1,0:T(8,128)(2,1)S(1)}, bf16[4,32,1024]{2,1,0:T(8,128)(2,1)S(1)}, u32[]{:S(2)}, u32[]{:S(2)}) collective-permute-start(bf16[4,32,1024]{2,1,0:T(8,128)(2,1)S(1)} %pad_maximum_fusion.1), channel_id=1, source_target_pairs={{0,192},{4,196},{8,200},{12,204},{16,208},{20,212},{24,216},{28,22... | collective-permute-start | bytes 786440 | tf_op jit(solution)/shard_map/ppermute | solution.py:456
  24.5 0.1 pad_add_fusion.where
  24.6 0.0 copy-done.3
  24.6 3.4 %parents.1 = (bf16[32,1024]{1,0:T(8,128)(2,1)S(1)}, bf16[32,1024]{1,0:T(8,128)(2,1)S(1)}, bf16[32,1024]{1,0:T(8,128)(2,1)S(1)}, bf16[256,128]{1,0:T(8,128)(2,1)S...) custom-call(s32[3]{0:T(128)S(1)} %pad_add_fusion.where, bf16[4,8,32,1024]{3,2,1,0:T(8,128)(2,1)S(1)} %copy-done, ...), custom_call_target="tpu_custom_call" | custom-call | tf_op jit(solution)/shard_map/parents/pallas_call | solution.py:172
  28.0 2.5 %collective-permute-start.6 = (bf16[32,1024]{1,0:T(8,128)(2,1)S(1)}, bf16[32,1024]{1,0:T(8,128)(2,1)S(1)}, u32[]{:S(2)}, u32[]{:S(2)}) collective-permute-start(bf16[32,1024]{1,0:T(8,128)(2,1)S(1)} %get-tuple-element.28), channel_id=1, source_target_pairs={{0,4},{1,5},{2,6},{3,7},{4,11},{5,10},{6,9},{7,8},{8,12},{9,13},{1... | collective-permute-start | bytes 196616 | tf_op jit(solution)/shard_map/ppermute | solution.py:470
  30.4 3.0 %collective-permute-done.6.zm = bf16[32,1024]{1,0:T(8,128)(2,1)S(1)} collective-permute-done((bf16[32,1024]{1,0:T(8,128)(2,1)S(1)}, bf16[32,1024]{1,0:T(8,128)(2,1)S(1)}, u32[]{:S(2)}, u32[]{:S(2)}) %collective-permute-start.6) | collective-permute-done | bytes 65568 | tf_op jit(solution)/shard_map/ppermute | solution.py:470
  33.5 8.5 %collective-permute-start.7 = (bf16[32,1024]{1,0:T(8,128)(2,1)S(1)}, bf16[32,1024]{1,0:T(8,128)(2,1)S(1)}, u32[]{:S(2)}, u32[]{:S(2)}) collective-permute-start(bf16[32,1024]{1,0:T(8,128)(2,1)S(1)} %get-tuple-element.29), channel_id=1, source_target_pairs={{0,255},{1,254},{2,253},{3,252},{4,0},{5,1},{6,2},{7,3},{8,7},{9,6... | collective-permute-start | bytes 196616 | tf_op jit(solution)/shard_map/ppermute | solution.py:470
  42.0 0.0 copy-done.1
  42.0 0.0 copy-done.2
  42.0 0.0 copy-done.4
  42.0 3.0 %weights.1 = (bf16[8,512,256]{2,1,0:T(8,128)(2,1)S(1)}, bf16[8,64,128]{2,1,0:T(8,128)(2,1)S(1)}, bf16[2,128,256]{2,1,0:T(8,128)(2,1)S(1)}, bf16[8,384,128]{2,1,0...) custom-call(s32[8]{0:T(128)S(1)} %copy-done.4, bf16[16,3,32,32]{3,2,1,0:T(8,128)(2,1)S(1)} %copy-done.1, ...), custom_call_target="tpu_custom_call" | custom-call | tf_op jit(solution)/shard_map/weights/pallas_call | solution.py:92
  45.0 0.0 collective-permute-done.7.zp
  45.1 0.1 collective-permute-start.9
  45.1 3.7 %shard_map.55.inner = bf16[8,16,64,256]{3,2,1,0:T(8,128)(2,1)S(1)} custom-call(bf16[8,32,1024]{2,1,0:T(8,128)(2,1)S(1)} %get-tuple-element.45.own, bf16[4,32,1024]{2,1,0:T(8,128)(2,1)S(1)} %collective-permute-done.zm, bf16[4,32,1024]{2,1,0:T(8,128)(2,1)S(1)} %collective-permute-done.1.zp, bf16[8,512,256]{2,1,0:T(8,128)(2,1)S(1)} %get-tuple-element.23.wz), custom_call_target="tpu_custom_call" | custom-call | tf_op jit(solution)/shard_map/pallas_call | solution.py:225
  48.8 0.0 collective-permute-done.3.xp_own
  48.8 1.5 %collective-permute-start.8 = (bf16[3,32,1024]{2,1,0:T(8,128)(2,1)S(1)}, bf16[3,32,1024]{2,1,0:T(8,128)(2,1)S(1)}, u32[]{:S(2)}, u32[]{:S(2)}) collective-permute-start(bf16[3,32,1024]{2,1,0:T(8,128)(2,1)S(1)} %pad_maximum_fusion.2), channel_id=1, source_target_pairs={{0,64},{4,68},{8,72},{12,76},{16,80},{20,84},{24,88},{28,92},{32,9... | collective-permute-start | bytes 589832 | tf_op jit(solution)/shard_map/ppermute | solution.py:456
  50.4 0.0 collective-permute-done.2.xm_own
  50.4 0.0 collective-permute-done.4.xm_far
  50.4 0.0 collective-permute-done.5.xp_far
  50.4 10.8 %shard_map.56 = (bf16[4,32,1024]{2,1,0:T(8,128)(2,1)S(1)}, bf16[4,32,1024]{2,1,0:T(8,128)(2,1)S(1)}, bf16[16,256,512]{2,1,0:T(8,128)(2,1)S(1)}) custom-call(bf16[8,16,64,256]{3,2,1,0:T(8,128)(2,1)S(1)} %shard_map.55.inner, bf16[4,32,1024]{2,1,0:T(8,128)(2,1)S(1)} %collective-permute-done.2.xm_own, bf16[4,32,1024]{2,1,0:T(8,128)(2,1)S(1)} %collective-permute-done.3.xp_own, ...), custom_call_target="tpu_custom_call" | custom-call | tf_op jit(solution)/shard_map/pallas_call | solution.py:296
  61.2 0.1 collective-permute-start.10
  61.3 4.8 %collective-permute-start.11 = (bf16[4,32,1024]{2,1,0:T(8,128)(2,1)S(1)}, bf16[4,32,1024]{2,1,0:T(8,128)(2,1)S(1)}, u32[]{:S(2)}, u32[]{:S(2)}) collective-permute-start(bf16[4,32,1024]{2,1,0:T(8,128)(2,1)S(1)} %get-tuple-element.35), channel_id=1, source_target_pairs={{0,240},{4,244},{8,248},{12,252},{16,0},{20,4},{24,8},{28,12},{32,... | collective-permute-start | bytes 786440 | tf_op jit(solution)/shard_map/ppermute | solution.py:456
  66.0 0.0 collective-permute-done.9.xp
  66.0 0.0 collective-permute-done.8.xm
  66.0 6.5 %shard_map.58 = (f32[32,1024]{1,0:T(8,128)S(1)}, bf16[32,1024]{1,0:T(8,128)(2,1)S(1)}, bf16[32,1024]{1,0:T(8,128)(2,1)S(1)}) custom-call(bf16[32,1024]{1,0:T(8,128)(2,1)S(1)} %get-tuple-element.27.par, bf16[32,1024]{1,0:T(8,128)(2,1)S(1)} %collective-permute-done.6.zm, bf16[32,1024]{1,0:T(8,128)(2,1)S(1)} %collective-permute-done.7.zp, ...), custom_call_target="tpu_custom_call" | custom-call | tf_op jit(solution)/shard_map/pallas_call | solution.py:403
  72.5 0.1 collective-permute-start.12
  72.6 4.8 %collective-permute-start.13 = (bf16[32,1024]{1,0:T(8,128)(2,1)S(1)}, bf16[32,1024]{1,0:T(8,128)(2,1)S(1)}, u32[]{:S(2)}, u32[]{:S(2)}) collective-permute-start(bf16[32,1024]{1,0:T(8,128)(2,1)S(1)} %get-tuple-element.37), channel_id=1, source_target_pairs={{0,240},{4,244},{8,248},{12,252},{16,0},{20,4},{24,8},{28,12},{32,... | collective-permute-start | bytes 196616 | tf_op jit(solution)/shard_map/ppermute | solution.py:456
  77.4 5.8 %shard_map.57.own = f32[8,32,1024]{2,1,0:T(8,128)S(1)} custom-call(bf16[16,256,512]{2,1,0:T(8,128)(2,1)S(1)} %get-tuple-element.26.packed, bf16[2,128,256]{2,1,0:T(8,128)(2,1)S(1)} %get-tuple-element.25.my), custom_call_target="tpu_custom_call" | custom-call | tf_op jit(solution)/shard_map/pallas_call | solution.py:334
  83.2 0.0 collective-permute-done.12.low_c
  83.2 0.0 collective-permute-done.13.high_c
  83.2 0.0 collective-permute-done.10.low
  83.2 0.0 collective-permute-done.11.high
  83.2 1.8 %shard_map.59 = bf16[8,32,1024]{2,1,0:T(8,128)(2,1)S(1)} custom-call(f32[8,32,1024]{2,1,0:T(8,128)S(1)} %shard_map.57.own, f32[32,1024]{1,0:T(8,128)S(1)} %get-tuple-element.33.own_c, bf16[4,32,1024]{2,1,0:T(8,128)(2,1)S(1)} %collective-permute-done.10.low, bf16[4,32,1024]{2,1,0:T(8,128)(2,1)S(1)} %collective-permute-done.11.high, ...), custom_call_target="tpu_custom_call" | custom-call | tf_op jit(solution)/shard_map/pallas_call | solution.py:447
  85.1 16.8 %all_to_all.5 = bf16[4,2,32,1024]{3,2,1,0:T(8,128)(2,1)S(1)} all-to-all(bf16[4,2,32,1024]{3,2,1,0:T(8,128)(2,1)S(1)} %bitcast.23), channel_id=1, replica_groups=mesh['box'=64,'term'=4] {'term'}, dimensions={0} | all-to-all | bytes 1048576 | tf_op jit(solution)/shard_map/all_to_all | solution.py:512
  101.9 1.1 %convert_element_type.3 = f32[4,2,32,1024]{3,2,1,0:T(8,128)} convert(bf16[4,2,32,1024]{3,2,1,0:T(8,128)(2,1)S(1)} %all_to_all.5) | non-fusion elementwise | flops 262144 | bytes 1572864 | tf_op jit(solution)/shard_map/convert_element_type | solution.py:513
  (9 shorter events, 0.1 us)
Async XLA Ops:
  0.0 9.5 %copy-start = (bf16[4,8,32,1024]{3,2,1,0:T(8,128)(2,1)S(1)}, bf16[4,8,32,1024]{3,2,1,0:T(8,128)(2,1)}, u32[]{:S(2)}) copy-start(bf16[4,8,32,1024]{3,2,1,0:T(8,128)(2,1)} %boxes.1) | copy-start | bytes 6291460
  1.7 22.9 %copy-start.3 = (bf16[32,64]{1,0:T(8,128)(2,1)S(1)}, bf16[32,64]{1,0:T(8,128)(2,1)}, u32[]{:S(2)}) copy-start(bf16[32,64]{1,0:T(8,128)(2,1)} %s.1) | copy-start | bytes 12292
  2.4 17.1 %collective-permute-start = (bf16[4,32,1024]{2,1,0:T(8,128)(2,1)}, bf16[4,32,1024]{2,1,0:T(8,128)(2,1)S(1)}, u32[]{:S(2)}, u32[]{:S(2)}) collective-permute-start(bf16[4,32,1024]{2,1,0:T(8,128)(2,1)} %slice_bitcast_fusion.1), channel_id=1, source_target_pairs={{0,4},{1,5},{2,6},{3,7},{4,11},{5,10},{6,9},{7,8},{8,12},{9,13},{1... | collective-permute-start | bytes 786440 | tf_op jit(solution)/shard_map/ppermute | solution.py:470
  9.4 12.1 %collective-permute-start.1 = (bf16[4,32,1024]{2,1,0:T(8,128)(2,1)S(1)}, bf16[4,32,1024]{2,1,0:T(8,128)(2,1)S(1)}, u32[]{:S(2)}, u32[]{:S(2)}) collective-permute-start(bf16[4,32,1024]{2,1,0:T(8,128)(2,1)S(1)} %slice_bitcast_fusion), channel_id=1, source_target_pairs={{0,255},{1,254},{2,253},{3,252},{4,0},{5,1},{6,2},{7,3},{8,7},{9,6... | collective-permute-start | bytes 786440 | tf_op jit(solution)/shard_map/ppermute | solution.py:470
  9.5 39.3 %collective-permute-start.3 = (bf16[4,32,1024]{2,1,0:T(8,128)(2,1)S(1)}, bf16[4,32,1024]{2,1,0:T(8,128)(2,1)S(1)}, u32[]{:S(2)}, u32[]{:S(2)}) collective-permute-start(bf16[4,32,1024]{2,1,0:T(8,128)(2,1)S(1)} %get-tuple-element.41), channel_id=1, source_target_pairs={{0,192},{4,196},{8,200},{12,204},{16,208},{20,212},{24,216},{28,22... | collective-permute-start | bytes 786440 | tf_op jit(solution)/shard_map/ppermute | solution.py:456
  12.4 29.7 %copy-start.1 = (bf16[16,3,32,32]{3,2,1,0:T(8,128)(2,1)S(1)}, bf16[16,3,32,32]{3,2,1,0:T(8,128)(2,1)}, u32[]{:S(2)}) copy-start(bf16[16,3,32,32]{3,2,1,0:T(8,128)(2,1)} %fine.1) | copy-start | bytes 294916
  12.4 29.7 %copy-start.2 = (bf16[16,3,32,32]{3,2,1,0:T(8,128)(2,1)S(1)}, bf16[16,3,32,32]{3,2,1,0:T(8,128)(2,1)}, u32[]{:S(2)}) copy-start(bf16[16,3,32,32]{3,2,1,0:T(8,128)(2,1)} %coarse.1) | copy-start | bytes 294916
  12.4 29.7 %copy-start.4 = (s32[8]{0:T(128)S(1)}, s32[8]{0:T(128)}, u32[]{:S(2)}) copy-start(s32[8]{0:T(128)} %exponents.1) | copy-start | bytes 100
  12.4 38.0 %collective-permute-start.2 = (bf16[4,32,1024]{2,1,0:T(8,128)(2,1)S(1)}, bf16[4,32,1024]{2,1,0:T(8,128)(2,1)S(1)}, u32[]{:S(2)}, u32[]{:S(2)}) collective-permute-start(bf16[4,32,1024]{2,1,0:T(8,128)(2,1)S(1)} %get-tuple-element.42), channel_id=1, source_target_pairs={{0,64},{4,68},{8,72},{12,76},{16,80},{20,84},{24,88},{28,92},{32,9... | collective-permute-start | bytes 786440 | tf_op jit(solution)/shard_map/ppermute | solution.py:456
  21.5 28.8 %collective-permute-start.4 = (bf16[4,32,1024]{2,1,0:T(8,128)(2,1)S(1)}, bf16[4,32,1024]{2,1,0:T(8,128)(2,1)S(1)}, u32[]{:S(2)}, u32[]{:S(2)}) collective-permute-start(bf16[4,32,1024]{2,1,0:T(8,128)(2,1)S(1)} %pad_maximum_fusion), channel_id=1, source_target_pairs={{0,64},{4,68},{8,72},{12,76},{16,80},{20,84},{24,88},{28,92},{32,9... | collective-permute-start | bytes 786440 | tf_op jit(solution)/shard_map/ppermute | solution.py:456
  22.9 27.4 %collective-permute-start.5 = (bf16[4,32,1024]{2,1,0:T(8,128)(2,1)S(1)}, bf16[4,32,1024]{2,1,0:T(8,128)(2,1)S(1)}, u32[]{:S(2)}, u32[]{:S(2)}) collective-permute-start(bf16[4,32,1024]{2,1,0:T(8,128)(2,1)S(1)} %pad_maximum_fusion.1), channel_id=1, source_target_pairs={{0,192},{4,196},{8,200},{12,204},{16,208},{20,212},{24,216},{28,22... | collective-permute-start | bytes 786440 | tf_op jit(solution)/shard_map/ppermute | solution.py:456
  28.0 5.5 %collective-permute-start.6 = (bf16[32,1024]{1,0:T(8,128)(2,1)S(1)}, bf16[32,1024]{1,0:T(8,128)(2,1)S(1)}, u32[]{:S(2)}, u32[]{:S(2)}) collective-permute-start(bf16[32,1024]{1,0:T(8,128)(2,1)S(1)} %get-tuple-element.28), channel_id=1, source_target_pairs={{0,4},{1,5},{2,6},{3,7},{4,11},{5,10},{6,9},{7,8},{8,12},{9,13},{1... | collective-permute-start | bytes 196616 | tf_op jit(solution)/shard_map/ppermute | solution.py:470
  33.5 11.5 %collective-permute-start.7 = (bf16[32,1024]{1,0:T(8,128)(2,1)S(1)}, bf16[32,1024]{1,0:T(8,128)(2,1)S(1)}, u32[]{:S(2)}, u32[]{:S(2)}) collective-permute-start(bf16[32,1024]{1,0:T(8,128)(2,1)S(1)} %get-tuple-element.29), channel_id=1, source_target_pairs={{0,255},{1,254},{2,253},{3,252},{4,0},{5,1},{6,2},{7,3},{8,7},{9,6... | collective-permute-start | bytes 196616 | tf_op jit(solution)/shard_map/ppermute | solution.py:470
  45.1 21.0 %collective-permute-start.9 = (bf16[3,32,1024]{2,1,0:T(8,128)(2,1)S(1)}, bf16[3,32,1024]{2,1,0:T(8,128)(2,1)S(1)}, u32[]{:S(2)}, u32[]{:S(2)}) collective-permute-start(bf16[3,32,1024]{2,1,0:T(8,128)(2,1)S(1)} %pad_maximum_fusion.2), channel_id=1, source_target_pairs={{0,192},{4,196},{8,200},{12,204},{16,208},{20,212},{24,216},{28,22... | collective-permute-start | bytes 589832 | tf_op jit(solution)/shard_map/ppermute | solution.py:456
  48.8 17.2 %collective-permute-start.8 = (bf16[3,32,1024]{2,1,0:T(8,128)(2,1)S(1)}, bf16[3,32,1024]{2,1,0:T(8,128)(2,1)S(1)}, u32[]{:S(2)}, u32[]{:S(2)}) collective-permute-start(bf16[3,32,1024]{2,1,0:T(8,128)(2,1)S(1)} %pad_maximum_fusion.2), channel_id=1, source_target_pairs={{0,64},{4,68},{8,72},{12,76},{16,80},{20,84},{24,88},{28,92},{32,9... | collective-permute-start | bytes 589832 | tf_op jit(solution)/shard_map/ppermute | solution.py:456
  61.2 22.1 %collective-permute-start.10 = (bf16[4,32,1024]{2,1,0:T(8,128)(2,1)S(1)}, bf16[4,32,1024]{2,1,0:T(8,128)(2,1)S(1)}, u32[]{:S(2)}, u32[]{:S(2)}) collective-permute-start(bf16[4,32,1024]{2,1,0:T(8,128)(2,1)S(1)} %get-tuple-element.34), channel_id=1, source_target_pairs={{0,16},{4,20},{8,24},{12,28},{16,32},{20,36},{24,40},{28,44},{32,4... | collective-permute-start | bytes 786440 | tf_op jit(solution)/shard_map/ppermute | solution.py:456
  61.3 22.0 %collective-permute-start.11 = (bf16[4,32,1024]{2,1,0:T(8,128)(2,1)S(1)}, bf16[4,32,1024]{2,1,0:T(8,128)(2,1)S(1)}, u32[]{:S(2)}, u32[]{:S(2)}) collective-permute-start(bf16[4,32,1024]{2,1,0:T(8,128)(2,1)S(1)} %get-tuple-element.35), channel_id=1, source_target_pairs={{0,240},{4,244},{8,248},{12,252},{16,0},{20,4},{24,8},{28,12},{32,... | collective-permute-start | bytes 786440 | tf_op jit(solution)/shard_map/ppermute | solution.py:456
  72.5 10.7 %collective-permute-start.12 = (bf16[32,1024]{1,0:T(8,128)(2,1)S(1)}, bf16[32,1024]{1,0:T(8,128)(2,1)S(1)}, u32[]{:S(2)}, u32[]{:S(2)}) collective-permute-start(bf16[32,1024]{1,0:T(8,128)(2,1)S(1)} %get-tuple-element.36), channel_id=1, source_target_pairs={{0,16},{4,20},{8,24},{12,28},{16,32},{20,36},{24,40},{28,44},{32,4... | collective-permute-start | bytes 196616 | tf_op jit(solution)/shard_map/ppermute | solution.py:456
  72.6 10.6 %collective-permute-start.13 = (bf16[32,1024]{1,0:T(8,128)(2,1)S(1)}, bf16[32,1024]{1,0:T(8,128)(2,1)S(1)}, u32[]{:S(2)}, u32[]{:S(2)}) collective-permute-start(bf16[32,1024]{1,0:T(8,128)(2,1)S(1)} %get-tuple-element.37), channel_id=1, source_target_pairs={{0,240},{4,244},{8,248},{12,252},{16,0},{20,4},{24,8},{28,12},{32,... | collective-permute-start | bytes 196616 | tf_op jit(solution)/shard_map/ppermute | solution.py:456

commit v5 on v4

--- a/solution.py
+++ b/solution.py
@@ -9,7 +9,10 @@
 BF = jnp.bfloat16
 F32 = jnp.float32
 INTERPRET = False
-PARAMS = dict(compiler_params=pltpu.CompilerParams(vmem_limit_bytes=40 * 1024 * 1024))
+
+
+def grant(mebibytes):
+    return dict(compiler_params=pltpu.CompilerParams(vmem_limit_bytes=mebibytes * 1024 * 1024))
 
 
 def dot(a, b):
@@ -25,8 +28,8 @@
     return hi, (value - hi.astype(F32)).astype(BF)
 
 
-def call(kernel, outs, scratch=()):
-    return pl.pallas_call(kernel, out_shape=outs, scratch_shapes=list(scratch), interpret=INTERPRET, **PARAMS)
+def call(kernel, outs, scratch=(), size=24):
+    return pl.pallas_call(kernel, out_shape=outs, scratch_shapes=list(scratch), interpret=INTERPRET, **grant(size))
 
 
 def same(rows, columns, test):
@@ -110,11 +113,11 @@
         ],
         interpret=INTERPRET,
         name="weights",
-        **PARAMS,
+        **grant(16),
     )(exponents, fine, coarse)
 
 
-def parent_kernel(where, boxes, s, out, up, dn, fz, ky, st2, rows, wide):
+def prepare_kernel(where, boxes, s, out, low_x, high_x, up, dn, fz, ky, st2, rows, wide):
     step = pl.program_id(0)
     scale = s[...]
 
@@ -155,42 +158,40 @@
     @pl.when(step == 0)
     def _():
         out[...] = parent
+        low_x[...] = boxes[0, :4]
+        high_x[...] = boxes[0, 4:]
 
     @pl.when(step == where[2])
     def _():
-        up[...] = parent
+        for i in range(4):
+            up[i] = boxes[0, 2 * i + 1]
+        up[4] = parent
 
     @pl.when(step != where[2])
     def _():
-        dn[...] = parent
-
-
-def parents_of(where, fine_coeffs, s):
+        for i in range(4):
+            dn[i] = boxes[0, 2 * i]
+        dn[4] = parent
+
+
+def prepare(where, fine_coeffs, s):
     def whole(*shape):
         return pl.BlockSpec(shape, lambda i, w: (0,) * len(shape))
 
+    shapes = [(32, 1024), (4, 32, 1024), (4, 32, 1024), (5, 32, 1024), (5, 32, 1024), (256, 128), (2048, 1024), (64, 64)]
     return pl.pallas_call(
-        parent_kernel,
-        out_shape=(
-            jax.ShapeDtypeStruct((32, 1024), BF),
-            jax.ShapeDtypeStruct((32, 1024), BF),
-            jax.ShapeDtypeStruct((32, 1024), BF),
-            jax.ShapeDtypeStruct((256, 128), BF),
-            jax.ShapeDtypeStruct((2048, 1024), BF),
-            jax.ShapeDtypeStruct((64, 64), BF),
-        ),
+        prepare_kernel,
+        out_shape=tuple(jax.ShapeDtypeStruct(shape, BF) for shape in shapes),
         grid_spec=pltpu.PrefetchScalarGridSpec(
             num_scalar_prefetch=1,
             grid=(2,),
             in_specs=[pl.BlockSpec((1, 8, 32, 1024), lambda i, w: (w[i], 0, 0, 0)), whole(32, 64)],
-            out_specs=[
-                whole(32, 1024), whole(32, 1024), whole(32, 1024), whole(256, 128), whole(2048, 1024), whole(64, 64),
-            ],
+            out_specs=[whole(*shape) for shape in shapes],
             scratch_shapes=[pltpu.VMEM((1024, 256), BF), pltpu.VMEM((64, 2048), BF)],
         ),
         interpret=INTERPRET,
-        name="parents",
-        **PARAMS,
+        name="prepare",
+        **grant(24),
     )(where, fine_coeffs, s)
 
 
@@ -205,11 +206,11 @@
             left[row + g * 64 : row + g * 64 + 32, zb * 128 : zb * 128 + 128] = sources[zb][:, g * 128 : g * 128 + 128]
 
 
-def inner_kernel(own, zm, zp, wz, mid, left):
+def inner_kernel(low_x, high_x, zm, zp, wz, mid, left):
     for cy in range(2):
         for cx in range(2):
-            at = 4 * cx + 2 * cy
-            fill_left(left, [zm[2 * cx + cy], own[at], own[at + 1], zp[2 * cx + cy]], cy * 512 + cx * 32)
+            own = high_x if cx else low_x
+            fill_left(left, [zm[2 * cx + cy], own[2 * cy], own[2 * cy + 1], zp[2 * cx + cy]], cy * 512 + cx * 32)
 
     def term(t, carry):
         weight = wz[t]
@@ -337,7 +338,7 @@
 def coarse_kernel(par, zm, zp, xm, xp, wz, wx, my, out, send_up, send_dn, left, mid, wide, done):
     sources = [
         [xm[1], xm[0], xm[2]],
-        [zm[...], par[...], zp[...]],
+        [zm[4], par[...], zp[4]],
         [xp[1], xp[0], xp[2]],
     ]
     for xb in range(3):
@@ -470,40 +471,28 @@
     return lax.ppermute(block, ("box", "term"), route)
 
 
-def z_layer(fine_coeffs, step, p, t):
-    other = lax.axis_size("term") - 1 - t
-    cross = (p % 2 == 1) if step == 1 else (p % 2 == 0)
-    chosen = lax.dynamic_index_in_dim(fine_coeffs, jnp.where(cross, other, t), 0, False)
-    layer = chosen.reshape(4, 2, 32, 1024)[:, 1 if step == 1 else 0]
-    return shift_z(layer, step)
-
-
 def steps(fine_coeffs, fine_blocks, coarse_blocks, two_scale, term_exponent):
     p = lax.axis_index("box")
     t = lax.axis_index("term")
-    zm = z_layer(fine_coeffs, 1, p, t)
-    zp = z_layer(fine_coeffs, -1, p, t)
-    own = lax.dynamic_index_in_dim(fine_coeffs, t, 0, False)
-    xm_own = shift(own[4:], 16)
-    xp_own = shift(own[:4], -16)
-
     other = lax.axis_size("term") - 1 - t
     where = jnp.stack([t, other, p % 2]).astype(jnp.int32)
-    par, par_up, par_dn, fz, ky, st2 = parents_of(where, fine_coeffs, two_scale)
+    par, low_x, high_x, up, dn, fz, ky, st2 = prepare(where, pltpu.with_memory_space_constraint(fine_coeffs, pltpu.HBM), two_scale)
+    zm = shift_z(up, 1)
+    zp = shift_z(dn, -1)
+    xm_own = shift(high_x, 16)
+    xp_own = shift(low_x, -16)
     wz, wx, my, cwz, cwx, cmy = weights(term_exponent, fine_blocks, coarse_blocks)
-    xm_far = shift(jnp.concatenate([zm[2:], zp[2:]], axis=0), 16)
+    xm_far = shift(jnp.concatenate([zm[2:4], zp[2:4]], axis=0), 16)
     xp_far = shift(jnp.concatenate([zm[:2], zp[:2]], axis=0), -16)
-    czm = shift_z(par_up, 1)
-    czp = shift_z(par_dn, -1)
-    mid = inner_pass(own, zm, zp, wz)
-    planes = jnp.stack([par, czm, czp])
+    mid = inner_pass(low_x, high_x, zm, zp, wz)
+    planes = jnp.stack([par, zm[4], zp[4]])
     cxm = shift(planes, 16)
     cxp = shift(planes, -16)
 
     send_up, send_dn, packed = outer_passes(mid, xm_own, xp_own, xm_far, xp_far, wz, wx, my)
     low = shift(send_up, 4)
     high = shift(send_dn, -4)
-    out_c, send_up_c, send_dn_c = coarse_passes(par, czm, czp, cxm, cxp, cwz, cwx, cmy)
+    out_c, send_up_c, send_dn_c = coarse_passes(par, zm, zp, cxm, cxp, cwz, cwx, cmy)
     low_c = shift(send_up_c, 4)
     high_c = shift(send_dn_c, -4)
     out = own_rows(packed, my)

time: 103 us -> 91.3 us (0.89)
  the two profiles are of different devices: /device:TPU:1 before, /device:TPU:32 now
where the time goes in v5:
time: 91.3 us; the launch traced here: 91.2 us
  Pallas kernels  36 us (39%)
  starting transfers between devices  28.7 us (31%)
  blocking collectives  21.3 us (23%)
  waiting for transfers between devices  2.87 us (3%)
  other arithmetic  1.24 us (1%)
    all_to_all x1, blocking collectives, steps(): mine = lax.all_to_all(total.reshape(groups, 2, 32, 1024), 'term', 0, 0)  21.3 us
    ppermute x10, starting transfers between devices, shift(): lax.ppermute(block, 'box', [(i, (i + distance) % count) for i in range(co...  18.6 us
    pallas_call x1, Pallas kernels, outer_passes(): call(outer_kernel, (jax.ShapeDtypeStruct((4, 32, 1024), BF), jax.ShapeDty...  10.8 us
    ppermute x2, starting transfers between devices, shift_z(): return lax.ppermute(block, ('box', 'term'), route)  10.1 us
    pallas_call x1, Pallas kernels, coarse_passes(): call(coarse_kernel, (jax.ShapeDtypeStruct((32, 1024), F32), jax.ShapeDtyp...  6.48 us
    pallas_call x1, Pallas kernels, own_rows(): call(own_kernel, jax.ShapeDtypeStruct((8, 32, 1024), F32), [pltpu.VMEM((6...  5.79 us
    pallas_call x1, Pallas kernels, prepare(): pl.pallas_call(prepare_kernel, out_shape=tuple((jax.ShapeDtypeStruct(shap...  4.5 us
    pallas_call x1, Pallas kernels, inner_pass(): call(inner_kernel, jax.ShapeDtypeStruct((8, 16, 64, 256), BF), [pltpu.VME...  3.66 us
  transfers between devices with their start and end apart: 12, of which 1 were waited for; matrix products, arithmetic and copies ran while one was open for 0% of the time, Pallas kernels for 33%

profile of v5, /device:TPU:32, one launch (start us, length us, event | category | flops | bytes accessed | tf_op | source)
XLA Modules:
  0.0 91.2 jit_solution(1973389311783822084)
XLA Ops:
  0.0 0.0 copy-start.1
  0.0 0.0 copy-start
  0.0 0.1 pad_add_fusion.where
  0.1 0.0 copy-start.2
  0.1 0.8 copy-done.2
  0.8 0.0 copy-start.3
  0.8 4.5 %prepare.1 = (bf16[32,1024]{1,0:T(8,128)(2,1)S(1)}, bf16[4,32,1024]{2,1,0:T(8,128)(2,1)S(1)}, bf16[4,32,1024]{2,1,0:T(8,128)(2,1)S(1)}, bf16[5,32,1024]{2,1,0:T(...) custom-call(s32[3]{0:T(128)S(1)} %pad_add_fusion.where, ...), custom_call_target="tpu_custom_call" | custom-call | tf_op jit(solution)/shard_map/prepare/pallas_call | solution.py:182
  5.3 0.1 collective-permute-start
  5.4 10.0 %collective-permute-start.1 = (bf16[5,32,1024]{2,1,0:T(8,128)(2,1)S(1)}, bf16[5,32,1024]{2,1,0:T(8,128)(2,1)S(1)}, u32[]{:S(2)}, u32[]{:S(2)}) collective-permute-start(bf16[5,32,1024]{2,1,0:T(8,128)(2,1)S(1)} %get-tuple-element.28), channel_id=1, source_target_pairs={{0,255},{1,254},{2,253},{3,252},{4,0},{5,1},{6,2},{7,3},{8,7},{9,6... | collective-permute-start | bytes 983048 | tf_op jit(solution)/shard_map/ppermute | solution.py:471
  15.4 0.7 collective-permute-start.3
  16.2 1.3 %collective-permute-start.2 = (bf16[4,32,1024]{2,1,0:T(8,128)(2,1)S(1)}, bf16[4,32,1024]{2,1,0:T(8,128)(2,1)S(1)}, u32[]{:S(2)}, u32[]{:S(2)}) collective-permute-start(bf16[4,32,1024]{2,1,0:T(8,128)(2,1)S(1)} %get-tuple-element.26.high_x), channel_id=1, source_target_pairs={{0,64},{4,68},{8,72},{12,76},{16,80},{20,84},{24,88},{28,92},{32,9... | collective-permute-start | bytes 786440 | tf_op jit(solution)/shard_map/ppermute | solution.py:457
  17.5 2.8 %collective-permute-done.zm = bf16[5,32,1024]{2,1,0:T(8,128)(2,1)S(1)} collective-permute-done((bf16[5,32,1024]{2,1,0:T(8,128)(2,1)S(1)}, bf16[5,32,1024]{2,1,0:T(8,128)(2,1)S(1)}, u32[]{:S(2)}, u32[]{:S(2)}) %collective-permute-start) | collective-permute-done | bytes 327712 | tf_op jit(solution)/shard_map/ppermute | solution.py:471
  20.3 0.0 collective-permute-done.1.zp
  20.4 0.1 collective-permute-start.4
  20.6 3.3 %collective-permute-start.5 = (bf16[4,32,1024]{2,1,0:T(8,128)(2,1)S(1)}, bf16[4,32,1024]{2,1,0:T(8,128)(2,1)S(1)}, u32[]{:S(2)}, u32[]{:S(2)}) collective-permute-start(bf16[4,32,1024]{2,1,0:T(8,128)(2,1)S(1)} %pad_maximum_fusion.1), channel_id=1, source_target_pairs={{0,192},{4,196},{8,200},{12,204},{16,208},{20,212},{24,216},{28,22... | collective-permute-start | bytes 786440 | tf_op jit(solution)/shard_map/ppermute | solution.py:457
  23.8 0.0 copy-done.1
  23.8 0.0 copy-done
  23.8 0.0 copy-done.3
  23.8 3.0 %weights.1 = (bf16[8,512,256]{2,1,0:T(8,128)(2,1)S(1)}, bf16[8,64,128]{2,1,0:T(8,128)(2,1)S(1)}, bf16[2,128,256]{2,1,0:T(8,128)(2,1)S(1)}, bf16[8,384,128]{2,1,0...) custom-call(s32[8]{0:T(128)S(1)} %copy-done.3, bf16[16,3,32,32]{3,2,1,0:T(8,128)(2,1)S(1)} %copy-done, ...), custom_call_target="tpu_custom_call" | custom-call | tf_op jit(solution)/shard_map/weights/pallas_call | solution.py:95
  26.9 0.4 collective-permute-start.7
  27.2 3.7 %shard_map.55.inner = bf16[8,16,64,256]{3,2,1,0:T(8,128)(2,1)S(1)} custom-call(bf16[4,32,1024]{2,1,0:T(8,128)(2,1)S(1)} %get-tuple-element.25.low_x, bf16[4,32,1024]{2,1,0:T(8,128)(2,1)S(1)} %get-tuple-element.26.high_x, bf16[5,32,1024]{2,1,0:T(8,128)(2,1)S(1)} %collective-permute-done.zm, bf16[5,32,1024]{2,1,0:T(8,128)(2,1)S(1)} %collective-permute-done.1.zp, ...), custom_call_target="tpu_custom_call" | custom-call | tf_op jit(solution)/shard_map/pallas_call | solution.py:226
  30.9 0.0 collective-permute-done.3.xp_own
  30.9 1.8 %collective-permute-start.6 = (bf16[3,32,1024]{2,1,0:T(8,128)(2,1)S(1)}, bf16[3,32,1024]{2,1,0:T(8,128)(2,1)S(1)}, u32[]{:S(2)}, u32[]{:S(2)}) collective-permute-start(bf16[3,32,1024]{2,1,0:T(8,128)(2,1)S(1)} %pad_maximum_fusion.2), channel_id=1, source_target_pairs={{0,64},{4,68},{8,72},{12,76},{16,80},{20,84},{24,88},{28,92},{32,9... | collective-permute-start | bytes 589832 | tf_op jit(solution)/shard_map/ppermute | solution.py:457
  32.7 0.0 collective-permute-done.2.xm_own
  32.8 0.0 collective-permute-done.4.xm_far
  32.8 0.0 collective-permute-done.5.xp_far
  32.8 10.8 %shard_map.56 = (bf16[4,32,1024]{2,1,0:T(8,128)(2,1)S(1)}, bf16[4,32,1024]{2,1,0:T(8,128)(2,1)S(1)}, bf16[16,256,512]{2,1,0:T(8,128)(2,1)S(1)}) custom-call(bf16[8,16,64,256]{3,2,1,0:T(8,128)(2,1)S(1)} %shard_map.55.inner, bf16[4,32,1024]{2,1,0:T(8,128)(2,1)S(1)} %collective-permute-done.2.xm_own, bf16[4,32,1024]{2,1,0:T(8,128)(2,1)S(1)} %collective-permute-done.3.xp_own, ...), custom_call_target="tpu_custom_call" | custom-call | tf_op jit(solution)/shard_map/pallas_call | solution.py:297
  43.5 0.1 collective-permute-start.8
  43.6 5.3 %collective-permute-start.9 = (bf16[4,32,1024]{2,1,0:T(8,128)(2,1)S(1)}, bf16[4,32,1024]{2,1,0:T(8,128)(2,1)S(1)}, u32[]{:S(2)}, u32[]{:S(2)}) collective-permute-start(bf16[4,32,1024]{2,1,0:T(8,128)(2,1)S(1)} %get-tuple-element.39), channel_id=1, source_target_pairs={{0,240},{4,244},{8,248},{12,252},{16,0},{20,4},{24,8},{28,12},{32,... | collective-permute-start | bytes 786440 | tf_op jit(solution)/shard_map/ppermute | solution.py:457
  49.0 0.0 collective-permute-done.7.xp
  49.0 0.0 collective-permute-done.6.xm
  49.0 6.5 %shard_map.58 = (f32[32,1024]{1,0:T(8,128)S(1)}, bf16[32,1024]{1,0:T(8,128)(2,1)S(1)}, bf16[32,1024]{1,0:T(8,128)(2,1)S(1)}) custom-call(bf16[32,1024]{1,0:T(8,128)(2,1)S(1)} %get-tuple-element.33.par, bf16[5,32,1024]{2,1,0:T(8,128)(2,1)S(1)} %collective-permute-done.zm, bf16[5,32,1024]{2,1,0:T(8,128)(2,1)S(1)} %collective-permute-done.1.zp, ...), custom_call_target="tpu_custom_call" | custom-call | tf_op jit(solution)/shard_map/pallas_call | solution.py:404
  55.5 0.3 collective-permute-start.10
  55.7 5.3 %collective-permute-start.11 = (bf16[32,1024]{1,0:T(8,128)(2,1)S(1)}, bf16[32,1024]{1,0:T(8,128)(2,1)S(1)}, u32[]{:S(2)}, u32[]{:S(2)}) collective-permute-start(bf16[32,1024]{1,0:T(8,128)(2,1)S(1)} %get-tuple-element.41), channel_id=1, source_target_pairs={{0,240},{4,244},{8,248},{12,252},{16,0},{20,4},{24,8},{28,12},{32,... | collective-permute-start | bytes 196616 | tf_op jit(solution)/shard_map/ppermute | solution.py:457
  61.1 5.8 %shard_map.57.own = f32[8,32,1024]{2,1,0:T(8,128)S(1)} custom-call(bf16[16,256,512]{2,1,0:T(8,128)(2,1)S(1)} %get-tuple-element.32.packed, bf16[2,128,256]{2,1,0:T(8,128)(2,1)S(1)} %get-tuple-element.31.my), custom_call_target="tpu_custom_call" | custom-call | tf_op jit(solution)/shard_map/pallas_call | solution.py:335
  66.9 0.0 collective-permute-done.10.low_c
  66.9 0.0 collective-permute-done.11.high_c
  66.9 0.0 collective-permute-done.8.low
  66.9 0.0 collective-permute-done.9.high
  66.9 1.8 %shard_map.59 = bf16[8,32,1024]{2,1,0:T(8,128)(2,1)S(1)} custom-call(f32[8,32,1024]{2,1,0:T(8,128)S(1)} %shard_map.57.own, f32[32,1024]{1,0:T(8,128)S(1)} %get-tuple-element.37.own_c, bf16[4,32,1024]{2,1,0:T(8,128)(2,1)S(1)} %collective-permute-done.8.low, bf16[4,32,1024]{2,1,0:T(8,128)(2,1)S(1)} %collective-permute-done.9.high, ...), custom_call_target="tpu_custom_call" | custom-call | tf_op jit(solution)/shard_map/pallas_call | solution.py:448
  68.7 21.3 %all_to_all.5 = bf16[4,2,32,1024]{3,2,1,0:T(8,128)(2,1)S(1)} all-to-all(bf16[4,2,32,1024]{3,2,1,0:T(8,128)(2,1)S(1)} %bitcast.5), channel_id=1, replica_groups=mesh['box'=64,'term'=4] {'term'}, dimensions={0} | all-to-all | bytes 1048576 | tf_op jit(solution)/shard_map/all_to_all | solution.py:501
  90.1 1.1 %convert_element_type.3 = f32[4,2,32,1024]{3,2,1,0:T(8,128)} convert(bf16[4,2,32,1024]{3,2,1,0:T(8,128)(2,1)S(1)} %all_to_all.5) | non-fusion elementwise | flops 262144 | bytes 1572864 | tf_op jit(solution)/shard_map/convert_element_type | solution.py:502
  (7 shorter events, 0.1 us)
Async XLA Ops:
  0.0 23.8 %copy-start.1 = (bf16[16,3,32,32]{3,2,1,0:T(8,128)(2,1)S(1)}, bf16[16,3,32,32]{3,2,1,0:T(8,128)(2,1)}, u32[]{:S(2)}) copy-start(bf16[16,3,32,32]{3,2,1,0:T(8,128)(2,1)} %coarse.1) | copy-start | bytes 294916
  0.0 23.8 %copy-start = (bf16[16,3,32,32]{3,2,1,0:T(8,128)(2,1)S(1)}, bf16[16,3,32,32]{3,2,1,0:T(8,128)(2,1)}, u32[]{:S(2)}) copy-start(bf16[16,3,32,32]{3,2,1,0:T(8,128)(2,1)} %fine.1) | copy-start | bytes 294916
  0.1 0.8 copy-start.2
  0.8 23.0 %copy-start.3 = (s32[8]{0:T(128)S(1)}, s32[8]{0:T(128)}, u32[]{:S(2)}) copy-start(s32[8]{0:T(128)} %exponents.1) | copy-start | bytes 100
  5.3 15.0 %collective-permute-start = (bf16[5,32,1024]{2,1,0:T(8,128)(2,1)S(1)}, bf16[5,32,1024]{2,1,0:T(8,128)(2,1)S(1)}, u32[]{:S(2)}, u32[]{:S(2)}) collective-permute-start(bf16[5,32,1024]{2,1,0:T(8,128)(2,1)S(1)} %get-tuple-element.27), channel_id=1, source_target_pairs={{0,4},{1,5},{2,6},{3,7},{4,11},{5,10},{6,9},{7,8},{8,12},{9,13},{1... | collective-permute-start | bytes 983048 | tf_op jit(solution)/shard_map/ppermute | solution.py:471
  5.4 14.9 %collective-permute-start.1 = (bf16[5,32,1024]{2,1,0:T(8,128)(2,1)S(1)}, bf16[5,32,1024]{2,1,0:T(8,128)(2,1)S(1)}, u32[]{:S(2)}, u32[]{:S(2)}) collective-permute-start(bf16[5,32,1024]{2,1,0:T(8,128)(2,1)S(1)} %get-tuple-element.28), channel_id=1, source_target_pairs={{0,255},{1,254},{2,253},{3,252},{4,0},{5,1},{6,2},{7,3},{8,7},{9,6... | collective-permute-start | bytes 983048 | tf_op jit(solution)/shard_map/ppermute | solution.py:471
  15.4 15.5 %collective-permute-start.3 = (bf16[4,32,1024]{2,1,0:T(8,128)(2,1)S(1)}, bf16[4,32,1024]{2,1,0:T(8,128)(2,1)S(1)}, u32[]{:S(2)}, u32[]{:S(2)}) collective-permute-start(bf16[4,32,1024]{2,1,0:T(8,128)(2,1)S(1)} %get-tuple-element.25.low_x), channel_id=1, source_target_pairs={{0,192},{4,196},{8,200},{12,204},{16,208},{20,212},{24,216},{28,22... | collective-permute-start | bytes 786440 | tf_op jit(solution)/shard_map/ppermute | solution.py:457
  16.2 16.6 %collective-permute-start.2 = (bf16[4,32,1024]{2,1,0:T(8,128)(2,1)S(1)}, bf16[4,32,1024]{2,1,0:T(8,128)(2,1)S(1)}, u32[]{:S(2)}, u32[]{:S(2)}) collective-permute-start(bf16[4,32,1024]{2,1,0:T(8,128)(2,1)S(1)} %get-tuple-element.26.high_x), channel_id=1, source_target_pairs={{0,64},{4,68},{8,72},{12,76},{16,80},{20,84},{24,88},{28,92},{32,9... | collective-permute-start | bytes 786440 | tf_op jit(solution)/shard_map/ppermute | solution.py:457
  20.4 12.3 %collective-permute-start.4 = (bf16[4,32,1024]{2,1,0:T(8,128)(2,1)S(1)}, bf16[4,32,1024]{2,1,0:T(8,128)(2,1)S(1)}, u32[]{:S(2)}, u32[]{:S(2)}) collective-permute-start(bf16[4,32,1024]{2,1,0:T(8,128)(2,1)S(1)} %pad_maximum_fusion), channel_id=1, source_target_pairs={{0,64},{4,68},{8,72},{12,76},{16,80},{20,84},{24,88},{28,92},{32,9... | collective-permute-start | bytes 786440 | tf_op jit(solution)/shard_map/ppermute | solution.py:457
  20.6 12.2 %collective-permute-start.5 = (bf16[4,32,1024]{2,1,0:T(8,128)(2,1)S(1)}, bf16[4,32,1024]{2,1,0:T(8,128)(2,1)S(1)}, u32[]{:S(2)}, u32[]{:S(2)}) collective-permute-start(bf16[4,32,1024]{2,1,0:T(8,128)(2,1)S(1)} %pad_maximum_fusion.1), channel_id=1, source_target_pairs={{0,192},{4,196},{8,200},{12,204},{16,208},{20,212},{24,216},{28,22... | collective-permute-start | bytes 786440 | tf_op jit(solution)/shard_map/ppermute | solution.py:457
  26.9 22.1 %collective-permute-start.7 = (bf16[3,32,1024]{2,1,0:T(8,128)(2,1)S(1)}, bf16[3,32,1024]{2,1,0:T(8,128)(2,1)S(1)}, u32[]{:S(2)}, u32[]{:S(2)}) collective-permute-start(bf16[3,32,1024]{2,1,0:T(8,128)(2,1)S(1)} %pad_maximum_fusion.2), channel_id=1, source_target_pairs={{0,192},{4,196},{8,200},{12,204},{16,208},{20,212},{24,216},{28,22... | collective-permute-start | bytes 589832 | tf_op jit(solution)/shard_map/ppermute | solution.py:457
  30.9 18.1 %collective-permute-start.6 = (bf16[3,32,1024]{2,1,0:T(8,128)(2,1)S(1)}, bf16[3,32,1024]{2,1,0:T(8,128)(2,1)S(1)}, u32[]{:S(2)}, u32[]{:S(2)}) collective-permute-start(bf16[3,32,1024]{2,1,0:T(8,128)(2,1)S(1)} %pad_maximum_fusion.2), channel_id=1, source_target_pairs={{0,64},{4,68},{8,72},{12,76},{16,80},{20,84},{24,88},{28,92},{32,9... | collective-permute-start | bytes 589832 | tf_op jit(solution)/shard_map/ppermute | solution.py:457
  43.5 23.4 %collective-permute-start.8 = (bf16[4,32,1024]{2,1,0:T(8,128)(2,1)S(1)}, bf16[4,32,1024]{2,1,0:T(8,128)(2,1)S(1)}, u32[]{:S(2)}, u32[]{:S(2)}) collective-permute-start(bf16[4,32,1024]{2,1,0:T(8,128)(2,1)S(1)} %get-tuple-element.38), channel_id=1, source_target_pairs={{0,16},{4,20},{8,24},{12,28},{16,32},{20,36},{24,40},{28,44},{32,4... | collective-permute-start | bytes 786440 | tf_op jit(solution)/shard_map/ppermute | solution.py:457
  43.6 23.3 %collective-permute-start.9 = (bf16[4,32,1024]{2,1,0:T(8,128)(2,1)S(1)}, bf16[4,32,1024]{2,1,0:T(8,128)(2,1)S(1)}, u32[]{:S(2)}, u32[]{:S(2)}) collective-permute-start(bf16[4,32,1024]{2,1,0:T(8,128)(2,1)S(1)} %get-tuple-element.39), channel_id=1, source_target_pairs={{0,240},{4,244},{8,248},{12,252},{16,0},{20,4},{24,8},{28,12},{32,... | collective-permute-start | bytes 786440 | tf_op jit(solution)/shard_map/ppermute | solution.py:457
  55.5 11.4 %collective-permute-start.10 = (bf16[32,1024]{1,0:T(8,128)(2,1)S(1)}, bf16[32,1024]{1,0:T(8,128)(2,1)S(1)}, u32[]{:S(2)}, u32[]{:S(2)}) collective-permute-start(bf16[32,1024]{1,0:T(8,128)(2,1)S(1)} %get-tuple-element.40), channel_id=1, source_target_pairs={{0,16},{4,20},{8,24},{12,28},{16,32},{20,36},{24,40},{28,44},{32,4... | collective-permute-start | bytes 196616 | tf_op jit(solution)/shard_map/ppermute | solution.py:457
  55.7 11.1 %collective-permute-start.11 = (bf16[32,1024]{1,0:T(8,128)(2,1)S(1)}, bf16[32,1024]{1,0:T(8,128)(2,1)S(1)}, u32[]{:S(2)}, u32[]{:S(2)}) collective-permute-start(bf16[32,1024]{1,0:T(8,128)(2,1)S(1)} %get-tuple-element.41), channel_id=1, source_target_pairs={{0,240},{4,244},{8,248},{12,252},{16,0},{20,4},{24,8},{28,12},{32,... | collective-permute-start | bytes 196616 | tf_op jit(solution)/shard_map/ppermute | solution.py:457

commit v6 on v5

--- a/solution.py
+++ b/solution.py
@@ -117,61 +117,58 @@
     )(exponents, fine, coarse)
 
 
-def prepare_kernel(where, boxes, s, out, low_x, high_x, up, dn, fz, ky, st2, rows, wide):
-    step = pl.program_id(0)
+def prepare_kernel(where, mine, other, s, out, low_x, high_x, up, dn, fz, ky, st2, rows, wide):
     scale = s[...]
-
-    @pl.when(step == 0)
-    def _():
-        tiled = lax.dot_general(
-            scale, same(32, 128, lambda i, j: j % 32 == i), (((0,), (0,)), ((), ())), preferred_element_type=F32
-        )
-        block = same(128, 128, lambda i, j: i // 32 == j // 32).astype(F32)
-        for cz in range(2):
-            part = tiled[cz * 32 : cz * 32 + 32]
-            fz[cz * 128 : cz * 128 + 128, :] = (jnp.concatenate([part] * 4, axis=0) * block).astype(BF)
-        st2[...] = lax.dot_general(
-            scale, same(32, 64, lambda i, j: j % 32 == i), (((0,), (0,)), ((), ())), preferred_element_type=F32
+    tiled = lax.dot_general(
+        scale, same(32, 128, lambda i, j: j % 32 == i), (((0,), (0,)), ((), ())), preferred_element_type=F32
+    )
+    block = same(128, 128, lambda i, j: i // 32 == j // 32).astype(F32)
+    for cz in range(2):
+        part = tiled[cz * 32 : cz * 32 + 32]
+        fz[cz * 128 : cz * 128 + 128, :] = (jnp.concatenate([part] * 4, axis=0) * block).astype(BF)
+    st2[...] = lax.dot_general(
+        scale, same(32, 64, lambda i, j: j % 32 == i), (((0,), (0,)), ((), ())), preferred_element_type=F32
+    ).astype(BF)
+    spread = lax.dot_general(
+        scale, same(32, 1024, lambda i, j: j // 32 == i), (((0,), (0,)), ((), ())), preferred_element_type=F32
+    )
+    lane = lax.broadcasted_iota(jnp.int32, (32, 1024), 1) % 32 == lax.broadcasted_iota(jnp.int32, (32, 1024), 0)
+    for y in range(64):
+        ky[y * 32 : y * 32 + 32, :] = jnp.where(
+            lane, jnp.broadcast_to(spread[y : y + 1], (32, 1024)), 0.0
         ).astype(BF)
-        spread = lax.dot_general(
-            scale, same(32, 1024, lambda i, j: j // 32 == i), (((0,), (0,)), ((), ())), preferred_element_type=F32
-        )
-        lane = lax.broadcasted_iota(jnp.int32, (32, 1024), 1) % 32 == lax.broadcasted_iota(jnp.int32, (32, 1024), 0)
-        for y in range(64):
-            ky[y * 32 : y * 32 + 32, :] = jnp.where(
-                lane, jnp.broadcast_to(spread[y : y + 1], (32, 1024)), 0.0
-            ).astype(BF)
-
     for yg in range(16):
         cy, g = divmod(yg, 8)
-        for cx in range(2):
-            for cz in range(2):
-                rows[yg * 64 + cx * 32 : yg * 64 + cx * 32 + 32, cz * 128 : cz * 128 + 128] = boxes[
-                    0, 4 * cx + 2 * cy + cz, :, g * 128 : g * 128 + 128
-                ]
+        for k, boxes in enumerate((mine, other)):
+            for cx in range(2):
+                for cz in range(2):
+                    row = yg * 128 + k * 64 + cx * 32
+                    rows[row : row + 32, cz * 128 : cz * 128 + 128] = boxes[
+                        0, 4 * cx + 2 * cy + cz, :, g * 128 : g * 128 + 128
+                    ]
     along_z = dot(rows[...], fz[...]).astype(BF)
     for yg in range(16):
-        wide[:, yg * 128 : yg * 128 + 128] = along_z[yg * 64 : yg * 64 + 64]
+        wide[:, yg * 128 : yg * 128 + 128] = along_z[yg * 128 : yg * 128 + 128]
     along_y = dot(wide[...], ky[...]).astype(BF)
-    parent = dot(scale, along_y).astype(BF)
-
-    @pl.when(step == 0)
+    parents = [dot(scale, along_y[k * 64 : k * 64 + 64]).astype(BF) for k in range(2)]
+    out[...] = parents[0]
+    low_x[...] = mine[0, :4]
+    high_x[...] = mine[0, 4:]
+
+    def fill(first, second):
+        for i in range(4):
+            up[i] = (mine, other)[first][0, 2 * i + 1]
+            dn[i] = (mine, other)[second][0, 2 * i]
+        up[4] = parents[first]
+        dn[4] = parents[second]
+
+    @pl.when(where[2] == 0)
     def _():
-        out[...] = parent
-        low_x[...] = boxes[0, :4]
-        high_x[...] = boxes[0, 4:]
-
-    @pl.when(step == where[2])
+        fill(0, 1)
+
+    @pl.when(where[2] != 0)
     def _():
-        for i in range(4):
-            up[i] = boxes[0, 2 * i + 1]
-        up[4] = parent
-
-    @pl.when(step != where[2])
-    def _():
-        for i in range(4):
-            dn[i] = boxes[0, 2 * i]
-        dn[4] = parent
+        fill(1, 0)
 
 
 def prepare(where, fine_coeffs, s):
@@ -184,15 +181,19 @@
         out_shape=tuple(jax.ShapeDtypeStruct(shape, BF) for shape in shapes),
         grid_spec=pltpu.PrefetchScalarGridSpec(
             num_scalar_prefetch=1,
-            grid=(2,),
-            in_specs=[pl.BlockSpec((1, 8, 32, 1024), lambda i, w: (w[i], 0, 0, 0)), whole(32, 64)],
+            grid=(1,),
+            in_specs=[
+                pl.BlockSpec((1, 8, 32, 1024), lambda i, w: (w[0], 0, 0, 0)),
+                pl.BlockSpec((1, 8, 32, 1024), lambda i, w: (w[1], 0, 0, 0)),
+                whole(32, 64),
+            ],
             out_specs=[whole(*shape) for shape in shapes],
-            scratch_shapes=[pltpu.VMEM((1024, 256), BF), pltpu.VMEM((64, 2048), BF)],
+            scratch_shapes=[pltpu.VMEM((2048, 256), BF), pltpu.VMEM((128, 2048), BF)],
         ),
         interpret=INTERPRET,
         name="prepare",
         **grant(24),
-    )(where, fine_coeffs, s)
+    )(where, fine_coeffs, fine_coeffs, s)
 
 
 PITCH_U = 68
@@ -245,18 +246,20 @@
 def outer_kernel(
     inner, xm_own, xp_own, xm_far, xp_far, wz, wx, my,
     send_up, send_dn, packed,
-    left, mid, wide, done,
+    left, mid_a, mid_b, wide, done,
 ):
     for cy in range(2):
         own = 2 * cy
         fill_left(left, [xm_far[cy], xm_own[own], xm_own[own + 1], xm_far[2 + cy]], cy * 512)
         fill_left(left, [xp_far[cy], xp_own[own], xp_own[own + 1], xp_far[2 + cy]], cy * 512 + 32)
 
-    def term(t, carry):
+    def along_z(t, mid):
         weight = wz[t]
         for m in range(2):
             passed = dot(left[m * 512 : m * 512 + 512, :], weight).astype(BF)
             mid[m * 8 : m * 8 + 8] = passed.reshape(8, 64, 256)
+
+    def along_x(t, mid):
         weight_x = wx[t]
         start = pl.multiple_of(t * (32 * PITCH_U), 8)
         for yg in range(16):
@@ -264,33 +267,46 @@
             passed = dot(weight_x, data)
             wide[pl.ds(start + 2 * yg * PITCH_U, 64), :] = passed[:, :128]
             wide[pl.ds(start + (2 * yg + 1) * PITCH_U, 64), :] = passed[:, 128:]
-        return carry
-
-    lax.fori_loop(0, 8, term, 0)
-
-    def rows(k, carry):
-        data = jnp.concatenate(
-            [wide[pl.ds(4 * k + i, 256, stride=PITCH_U), :].astype(BF) for i in range(4)], axis=1
-        )
-        packed[k] = data
-        fold_rows(dot(my[0], data), done, pl.multiple_of(k * (4 * PITCH_U), 8), PITCH_U)
-        return carry
-
-    lax.fori_loop(0, 16, rows, 0)
+
+    along_z(0, mid_a)
+
+    def terms(k, carry):
+        along_z(2 * k + 1, mid_b)
+        along_x(2 * k, mid_a)
+        along_z(2 * k + 2, mid_a)
+        along_x(2 * k + 1, mid_b)
+        return carry
+
+    lax.fori_loop(0, 3, terms, 0)
+    along_z(7, mid_b)
+    along_x(6, mid_a)
+    along_x(7, mid_b)
+
+    def rows(step, carry):
+        for k in (2 * step, 2 * step + 1):
+            data = jnp.concatenate(
+                [wide[pl.ds(4 * k + i, 256, stride=PITCH_U), :].astype(BF) for i in range(4)], axis=1
+            )
+            packed[k] = data
+            fold_rows(dot(my[0], data), done, pl.multiple_of(k * (4 * PITCH_U), 8), PITCH_U)
+        return carry
+
+    lax.fori_loop(0, 8, rows, 0)
 
     lane = lax.broadcasted_iota(jnp.int32, (64, 128), 1) // 32
 
-    def relay(g, carry):
-        at = pl.multiple_of(g * 128, 128)
-        for side in range(2):
-            target = send_up if side else send_dn
-            for cz in range(2):
-                block = gather_lanes(done, side * 32, g, cz, lane).astype(BF)
-                for cx in range(2):
-                    target[2 * cx + cz, :, pl.ds(at, 128)] = block[cx * 32 : cx * 32 + 32]
-        return carry
-
-    lax.fori_loop(0, 8, relay, 0)
+    def relay(step, carry):
+        for g in (2 * step, 2 * step + 1):
+            at = pl.multiple_of(g * 128, 128)
+            for side in range(2):
+                target = send_up if side else send_dn
+                for cz in range(2):
+                    block = gather_lanes(done, side * 32, g, cz, lane).astype(BF)
+                    for cx in range(2):
+                        target[2 * cx + cz, :, pl.ds(at, 128)] = block[cx * 32 : cx * 32 + 32]
+        return carry
+
+    lax.fori_loop(0, 4, relay, 0)
 
 
 def outer_passes(*operands):
@@ -304,6 +320,7 @@
         [
             pltpu.VMEM((1024, 512), BF),
             pltpu.VMEM((16, 64, 256), BF),
+            pltpu.VMEM((16, 64, 256), BF),
             pltpu.VMEM((256 * PITCH_U, 128), F32),
             pltpu.VMEM((64 * PITCH_U, 128), F32),
         ],
@@ -335,7 +352,13 @@
     return call(own_kernel, jax.ShapeDtypeStruct((8, 32, 1024), F32), [pltpu.VMEM((64 * PITCH_U, 128), F32)])(*operands)
 
 
-def coarse_kernel(par, zm, zp, xm, xp, wz, wx, my, out, send_up, send_dn, left, mid, wide, done):
+def coarse_kernel(
+    par, zm, zp, xm, xp, wz, wx, my, fine_up, fine_dn,
+    out, send_up, send_dn,
+    left, mid_a, mid_b, wide, done,
+):
+    send_up[:4] = fine_up[...]
+    send_dn[:4] = fine_dn[...]
     sources = [
         [xm[1], xm[0], xm[2]],
         [zm[4], par[...], zp[4]],
@@ -347,10 +370,11 @@
                 row = g * 96 + xb * 32
                 left[row : row + 32, zb * 128 : zb * 128 + 128] = sources[xb][zb][:, g * 128 : g * 128 + 128]
 
-    def pair(h, carry):
+    def along_z(h, mid):
         weight = jnp.concatenate([wz[2 * h], wz[2 * h + 1]], axis=1)
         mid[...] = dot(left[...], weight).astype(BF).reshape(8, 96, 256)
-        start = pl.multiple_of(h * (16 * PITCH_CU), 8)
+
+    def along_x(h, mid):
         for i in range(2):
             weight_x = wx[2 * h + i]
             for g in range(0, 8, 2):
@@ -358,11 +382,16 @@
                     [mid[g, :, i * 128 : i * 128 + 128], mid[g + 1, :, i * 128 : i * 128 + 128]], axis=1
                 )
                 moved = dot(weight_x, data)
-                wide[pl.ds(start + (i * 8 + g) * PITCH_CU, 32), :] = moved[:, :128]
-                wide[pl.ds(start + (i * 8 + g + 1) * PITCH_CU, 32), :] = moved[:, 128:]
-        return carry
-
-    lax.fori_loop(0, 4, pair, 0)
+                row = (h * 16 + i * 8 + g) * PITCH_CU
+                wide[row : row + 32, :] = moved[:, :128]
+                wide[row + PITCH_CU : row + PITCH_CU + 32, :] = moved[:, 128:]
+
+    mids = (mid_a, mid_b)
+    along_z(0, mid_a)
+    for h in range(4):
+        if h < 3:
+            along_z(h + 1, mids[(h + 1) % 2])
+        along_x(h, mids[h % 2])
 
     def rows(k, carry):
         data = jnp.concatenate(
@@ -390,9 +419,9 @@
                 part = done[pl.ds(vb * 32 + 4 * g + j, 32, stride=PITCH_CV), :]
                 block = jnp.where(lane == j, pltpu.roll(part, 32 * j, 1), block)
             if vb == 0:
-                send_dn[:, pl.ds(at, 128)] = block.astype(BF)
+                send_dn[4, :, pl.ds(at, 128)] = block.astype(BF)
             elif vb == 2:
-                send_up[:, pl.ds(at, 128)] = block.astype(BF)
+                send_up[4, :, pl.ds(at, 128)] = block.astype(BF)
             else:
                 out[:, pl.ds(at, 128)] = block
         return carry
@@ -405,11 +434,12 @@
         coarse_kernel,
         (
             jax.ShapeDtypeStruct((32, 1024), F32),
-            jax.ShapeDtypeStruct((32, 1024), BF),
-            jax.ShapeDtypeStruct((32, 1024), BF),
+            jax.ShapeDtypeStruct((5, 32, 1024), BF),
+            jax.ShapeDtypeStruct((5, 32, 1024), BF),
         ),
         [
             pltpu.VMEM((768, 384), BF),
+            pltpu.VMEM((8, 96, 256), BF),
             pltpu.VMEM((8, 96, 256), BF),
             pltpu.VMEM((64 * PITCH_CU, 128), F32),
             pltpu.VMEM((32 * PITCH_CV, 128), F32),
@@ -417,8 +447,8 @@
     )(*operands)
 
 
-def final_kernel(own, own_c, low, high, low_c, high_c, fz, ky, st2, out, rows, mixed, deep):
-    total = own_c[...] + low_c[...].astype(F32) + high_c[...].astype(F32)
+def final_kernel(own, own_c, low, high, fz, ky, st2, out, rows, mixed, deep):
+    total = own_c[...] + low[4].astype(F32) + high[4].astype(F32)
     hi, lo = split(total)
     for g in range(8):
         rows[g * 64 : g * 64 + 32, :] = hi[:, g * 128 : g * 128 + 128]
@@ -471,12 +501,16 @@
     return lax.ppermute(block, ("box", "term"), route)
 
 
+def in_hbm(array):
+    return pltpu.with_memory_space_constraint(array, pltpu.HBM)
+
+
 def steps(fine_coeffs, fine_blocks, coarse_blocks, two_scale, term_exponent):
     p = lax.axis_index("box")
     t = lax.axis_index("term")
     other = lax.axis_size("term") - 1 - t
     where = jnp.stack([t, other, p % 2]).astype(jnp.int32)
-    par, low_x, high_x, up, dn, fz, ky, st2 = prepare(where, pltpu.with_memory_space_constraint(fine_coeffs, pltpu.HBM), two_scale)
+    par, low_x, high_x, up, dn, fz, ky, st2 = prepare(where, in_hbm(fine_coeffs), in_hbm(two_scale))
     zm = shift_z(up, 1)
     zp = shift_z(dn, -1)
     xm_own = shift(high_x, 16)
@@ -490,13 +524,11 @@
     cxp = shift(planes, -16)
 
     send_up, send_dn, packed = outer_passes(mid, xm_own, xp_own, xm_far, xp_far, wz, wx, my)
-    low = shift(send_up, 4)
-    high = shift(send_dn, -4)
-    out_c, send_up_c, send_dn_c = coarse_passes(par, zm, zp, cxm, cxp, cwz, cwx, cmy)
-    low_c = shift(send_up_c, 4)
-    high_c = shift(send_dn_c, -4)
+    out_c, full_up, full_dn = coarse_passes(par, zm, zp, cxm, cxp, cwz, cwx, cmy, send_up, send_dn)
+    low = shift(full_up, 4)
+    high = shift(full_dn, -4)
     out = own_rows(packed, my)
-    total = finish(out, out_c, low, high, low_c, high_c, fz, ky, st2)
+    total = finish(out, out_c, low, high, fz, ky, st2)
     groups = lax.axis_size("term")
     mine = lax.all_to_all(total.reshape(groups, 2, 32, 1024), "term", 0, 0)
     return mine.astype(F32)

time: 91.3 us -> 82.5 us (0.904)
  the two profiles are of different devices: /device:TPU:32 before, /device:TPU:30 now
where the time goes in v6:
time: 82.5 us; the launch traced here: 82.4 us
  Pallas kernels  31.4 us (38%)
  starting transfers between devices  19.1 us (23%)
  waiting for transfers between devices  17.3 us (21%)
  blocking collectives  13.2 us (16%)
  other arithmetic  1.24 us (2%)
    ppermute x8, starting transfers between devices, shift(): lax.ppermute(block, 'box', [(i, (i + distance) % count) for i in range(co...  13.3 us
    all_to_all x1, blocking collectives, steps(): mine = lax.all_to_all(total.reshape(groups, 2, 32, 1024), 'term', 0, 0)  13.2 us
    ppermute x2, waiting for transfers between devices, shift_z(): return lax.ppermute(block, ('box', 'term'), route)  12.7 us
    pallas_call x1, Pallas kernels, outer_passes(): call(outer_kernel, (jax.ShapeDtypeStruct((4, 32, 1024), BF), jax.ShapeDty...  7.54 us
    pallas_call x1, Pallas kernels, own_rows(): call(own_kernel, jax.ShapeDtypeStruct((8, 32, 1024), F32), [pltpu.VMEM((6...  5.8 us
    ppermute x2, starting transfers between devices, shift_z(): return lax.ppermute(block, ('box', 'term'), route)  5.75 us
    pallas_call x1, Pallas kernels, coarse_passes(): call(coarse_kernel, (jax.ShapeDtypeStruct((32, 1024), F32), jax.ShapeDtyp...  5.48 us
    ppermute x8, waiting for transfers between devices, shift(): lax.ppermute(block, 'box', [(i, (i + distance) % count) for i in range(co...  4.6 us
  transfers between devices with their start and end apart: 10, of which 3 were waited for; matrix products, arithmetic and copies ran while one was open for 0% of the time, Pallas kernels for 24%

profile of v6, /device:TPU:30, one launch (start us, length us, event | category | flops | bytes accessed | tf_op | source)
XLA Modules:
  0.0 82.4 jit_solution(5105722930228428157)
XLA Ops:
  0.0 0.0 copy-start
  0.0 0.0 copy-start.1
  0.0 0.0 copy-start.2
  0.0 0.1 pad_add_fusion.where
  0.1 4.1 %prepare.1 = (bf16[32,1024]{1,0:T(8,128)(2,1)S(1)}, bf16[4,32,1024]{2,1,0:T(8,128)(2,1)S(1)}, bf16[4,32,1024]{2,1,0:T(8,128)(2,1)S(1)}, bf16[5,32,1024]{2,1,0:T(...) custom-call(s32[3]{0:T(128)S(1)} %pad_add_fusion.where, ...), custom_call_target="tpu_custom_call" | custom-call | tf_op jit(solution)/shard_map/prepare/pallas_call | solution.py:179
  4.2 0.1 collective-permute-start
  4.3 5.7 %collective-permute-start.1 = (bf16[5,32,1024]{2,1,0:T(8,128)(2,1)S(1)}, bf16[5,32,1024]{2,1,0:T(8,128)(2,1)S(1)}, u32[]{:S(2)}, u32[]{:S(2)}) collective-permute-start(bf16[5,32,1024]{2,1,0:T(8,128)(2,1)S(1)} %get-tuple-element.28), channel_id=1, source_target_pairs={{0,255},{1,254},{2,253},{3,252},{4,0},{5,1},{6,2},{7,3},{8,7},{9,6... | collective-permute-start | bytes 983048 | tf_op jit(solution)/shard_map/ppermute | solution.py:501
  10.0 0.2 collective-permute-start.2
  10.2 1.8 %collective-permute-start.3 = (bf16[4,32,1024]{2,1,0:T(8,128)(2,1)S(1)}, bf16[4,32,1024]{2,1,0:T(8,128)(2,1)S(1)}, u32[]{:S(2)}, u32[]{:S(2)}) collective-permute-start(bf16[4,32,1024]{2,1,0:T(8,128)(2,1)S(1)} %get-tuple-element.25.low_x), channel_id=1, source_target_pairs={{0,192},{4,196},{8,200},{12,204},{16,208},{20,212},{24,216},{28,22... | collective-permute-start | bytes 786440 | tf_op jit(solution)/shard_map/ppermute | solution.py:487
  12.0 12.6 %collective-permute-done.zm = bf16[5,32,1024]{2,1,0:T(8,128)(2,1)S(1)} collective-permute-done((bf16[5,32,1024]{2,1,0:T(8,128)(2,1)S(1)}, bf16[5,32,1024]{2,1,0:T(8,128)(2,1)S(1)}, u32[]{:S(2)}, u32[]{:S(2)}) %collective-permute-start) | collective-permute-done | bytes 327712 | tf_op jit(solution)/shard_map/ppermute | solution.py:501
  24.6 0.1 collective-permute-done.1.zp
  24.8 0.3 collective-permute-start.4
  25.1 1.9 %collective-permute-start.5 = (bf16[4,32,1024]{2,1,0:T(8,128)(2,1)S(1)}, bf16[4,32,1024]{2,1,0:T(8,128)(2,1)S(1)}, u32[]{:S(2)}, u32[]{:S(2)}) collective-permute-start(bf16[4,32,1024]{2,1,0:T(8,128)(2,1)S(1)} %pad_maximum_fusion.1), channel_id=1, source_target_pairs={{0,192},{4,196},{8,200},{12,204},{16,208},{20,212},{24,216},{28,22... | collective-permute-start | bytes 786440 | tf_op jit(solution)/shard_map/ppermute | solution.py:487
  27.0 1.5 %collective-permute-start.6 = (bf16[3,32,1024]{2,1,0:T(8,128)(2,1)S(1)}, bf16[3,32,1024]{2,1,0:T(8,128)(2,1)S(1)}, u32[]{:S(2)}, u32[]{:S(2)}) collective-permute-start(bf16[3,32,1024]{2,1,0:T(8,128)(2,1)S(1)} %pad_maximum_fusion.2), channel_id=1, source_target_pairs={{0,64},{4,68},{8,72},{12,76},{16,80},{20,84},{24,88},{28,92},{32,9... | collective-permute-start | bytes 589832 | tf_op jit(solution)/shard_map/ppermute | solution.py:487
  28.5 0.0 collective-permute-done.2.xm_own
  28.5 0.6 collective-permute-start.7
  29.1 0.0 copy-done
  29.1 0.0 copy-done.1
  29.1 0.0 copy-done.2
  29.1 3.0 %weights.1 = (bf16[8,512,256]{2,1,0:T(8,128)(2,1)S(1)}, bf16[8,64,128]{2,1,0:T(8,128)(2,1)S(1)}, bf16[2,128,256]{2,1,0:T(8,128)(2,1)S(1)}, bf16[8,384,128]{2,1,0...) custom-call(s32[8]{0:T(128)S(1)} %copy-done.2, bf16[16,3,32,32]{3,2,1,0:T(8,128)(2,1)S(1)} %copy-done, ...), custom_call_target="tpu_custom_call" | custom-call | tf_op jit(solution)/shard_map/weights/pallas_call | solution.py:95
  32.1 3.7 %shard_map.55.inner = bf16[8,16,64,256]{3,2,1,0:T(8,128)(2,1)S(1)} custom-call(bf16[4,32,1024]{2,1,0:T(8,128)(2,1)S(1)} %get-tuple-element.25.low_x, bf16[4,32,1024]{2,1,0:T(8,128)(2,1)S(1)} %get-tuple-element.26.high_x, bf16[5,32,1024]{2,1,0:T(8,128)(2,1)S(1)} %collective-permute-done.zm, bf16[5,32,1024]{2,1,0:T(8,128)(2,1)S(1)} %collective-permute-done.1.zp, ...), custom_call_target="tpu_custom_call" | custom-call | tf_op jit(solution)/shard_map/pallas_call | solution.py:227
  35.8 0.0 collective-permute-done.3.xp_own
  35.8 0.0 collective-permute-done.4.xm_far
  35.8 0.0 collective-permute-done.5.xp_far
  35.8 7.5 %shard_map.56 = (bf16[4,32,1024]{2,1,0:T(8,128)(2,1)S(1)}, bf16[4,32,1024]{2,1,0:T(8,128)(2,1)S(1)}, bf16[16,256,512]{2,1,0:T(8,128)(2,1)S(1)}) custom-call(bf16[8,16,64,256]{3,2,1,0:T(8,128)(2,1)S(1)} %shard_map.55.inner, bf16[4,32,1024]{2,1,0:T(8,128)(2,1)S(1)} %collective-permute-done.2.xm_own, bf16[4,32,1024]{2,1,0:T(8,128)(2,1)S(1)} %collective-permute-done.3.xp_own, ...), custom_call_target="tpu_custom_call" | custom-call | tf_op jit(solution)/shard_map/pallas_call | solution.py:313
  43.4 0.0 collective-permute-done.6.xm
  43.4 0.0 collective-permute-done.7.xp
  43.4 5.5 %shard_map.58 = (f32[32,1024]{1,0:T(8,128)S(1)}, bf16[5,32,1024]{2,1,0:T(8,128)(2,1)S(1)}, bf16[5,32,1024]{2,1,0:T(8,128)(2,1)S(1)}) custom-call(bf16[32,1024]{1,0:T(8,128)(2,1)S(1)} %get-tuple-element.33.par, bf16[5,32,1024]{2,1,0:T(8,128)(2,1)S(1)} %collective-permute-done.zm, bf16[5,32,1024]{2,1,0:T(8,128)(2,1)S(1)} %collective-permute-done.1.zp, ...), custom_call_target="tpu_custom_call" | custom-call | tf_op jit(solution)/shard_map/pallas_call | solution.py:433
  48.9 7.0 %collective-permute-start.8 = (bf16[5,32,1024]{2,1,0:T(8,128)(2,1)S(1)}, bf16[5,32,1024]{2,1,0:T(8,128)(2,1)S(1)}, u32[]{:S(2)}, u32[]{:S(2)}) collective-permute-start(bf16[5,32,1024]{2,1,0:T(8,128)(2,1)S(1)} %get-tuple-element.40), channel_id=1, source_target_pairs={{0,16},{4,20},{8,24},{12,28},{16,32},{20,36},{24,40},{28,44},{32,4... | collective-permute-start | bytes 983048 | tf_op jit(solution)/shard_map/ppermute | solution.py:487
  55.9 0.0 collective-permute-start.9
  55.9 5.8 %shard_map.57.own = f32[8,32,1024]{2,1,0:T(8,128)S(1)} custom-call(bf16[16,256,512]{2,1,0:T(8,128)(2,1)S(1)} %get-tuple-element.32.packed, bf16[2,128,256]{2,1,0:T(8,128)(2,1)S(1)} %get-tuple-element.31.my), custom_call_target="tpu_custom_call" | custom-call | tf_op jit(solution)/shard_map/pallas_call | solution.py:352
  61.7 0.0 collective-permute-done.8.low
  61.7 4.6 %collective-permute-done.9.high = bf16[5,32,1024]{2,1,0:T(8,128)(2,1)S(1)} collective-permute-done((bf16[5,32,1024]{2,1,0:T(8,128)(2,1)S(1)}, bf16[5,32,1024]{2,1,0:T(8,128)(2,1)S(1)}, u32[]{:S(2)}, u32[]{:S(2)}) %collective-permute-start.9) | collective-permute-done | bytes 327712 | tf_op jit(solution)/shard_map/ppermute | solution.py:487
  66.3 1.8 %shard_map.59 = bf16[8,32,1024]{2,1,0:T(8,128)(2,1)S(1)} custom-call(f32[8,32,1024]{2,1,0:T(8,128)S(1)} %shard_map.57.own, f32[32,1024]{1,0:T(8,128)S(1)} %get-tuple-element.39.own_c, bf16[5,32,1024]{2,1,0:T(8,128)(2,1)S(1)} %collective-permute-done.8.low, bf16[5,32,1024]{2,1,0:T(8,128)(2,1)S(1)} %collective-permute-done.9.high, ...), custom_call_target="tpu_custom_call" | custom-call | tf_op jit(solution)/shard_map/pallas_call | solution.py:478
  68.1 13.2 %all_to_all.5 = bf16[4,2,32,1024]{3,2,1,0:T(8,128)(2,1)S(1)} all-to-all(bf16[4,2,32,1024]{3,2,1,0:T(8,128)(2,1)S(1)} %bitcast.5), channel_id=1, replica_groups=mesh['box'=64,'term'=4] {'term'}, dimensions={0} | all-to-all | bytes 1048576 | tf_op jit(solution)/shard_map/all_to_all | solution.py:533
  81.3 1.1 %convert_element_type.3 = f32[4,2,32,1024]{3,2,1,0:T(8,128)} convert(bf16[4,2,32,1024]{3,2,1,0:T(8,128)(2,1)S(1)} %all_to_all.5) | non-fusion elementwise | flops 262144 | bytes 1572864 | tf_op jit(solution)/shard_map/convert_element_type | solution.py:534
  (7 shorter events, 0.1 us)
Async XLA Ops:
  0.0 29.1 %copy-start = (bf16[16,3,32,32]{3,2,1,0:T(8,128)(2,1)S(1)}, bf16[16,3,32,32]{3,2,1,0:T(8,128)(2,1)}, u32[]{:S(2)}) copy-start(bf16[16,3,32,32]{3,2,1,0:T(8,128)(2,1)} %fine.1) | copy-start | bytes 294916
  0.0 29.1 %copy-start.1 = (bf16[16,3,32,32]{3,2,1,0:T(8,128)(2,1)S(1)}, bf16[16,3,32,32]{3,2,1,0:T(8,128)(2,1)}, u32[]{:S(2)}) copy-start(bf16[16,3,32,32]{3,2,1,0:T(8,128)(2,1)} %coarse.1) | copy-start | bytes 294916
  0.0 29.1 %copy-start.2 = (s32[8]{0:T(128)S(1)}, s32[8]{0:T(128)}, u32[]{:S(2)}) copy-start(s32[8]{0:T(128)} %exponents.1) | copy-start | bytes 100
  4.2 20.3 %collective-permute-start = (bf16[5,32,1024]{2,1,0:T(8,128)(2,1)S(1)}, bf16[5,32,1024]{2,1,0:T(8,128)(2,1)S(1)}, u32[]{:S(2)}, u32[]{:S(2)}) collective-permute-start(bf16[5,32,1024]{2,1,0:T(8,128)(2,1)S(1)} %get-tuple-element.27), channel_id=1, source_target_pairs={{0,4},{1,5},{2,6},{3,7},{4,11},{5,10},{6,9},{7,8},{8,12},{9,13},{1... | collective-permute-start | bytes 983048 | tf_op jit(solution)/shard_map/ppermute | solution.py:501
  4.3 20.4 %collective-permute-start.1 = (bf16[5,32,1024]{2,1,0:T(8,128)(2,1)S(1)}, bf16[5,32,1024]{2,1,0:T(8,128)(2,1)S(1)}, u32[]{:S(2)}, u32[]{:S(2)}) collective-permute-start(bf16[5,32,1024]{2,1,0:T(8,128)(2,1)S(1)} %get-tuple-element.28), channel_id=1, source_target_pairs={{0,255},{1,254},{2,253},{3,252},{4,0},{5,1},{6,2},{7,3},{8,7},{9,6... | collective-permute-start | bytes 983048 | tf_op jit(solution)/shard_map/ppermute | solution.py:501
  10.0 18.6 %collective-permute-start.2 = (bf16[4,32,1024]{2,1,0:T(8,128)(2,1)S(1)}, bf16[4,32,1024]{2,1,0:T(8,128)(2,1)S(1)}, u32[]{:S(2)}, u32[]{:S(2)}) collective-permute-start(bf16[4,32,1024]{2,1,0:T(8,128)(2,1)S(1)} %get-tuple-element.26.high_x), channel_id=1, source_target_pairs={{0,64},{4,68},{8,72},{12,76},{16,80},{20,84},{24,88},{28,92},{32,9... | collective-permute-start | bytes 786440 | tf_op jit(solution)/shard_map/ppermute | solution.py:487
  10.2 25.6 %collective-permute-start.3 = (bf16[4,32,1024]{2,1,0:T(8,128)(2,1)S(1)}, bf16[4,32,1024]{2,1,0:T(8,128)(2,1)S(1)}, u32[]{:S(2)}, u32[]{:S(2)}) collective-permute-start(bf16[4,32,1024]{2,1,0:T(8,128)(2,1)S(1)} %get-tuple-element.25.low_x), channel_id=1, source_target_pairs={{0,192},{4,196},{8,200},{12,204},{16,208},{20,212},{24,216},{28,22... | collective-permute-start | bytes 786440 | tf_op jit(solution)/shard_map/ppermute | solution.py:487
  24.8 11.0 %collective-permute-start.4 = (bf16[4,32,1024]{2,1,0:T(8,128)(2,1)S(1)}, bf16[4,32,1024]{2,1,0:T(8,128)(2,1)S(1)}, u32[]{:S(2)}, u32[]{:S(2)}) collective-permute-start(bf16[4,32,1024]{2,1,0:T(8,128)(2,1)S(1)} %pad_maximum_fusion), channel_id=1, source_target_pairs={{0,64},{4,68},{8,72},{12,76},{16,80},{20,84},{24,88},{28,92},{32,9... | collective-permute-start | bytes 786440 | tf_op jit(solution)/shard_map/ppermute | solution.py:487
  25.1 10.7 %collective-permute-start.5 = (bf16[4,32,1024]{2,1,0:T(8,128)(2,1)S(1)}, bf16[4,32,1024]{2,1,0:T(8,128)(2,1)S(1)}, u32[]{:S(2)}, u32[]{:S(2)}) collective-permute-start(bf16[4,32,1024]{2,1,0:T(8,128)(2,1)S(1)} %pad_maximum_fusion.1), channel_id=1, source_target_pairs={{0,192},{4,196},{8,200},{12,204},{16,208},{20,212},{24,216},{28,22... | collective-permute-start | bytes 786440 | tf_op jit(solution)/shard_map/ppermute | solution.py:487
  27.0 16.4 %collective-permute-start.6 = (bf16[3,32,1024]{2,1,0:T(8,128)(2,1)S(1)}, bf16[3,32,1024]{2,1,0:T(8,128)(2,1)S(1)}, u32[]{:S(2)}, u32[]{:S(2)}) collective-permute-start(bf16[3,32,1024]{2,1,0:T(8,128)(2,1)S(1)} %pad_maximum_fusion.2), channel_id=1, source_target_pairs={{0,64},{4,68},{8,72},{12,76},{16,80},{20,84},{24,88},{28,92},{32,9... | collective-permute-start | bytes 589832 | tf_op jit(solution)/shard_map/ppermute | solution.py:487
  28.5 14.8 %collective-permute-start.7 = (bf16[3,32,1024]{2,1,0:T(8,128)(2,1)S(1)}, bf16[3,32,1024]{2,1,0:T(8,128)(2,1)S(1)}, u32[]{:S(2)}, u32[]{:S(2)}) collective-permute-start(bf16[3,32,1024]{2,1,0:T(8,128)(2,1)S(1)} %pad_maximum_fusion.2), channel_id=1, source_target_pairs={{0,192},{4,196},{8,200},{12,204},{16,208},{20,212},{24,216},{28,22... | collective-permute-start | bytes 589832 | tf_op jit(solution)/shard_map/ppermute | solution.py:487
  48.9 12.8 %collective-permute-start.8 = (bf16[5,32,1024]{2,1,0:T(8,128)(2,1)S(1)}, bf16[5,32,1024]{2,1,0:T(8,128)(2,1)S(1)}, u32[]{:S(2)}, u32[]{:S(2)}) collective-permute-start(bf16[5,32,1024]{2,1,0:T(8,128)(2,1)S(1)} %get-tuple-element.40), channel_id=1, source_target_pairs={{0,16},{4,20},{8,24},{12,28},{16,32},{20,36},{24,40},{28,44},{32,4... | collective-permute-start | bytes 983048 | tf_op jit(solution)/shard_map/ppermute | solution.py:487
  55.9 10.4 %collective-permute-start.9 = (bf16[5,32,1024]{2,1,0:T(8,128)(2,1)S(1)}, bf16[5,32,1024]{2,1,0:T(8,128)(2,1)S(1)}, u32[]{:S(2)}, u32[]{:S(2)}) collective-permute-start(bf16[5,32,1024]{2,1,0:T(8,128)(2,1)S(1)} %get-tuple-element.41), channel_id=1, source_target_pairs={{0,240},{4,244},{8,248},{12,252},{16,0},{20,4},{24,8},{28,12},{32,... | collective-permute-start | bytes 983048 | tf_op jit(solution)/shard_map/ppermute | solution.py:487

commit v7 on v6

--- a/solution.py
+++ b/solution.py
@@ -26,6 +26,15 @@
 def split(value):
     hi = value.astype(BF)
     return hi, (value - hi.astype(F32)).astype(BF)
+
+
+def repeat(count, factor, body):
+    def step(s, carry):
+        for k in range(factor):
+            body(s * factor + k)
+        return carry
+
+    lax.fori_loop(0, count // factor, step, 0)
 
 
 def call(kernel, outs, scratch=(), size=24):
@@ -132,11 +141,11 @@
     spread = lax.dot_general(
         scale, same(32, 1024, lambda i, j: j // 32 == i), (((0,), (0,)), ((), ())), preferred_element_type=F32
     )
-    lane = lax.broadcasted_iota(jnp.int32, (32, 1024), 1) % 32 == lax.broadcasted_iota(jnp.int32, (32, 1024), 0)
+    mask = same(32, 1024, lambda i, j: j % 32 == i)
     for y in range(64):
-        ky[y * 32 : y * 32 + 32, :] = jnp.where(
-            lane, jnp.broadcast_to(spread[y : y + 1], (32, 1024)), 0.0
-        ).astype(BF)
+        line = jnp.broadcast_to(spread[y : y + 1], (16, 1024)).astype(BF)
+        ky[y * 32 : y * 32 + 16, :] = line * mask[:16]
+        ky[y * 32 + 16 : y * 32 + 32, :] = line * mask[16:]
     for yg in range(16):
         cy, g = divmod(yg, 8)
         for k, boxes in enumerate((mine, other)):
@@ -213,14 +222,13 @@
             own = high_x if cx else low_x
             fill_left(left, [zm[2 * cx + cy], own[2 * cy], own[2 * cy + 1], zp[2 * cx + cy]], cy * 512 + cx * 32)
 
-    def term(t, carry):
+    def term(t):
         weight = wz[t]
         for m in range(2):
             passed = dot(left[m * 512 : m * 512 + 512, :], weight).astype(BF)
             mid[t, m * 8 : m * 8 + 8] = passed.reshape(8, 64, 256)
-        return carry
-
-    lax.fori_loop(0, 8, term, 0)
+
+    repeat(8, 2, term)
 
 
 def inner_pass(*operands):
@@ -282,31 +290,27 @@
     along_x(6, mid_a)
     along_x(7, mid_b)
 
-    def rows(step, carry):
-        for k in (2 * step, 2 * step + 1):
-            data = jnp.concatenate(
-                [wide[pl.ds(4 * k + i, 256, stride=PITCH_U), :].astype(BF) for i in range(4)], axis=1
-            )
-            packed[k] = data
-            fold_rows(dot(my[0], data), done, pl.multiple_of(k * (4 * PITCH_U), 8), PITCH_U)
-        return carry
-
-    lax.fori_loop(0, 8, rows, 0)
+    def rows(k):
+        data = jnp.concatenate(
+            [wide[pl.ds(4 * k + i, 256, stride=PITCH_U), :].astype(BF) for i in range(4)], axis=1
+        )
+        packed[k] = data
+        fold_rows(dot(my[0], data), done, pl.multiple_of(k * (4 * PITCH_U), 8), PITCH_U)
+
+    repeat(16, 4, rows)
 
     lane = lax.broadcasted_iota(jnp.int32, (64, 128), 1) // 32
 
-    def relay(step, carry):
-        for g in (2 * step, 2 * step + 1):
-            at = pl.multiple_of(g * 128, 128)
-            for side in range(2):
-                target = send_up if side else send_dn
-                for cz in range(2):
-                    block = gather_lanes(done, side * 32, g, cz, lane).astype(BF)
-                    for cx in range(2):
-                        target[2 * cx + cz, :, pl.ds(at, 128)] = block[cx * 32 : cx * 32 + 32]
-        return carry
-
-    lax.fori_loop(0, 4, relay, 0)
+    def relay(g):
+        at = pl.multiple_of(g * 128, 128)
+        for side in range(2):
+            target = send_up if side else send_dn
+            for cz in range(2):
+                block = gather_lanes(done, side * 32, g, cz, lane).astype(BF)
+                for cx in range(2):
+                    target[2 * cx + cz, :, pl.ds(at, 128)] = block[cx * 32 : cx * 32 + 32]
+
+    repeat(8, 4, relay)
 
 
 def outer_passes(*operands):
@@ -328,24 +332,22 @@
 
 
 def own_kernel(packed, my, out, done):
-    def rows(k, carry):
+    def rows(k):
         fold_rows(dot(my[1], packed[k]), done, pl.multiple_of(k * (4 * PITCH_U), 8), PITCH_U)
-        return carry
-
-    lax.fori_loop(0, 16, rows, 0)
+
+    repeat(16, 4, rows)
 
     lane = lax.broadcasted_iota(jnp.int32, (64, 128), 1) // 32
 
-    def relay(g, carry):
+    def relay(g):
         at = pl.multiple_of(g * 128, 128)
         for cy in range(2):
             for cz in range(2):
                 block = gather_lanes(done, cy * 32, g, cz, lane)
                 for cx in range(2):
                     out[4 * cx + 2 * cy + cz, :, pl.ds(at, 128)] = block[cx * 32 : cx * 32 + 32]
-        return carry
-
-    lax.fori_loop(0, 8, relay, 0)
+
+    repeat(8, 4, relay)
 
 
 def own_rows(*operands):
@@ -393,7 +395,7 @@
             along_z(h + 1, mids[(h + 1) % 2])
         along_x(h, mids[h % 2])
 
-    def rows(k, carry):
+    def rows(k):
         data = jnp.concatenate(
             [wide[pl.ds(4 * k + i, 64, stride=PITCH_CU), :].astype(BF) for i in range(4)], axis=1
         )
@@ -405,13 +407,12 @@
             for j in range(1, 4):
                 total = total + pltpu.roll(lanes[j * 96 : j * 96 + 96], 128 - 32 * j, 1)
             done[pl.ds(start + i * PITCH_CV, 96), :] = total
-        return carry
-
-    lax.fori_loop(0, 8, rows, 0)
+
+    repeat(8, 4, rows)
 
     lane = lax.broadcasted_iota(jnp.int32, (32, 128), 1) // 32
 
-    def relay(g, carry):
+    def relay(g):
         at = pl.multiple_of(g * 128, 128)
         for vb in range(3):
             block = done[pl.ds(vb * 32 + 4 * g, 32, stride=PITCH_CV), :]
@@ -424,9 +425,8 @@
                 send_up[4, :, pl.ds(at, 128)] = block.astype(BF)
             else:
                 out[:, pl.ds(at, 128)] = block
-        return carry
-
-    lax.fori_loop(0, 8, relay, 0)
+
+    repeat(8, 8, relay)
 
 
 def coarse_passes(*operands):

time: 82.5 us -> 79 us (0.958)
  Pallas kernels: 31.4 us -> 24.6 us
  waiting for transfers between devices: 17.3 us -> 21 us
    ppermute x8, waiting for transfers between devices: 4.6 us -> 8.28 us  [shift(): lax.ppermute(block, 'box', [(i, (i + distance) % count) for i in range(co...]
    pallas_call x1, Pallas kernels: 5.8 us -> 2.52 us  [own_rows(): call(own_kernel, jax.ShapeDtypeStruct((8, 32, 1024), F32), [pltpu.VMEM((6...]
    pallas_call x1, Pallas kernels: 5.48 us -> 3.62 us  [coarse_passes(): call(coarse_kernel, (jax.ShapeDtypeStruct((32, 1024), F32), jax.ShapeDtyp...]
    pallas_call x1, Pallas kernels: 7.54 us -> 6.58 us  [outer_passes(): call(outer_kernel, (jax.ShapeDtypeStruct((4, 32, 1024), BF), jax.ShapeDty...]
  transfers between devices with their start and end apart: 10 -> 10, of which waited for: 3 -> 5; matrix products, arithmetic and copies ran while one was open for 0% -> 0% of each run, Pallas kernels for 24% -> 19%
where the time goes in v7:
time: 79 us; the launch traced here: 78.9 us
  Pallas kernels  24.6 us (31%)
  waiting for transfers between devices  21 us (27%)
  starting transfers between devices  18.7 us (24%)
  blocking collectives  13.2 us (17%)
  other arithmetic  1.24 us (2%)
    all_to_all x1, blocking collectives, steps(): mine = lax.all_to_all(total.reshape(groups, 2, 32, 1024), 'term', 0, 0)  13.2 us
    ppermute x8, starting transfers between devices, shift(): lax.ppermute(block, 'box', [(i, (i + distance) % count) for i in range(co...  12.9 us
    ppermute x2, waiting for transfers between devices, shift_z(): return lax.ppermute(block, ('box', 'term'), route)  12.7 us
    ppermute x8, waiting for transfers between devices, shift(): lax.ppermute(block, 'box', [(i, (i + distance) % count) for i in range(co...  8.28 us
    pallas_call x1, Pallas kernels, outer_passes(): call(outer_kernel, (jax.ShapeDtypeStruct((4, 32, 1024), BF), jax.ShapeDty...  6.58 us
    ppermute x2, starting transfers between devices, shift_z(): return lax.ppermute(block, ('box', 'term'), route)  5.75 us
    pallas_call x1, Pallas kernels, prepare(): pl.pallas_call(prepare_kernel, out_shape=tuple((jax.ShapeDtypeStruct(shap...  4.11 us
    pallas_call x1, Pallas kernels, coarse_passes(): call(coarse_kernel, (jax.ShapeDtypeStruct((32, 1024), F32), jax.ShapeDtyp...  3.62 us
  transfers between devices with their start and end apart: 10, of which 5 were waited for; matrix products, arithmetic and copies ran while one was open for 0% of the time, Pallas kernels for 19%

profile of v7, /device:TPU:30, one launch (start us, length us, event | category | flops | bytes accessed | tf_op | source)
XLA Modules:
  0.0 78.9 jit_solution(13219361175875224522)
XLA Ops:
  0.0 0.0 copy-start
  0.0 0.0 copy-start.1
  0.0 0.0 copy-start.2
  0.0 0.1 pad_add_fusion.where
  0.1 4.1 %prepare.1 = (bf16[32,1024]{1,0:T(8,128)(2,1)S(1)}, bf16[4,32,1024]{2,1,0:T(8,128)(2,1)S(1)}, bf16[4,32,1024]{2,1,0:T(8,128)(2,1)S(1)}, bf16[5,32,1024]{2,1,0:T(...) custom-call(s32[3]{0:T(128)S(1)} %pad_add_fusion.where, ...), custom_call_target="tpu_custom_call" | custom-call | tf_op jit(solution)/shard_map/prepare/pallas_call | solution.py:188
  4.2 0.1 collective-permute-start
  4.3 5.7 %collective-permute-start.1 = (bf16[5,32,1024]{2,1,0:T(8,128)(2,1)S(1)}, bf16[5,32,1024]{2,1,0:T(8,128)(2,1)S(1)}, u32[]{:S(2)}, u32[]{:S(2)}) collective-permute-start(bf16[5,32,1024]{2,1,0:T(8,128)(2,1)S(1)} %get-tuple-element.28), channel_id=1, source_target_pairs={{0,255},{1,254},{2,253},{3,252},{4,0},{5,1},{6,2},{7,3},{8,7},{9,6... | collective-permute-start | bytes 983048 | tf_op jit(solution)/shard_map/ppermute | solution.py:501
  10.0 0.2 collective-permute-start.2
  10.2 1.8 %collective-permute-start.3 = (bf16[4,32,1024]{2,1,0:T(8,128)(2,1)S(1)}, bf16[4,32,1024]{2,1,0:T(8,128)(2,1)S(1)}, u32[]{:S(2)}, u32[]{:S(2)}) collective-permute-start(bf16[4,32,1024]{2,1,0:T(8,128)(2,1)S(1)} %get-tuple-element.25.low_x), channel_id=1, source_target_pairs={{0,192},{4,196},{8,200},{12,204},{16,208},{20,212},{24,216},{28,22... | collective-permute-start | bytes 786440 | tf_op jit(solution)/shard_map/ppermute | solution.py:487
  12.0 12.6 %collective-permute-done.zm = bf16[5,32,1024]{2,1,0:T(8,128)(2,1)S(1)} collective-permute-done((bf16[5,32,1024]{2,1,0:T(8,128)(2,1)S(1)}, bf16[5,32,1024]{2,1,0:T(8,128)(2,1)S(1)}, u32[]{:S(2)}, u32[]{:S(2)}) %collective-permute-start) | collective-permute-done | bytes 327712 | tf_op jit(solution)/shard_map/ppermute | solution.py:501
  24.6 0.1 collective-permute-done.1.zp
  24.8 0.3 collective-permute-start.4
  25.1 1.9 %collective-permute-start.5 = (bf16[4,32,1024]{2,1,0:T(8,128)(2,1)S(1)}, bf16[4,32,1024]{2,1,0:T(8,128)(2,1)S(1)}, u32[]{:S(2)}, u32[]{:S(2)}) collective-permute-start(bf16[4,32,1024]{2,1,0:T(8,128)(2,1)S(1)} %pad_maximum_fusion.1), channel_id=1, source_target_pairs={{0,192},{4,196},{8,200},{12,204},{16,208},{20,212},{24,216},{28,22... | collective-permute-start | bytes 786440 | tf_op jit(solution)/shard_map/ppermute | solution.py:487
  27.0 1.5 %collective-permute-start.6 = (bf16[3,32,1024]{2,1,0:T(8,128)(2,1)S(1)}, bf16[3,32,1024]{2,1,0:T(8,128)(2,1)S(1)}, u32[]{:S(2)}, u32[]{:S(2)}) collective-permute-start(bf16[3,32,1024]{2,1,0:T(8,128)(2,1)S(1)} %pad_maximum_fusion.2), channel_id=1, source_target_pairs={{0,64},{4,68},{8,72},{12,76},{16,80},{20,84},{24,88},{28,92},{32,9... | collective-permute-start | bytes 589832 | tf_op jit(solution)/shard_map/ppermute | solution.py:487
  28.5 0.0 collective-permute-done.2.xm_own
  28.5 0.6 collective-permute-start.7
  29.1 0.0 copy-done
  29.1 0.0 copy-done.1
  29.1 0.0 copy-done.2
  29.1 3.0 %weights.1 = (bf16[8,512,256]{2,1,0:T(8,128)(2,1)S(1)}, bf16[8,64,128]{2,1,0:T(8,128)(2,1)S(1)}, bf16[2,128,256]{2,1,0:T(8,128)(2,1)S(1)}, bf16[8,384,128]{2,1,0...) custom-call(s32[8]{0:T(128)S(1)} %copy-done.2, bf16[16,3,32,32]{3,2,1,0:T(8,128)(2,1)S(1)} %copy-done, ...), custom_call_target="tpu_custom_call" | custom-call | tf_op jit(solution)/shard_map/weights/pallas_call | solution.py:104
  32.1 3.0 %shard_map.55.inner = bf16[8,16,64,256]{3,2,1,0:T(8,128)(2,1)S(1)} custom-call(bf16[4,32,1024]{2,1,0:T(8,128)(2,1)S(1)} %get-tuple-element.25.low_x, bf16[4,32,1024]{2,1,0:T(8,128)(2,1)S(1)} %get-tuple-element.26.high_x, bf16[5,32,1024]{2,1,0:T(8,128)(2,1)S(1)} %collective-permute-done.zm, bf16[5,32,1024]{2,1,0:T(8,128)(2,1)S(1)} %collective-permute-done.1.zp, ...), custom_call_target="tpu_custom_call" | custom-call | tf_op jit(solution)/shard_map/pallas_call | solution.py:235
  35.1 0.0 collective-permute-done.3.xp_own
  35.1 0.0 collective-permute-done.4.xm_far
  35.1 0.4 collective-permute-done.5.xp_far
  35.6 6.6 %shard_map.56 = (bf16[4,32,1024]{2,1,0:T(8,128)(2,1)S(1)}, bf16[4,32,1024]{2,1,0:T(8,128)(2,1)S(1)}, bf16[16,256,512]{2,1,0:T(8,128)(2,1)S(1)}) custom-call(bf16[8,16,64,256]{3,2,1,0:T(8,128)(2,1)S(1)} %shard_map.55.inner, bf16[4,32,1024]{2,1,0:T(8,128)(2,1)S(1)} %collective-permute-done.2.xm_own, bf16[4,32,1024]{2,1,0:T(8,128)(2,1)S(1)} %collective-permute-done.3.xp_own, ...), custom_call_target="tpu_custom_call" | custom-call | tf_op jit(solution)/shard_map/pallas_call | solution.py:317
  42.1 0.0 collective-permute-done.6.xm
  42.1 0.0 collective-permute-done.7.xp
  42.2 3.6 %shard_map.58 = (f32[32,1024]{1,0:T(8,128)S(1)}, bf16[5,32,1024]{2,1,0:T(8,128)(2,1)S(1)}, bf16[5,32,1024]{2,1,0:T(8,128)(2,1)S(1)}) custom-call(bf16[32,1024]{1,0:T(8,128)(2,1)S(1)} %get-tuple-element.33.par, bf16[5,32,1024]{2,1,0:T(8,128)(2,1)S(1)} %collective-permute-done.zm, bf16[5,32,1024]{2,1,0:T(8,128)(2,1)S(1)} %collective-permute-done.1.zp, ...), custom_call_target="tpu_custom_call" | custom-call | tf_op jit(solution)/shard_map/pallas_call | solution.py:433
  45.8 6.6 %collective-permute-start.8 = (bf16[5,32,1024]{2,1,0:T(8,128)(2,1)S(1)}, bf16[5,32,1024]{2,1,0:T(8,128)(2,1)S(1)}, u32[]{:S(2)}, u32[]{:S(2)}) collective-permute-start(bf16[5,32,1024]{2,1,0:T(8,128)(2,1)S(1)} %get-tuple-element.40), channel_id=1, source_target_pairs={{0,16},{4,20},{8,24},{12,28},{16,32},{20,36},{24,40},{28,44},{32,4... | collective-permute-start | bytes 983048 | tf_op jit(solution)/shard_map/ppermute | solution.py:487
  52.4 0.0 collective-permute-start.9
  52.4 2.5 %shard_map.57.own = f32[8,32,1024]{2,1,0:T(8,128)S(1)} custom-call(bf16[16,256,512]{2,1,0:T(8,128)(2,1)S(1)} %get-tuple-element.32.packed, bf16[2,128,256]{2,1,0:T(8,128)(2,1)S(1)} %get-tuple-element.31.my), custom_call_target="tpu_custom_call" | custom-call | tf_op jit(solution)/shard_map/pallas_call | solution.py:354
  54.9 2.1 %collective-permute-done.8.low = bf16[5,32,1024]{2,1,0:T(8,128)(2,1)S(1)} collective-permute-done((bf16[5,32,1024]{2,1,0:T(8,128)(2,1)S(1)}, bf16[5,32,1024]{2,1,0:T(8,128)(2,1)S(1)}, u32[]{:S(2)}, u32[]{:S(2)}) %collective-permute-start.8) | collective-permute-done | bytes 327712 | tf_op jit(solution)/shard_map/ppermute | solution.py:487
  57.0 5.8 %collective-permute-done.9.high = bf16[5,32,1024]{2,1,0:T(8,128)(2,1)S(1)} collective-permute-done((bf16[5,32,1024]{2,1,0:T(8,128)(2,1)S(1)}, bf16[5,32,1024]{2,1,0:T(8,128)(2,1)S(1)}, u32[]{:S(2)}, u32[]{:S(2)}) %collective-permute-start.9) | collective-permute-done | bytes 327712 | tf_op jit(solution)/shard_map/ppermute | solution.py:487
  62.8 1.8 %shard_map.59 = bf16[8,32,1024]{2,1,0:T(8,128)(2,1)S(1)} custom-call(f32[8,32,1024]{2,1,0:T(8,128)S(1)} %shard_map.57.own, f32[32,1024]{1,0:T(8,128)S(1)} %get-tuple-element.39.own_c, bf16[5,32,1024]{2,1,0:T(8,128)(2,1)S(1)} %collective-permute-done.8.low, bf16[5,32,1024]{2,1,0:T(8,128)(2,1)S(1)} %collective-permute-done.9.high, ...), custom_call_target="tpu_custom_call" | custom-call | tf_op jit(solution)/shard_map/pallas_call | solution.py:478
  64.6 13.2 %all_to_all.5 = bf16[4,2,32,1024]{3,2,1,0:T(8,128)(2,1)S(1)} all-to-all(bf16[4,2,32,1024]{3,2,1,0:T(8,128)(2,1)S(1)} %bitcast.5), channel_id=1, replica_groups=mesh['box'=64,'term'=4] {'term'}, dimensions={0} | all-to-all | bytes 1048576 | tf_op jit(solution)/shard_map/all_to_all | solution.py:533
  77.8 1.1 %convert_element_type.3 = f32[4,2,32,1024]{3,2,1,0:T(8,128)} convert(bf16[4,2,32,1024]{3,2,1,0:T(8,128)(2,1)S(1)} %all_to_all.5) | non-fusion elementwise | flops 262144 | bytes 1572864 | tf_op jit(solution)/shard_map/convert_element_type | solution.py:534
  (7 shorter events, 0.1 us)
Async XLA Ops:
  0.0 29.1 %copy-start = (bf16[16,3,32,32]{3,2,1,0:T(8,128)(2,1)S(1)}, bf16[16,3,32,32]{3,2,1,0:T(8,128)(2,1)}, u32[]{:S(2)}) copy-start(bf16[16,3,32,32]{3,2,1,0:T(8,128)(2,1)} %fine.1) | copy-start | bytes 294916
  0.0 29.1 %copy-start.1 = (bf16[16,3,32,32]{3,2,1,0:T(8,128)(2,1)S(1)}, bf16[16,3,32,32]{3,2,1,0:T(8,128)(2,1)}, u32[]{:S(2)}) copy-start(bf16[16,3,32,32]{3,2,1,0:T(8,128)(2,1)} %coarse.1) | copy-start | bytes 294916
  0.0 29.1 %copy-start.2 = (s32[8]{0:T(128)S(1)}, s32[8]{0:T(128)}, u32[]{:S(2)}) copy-start(s32[8]{0:T(128)} %exponents.1) | copy-start | bytes 100
  4.2 20.3 %collective-permute-start = (bf16[5,32,1024]{2,1,0:T(8,128)(2,1)S(1)}, bf16[5,32,1024]{2,1,0:T(8,128)(2,1)S(1)}, u32[]{:S(2)}, u32[]{:S(2)}) collective-permute-start(bf16[5,32,1024]{2,1,0:T(8,128)(2,1)S(1)} %get-tuple-element.27), channel_id=1, source_target_pairs={{0,4},{1,5},{2,6},{3,7},{4,11},{5,10},{6,9},{7,8},{8,12},{9,13},{1... | collective-permute-start | bytes 983048 | tf_op jit(solution)/shard_map/ppermute | solution.py:501
  4.3 20.4 %collective-permute-start.1 = (bf16[5,32,1024]{2,1,0:T(8,128)(2,1)S(1)}, bf16[5,32,1024]{2,1,0:T(8,128)(2,1)S(1)}, u32[]{:S(2)}, u32[]{:S(2)}) collective-permute-start(bf16[5,32,1024]{2,1,0:T(8,128)(2,1)S(1)} %get-tuple-element.28), channel_id=1, source_target_pairs={{0,255},{1,254},{2,253},{3,252},{4,0},{5,1},{6,2},{7,3},{8,7},{9,6... | collective-permute-start | bytes 983048 | tf_op jit(solution)/shard_map/ppermute | solution.py:501
  10.0 18.6 %collective-permute-start.2 = (bf16[4,32,1024]{2,1,0:T(8,128)(2,1)S(1)}, bf16[4,32,1024]{2,1,0:T(8,128)(2,1)S(1)}, u32[]{:S(2)}, u32[]{:S(2)}) collective-permute-start(bf16[4,32,1024]{2,1,0:T(8,128)(2,1)S(1)} %get-tuple-element.26.high_x), channel_id=1, source_target_pairs={{0,64},{4,68},{8,72},{12,76},{16,80},{20,84},{24,88},{28,92},{32,9... | collective-permute-start | bytes 786440 | tf_op jit(solution)/shard_map/ppermute | solution.py:487
  10.2 24.9 %collective-permute-start.3 = (bf16[4,32,1024]{2,1,0:T(8,128)(2,1)S(1)}, bf16[4,32,1024]{2,1,0:T(8,128)(2,1)S(1)}, u32[]{:S(2)}, u32[]{:S(2)}) collective-permute-start(bf16[4,32,1024]{2,1,0:T(8,128)(2,1)S(1)} %get-tuple-element.25.low_x), channel_id=1, source_target_pairs={{0,192},{4,196},{8,200},{12,204},{16,208},{20,212},{24,216},{28,22... | collective-permute-start | bytes 786440 | tf_op jit(solution)/shard_map/ppermute | solution.py:487
  24.8 10.4 %collective-permute-start.4 = (bf16[4,32,1024]{2,1,0:T(8,128)(2,1)S(1)}, bf16[4,32,1024]{2,1,0:T(8,128)(2,1)S(1)}, u32[]{:S(2)}, u32[]{:S(2)}) collective-permute-start(bf16[4,32,1024]{2,1,0:T(8,128)(2,1)S(1)} %pad_maximum_fusion), channel_id=1, source_target_pairs={{0,64},{4,68},{8,72},{12,76},{16,80},{20,84},{24,88},{28,92},{32,9... | collective-permute-start | bytes 786440 | tf_op jit(solution)/shard_map/ppermute | solution.py:487
  25.1 10.5 %collective-permute-start.5 = (bf16[4,32,1024]{2,1,0:T(8,128)(2,1)S(1)}, bf16[4,32,1024]{2,1,0:T(8,128)(2,1)S(1)}, u32[]{:S(2)}, u32[]{:S(2)}) collective-permute-start(bf16[4,32,1024]{2,1,0:T(8,128)(2,1)S(1)} %pad_maximum_fusion.1), channel_id=1, source_target_pairs={{0,192},{4,196},{8,200},{12,204},{16,208},{20,212},{24,216},{28,22... | collective-permute-start | bytes 786440 | tf_op jit(solution)/shard_map/ppermute | solution.py:487
  27.0 15.1 %collective-permute-start.6 = (bf16[3,32,1024]{2,1,0:T(8,128)(2,1)S(1)}, bf16[3,32,1024]{2,1,0:T(8,128)(2,1)S(1)}, u32[]{:S(2)}, u32[]{:S(2)}) collective-permute-start(bf16[3,32,1024]{2,1,0:T(8,128)(2,1)S(1)} %pad_maximum_fusion.2), channel_id=1, source_target_pairs={{0,64},{4,68},{8,72},{12,76},{16,80},{20,84},{24,88},{28,92},{32,9... | collective-permute-start | bytes 589832 | tf_op jit(solution)/shard_map/ppermute | solution.py:487
  28.5 13.6 %collective-permute-start.7 = (bf16[3,32,1024]{2,1,0:T(8,128)(2,1)S(1)}, bf16[3,32,1024]{2,1,0:T(8,128)(2,1)S(1)}, u32[]{:S(2)}, u32[]{:S(2)}) collective-permute-start(bf16[3,32,1024]{2,1,0:T(8,128)(2,1)S(1)} %pad_maximum_fusion.2), channel_id=1, source_target_pairs={{0,192},{4,196},{8,200},{12,204},{16,208},{20,212},{24,216},{28,22... | collective-permute-start | bytes 589832 | tf_op jit(solution)/shard_map/ppermute | solution.py:487
  45.8 11.2 %collective-permute-start.8 = (bf16[5,32,1024]{2,1,0:T(8,128)(2,1)S(1)}, bf16[5,32,1024]{2,1,0:T(8,128)(2,1)S(1)}, u32[]{:S(2)}, u32[]{:S(2)}) collective-permute-start(bf16[5,32,1024]{2,1,0:T(8,128)(2,1)S(1)} %get-tuple-element.40), channel_id=1, source_target_pairs={{0,16},{4,20},{8,24},{12,28},{16,32},{20,36},{24,40},{28,44},{32,4... | collective-permute-start | bytes 983048 | tf_op jit(solution)/shard_map/ppermute | solution.py:487
  52.4 10.4 %collective-permute-start.9 = (bf16[5,32,1024]{2,1,0:T(8,128)(2,1)S(1)}, bf16[5,32,1024]{2,1,0:T(8,128)(2,1)S(1)}, u32[]{:S(2)}, u32[]{:S(2)}) collective-permute-start(bf16[5,32,1024]{2,1,0:T(8,128)(2,1)S(1)} %get-tuple-element.41), channel_id=1, source_target_pairs={{0,240},{4,244},{8,248},{12,252},{16,0},{20,4},{24,8},{28,12},{32,... | collective-permute-start | bytes 983048 | tf_op jit(solution)/shard_map/ppermute | solution.py:487

commit v8 on v7

--- a/solution.py
+++ b/solution.py
@@ -126,8 +126,16 @@
     )(exponents, fine, coarse)
 
 
-def prepare_kernel(where, mine, other, s, out, low_x, high_x, up, dn, fz, ky, st2, rows, wide):
-    scale = s[...]
+def prepare_kernel(where, boxes_in, s, out, low_x, high_x, up, dn, fz, ky, st2, rows, wide, mine, other, filters, arrived):
+    copies = [
+        pltpu.make_async_copy(boxes_in.at[where[k]], target, arrived.at[k]) for k, target in enumerate((mine, other))
+    ]
+    for copy in copies:
+        copy.start()
+    first = pltpu.make_async_copy(s, filters, arrived.at[2])
+    first.start()
+    first.wait()
+    scale = filters[...]
     tiled = lax.dot_general(
         scale, same(32, 128, lambda i, j: j % 32 == i), (((0,), (0,)), ((), ())), preferred_element_type=F32
     )
@@ -146,6 +154,8 @@
         line = jnp.broadcast_to(spread[y : y + 1], (16, 1024)).astype(BF)
         ky[y * 32 : y * 32 + 16, :] = line * mask[:16]
         ky[y * 32 + 16 : y * 32 + 32, :] = line * mask[16:]
+    for copy in copies:
+        copy.wait()
     for yg in range(16):
         cy, g = divmod(yg, 8)
         for k, boxes in enumerate((mine, other)):
@@ -153,7 +163,7 @@
                 for cz in range(2):
                     row = yg * 128 + k * 64 + cx * 32
                     rows[row : row + 32, cz * 128 : cz * 128 + 128] = boxes[
-                        0, 4 * cx + 2 * cy + cz, :, g * 128 : g * 128 + 128
+                        4 * cx + 2 * cy + cz, :, g * 128 : g * 128 + 128
                     ]
     along_z = dot(rows[...], fz[...]).astype(BF)
     for yg in range(16):
@@ -161,13 +171,13 @@
     along_y = dot(wide[...], ky[...]).astype(BF)
     parents = [dot(scale, along_y[k * 64 : k * 64 + 64]).astype(BF) for k in range(2)]
     out[...] = parents[0]
-    low_x[...] = mine[0, :4]
-    high_x[...] = mine[0, 4:]
+    low_x[...] = mine[:4]
+    high_x[...] = mine[4:]
 
     def fill(first, second):
         for i in range(4):
-            up[i] = (mine, other)[first][0, 2 * i + 1]
-            dn[i] = (mine, other)[second][0, 2 * i]
+            up[i] = (mine, other)[first][2 * i + 1]
+            dn[i] = (mine, other)[second][2 * i]
         up[4] = parents[first]
         dn[4] = parents[second]
 
@@ -181,28 +191,27 @@
 
 
 def prepare(where, fine_coeffs, s):
-    def whole(*shape):
-        return pl.BlockSpec(shape, lambda i, w: (0,) * len(shape))
-
     shapes = [(32, 1024), (4, 32, 1024), (4, 32, 1024), (5, 32, 1024), (5, 32, 1024), (256, 128), (2048, 1024), (64, 64)]
     return pl.pallas_call(
         prepare_kernel,
         out_shape=tuple(jax.ShapeDtypeStruct(shape, BF) for shape in shapes),
-        grid_spec=pltpu.PrefetchScalarGridSpec(
-            num_scalar_prefetch=1,
-            grid=(1,),
-            in_specs=[
-                pl.BlockSpec((1, 8, 32, 1024), lambda i, w: (w[0], 0, 0, 0)),
-                pl.BlockSpec((1, 8, 32, 1024), lambda i, w: (w[1], 0, 0, 0)),
-                whole(32, 64),
-            ],
-            out_specs=[whole(*shape) for shape in shapes],
-            scratch_shapes=[pltpu.VMEM((2048, 256), BF), pltpu.VMEM((128, 2048), BF)],
-        ),
+        in_specs=[
+            pl.BlockSpec(memory_space=pltpu.SMEM),
+            pl.BlockSpec(memory_space=pl.ANY),
+            pl.BlockSpec(memory_space=pl.ANY),
+        ],
+        scratch_shapes=[
+            pltpu.VMEM((2048, 256), BF),
+            pltpu.VMEM((128, 2048), BF),
+            pltpu.VMEM((8, 32, 1024), BF),
+            pltpu.VMEM((8, 32, 1024), BF),
+            pltpu.VMEM((32, 64), BF),
+            pltpu.SemaphoreType.DMA((3,)),
+        ],
         interpret=INTERPRET,
         name="prepare",
         **grant(24),
-    )(where, fine_coeffs, fine_coeffs, s)
+    )(where, fine_coeffs, s)
 
 
 PITCH_U = 68

time: 79 us -> 79 us (level)
  no operation moved by 1% of the time
where the time goes in v8:
time: 79 us; the launch traced here: 78.8 us
  Pallas kernels  24.5 us (31%)
  waiting for transfers between devices  21 us (27%)
  starting transfers between devices  18.7 us (24%)
  blocking collectives  13.2 us (17%)
  other arithmetic  1.24 us (2%)
    all_to_all x1, blocking collectives, steps(): mine = lax.all_to_all(total.reshape(groups, 2, 32, 1024), 'term', 0, 0)  13.2 us
    ppermute x8, starting transfers between devices, shift(): lax.ppermute(block, 'box', [(i, (i + distance) % count) for i in range(co...  12.9 us
    ppermute x2, waiting for transfers between devices, shift_z(): return lax.ppermute(block, ('box', 'term'), route)  12.7 us
    ppermute x8, waiting for transfers between devices, shift(): lax.ppermute(block, 'box', [(i, (i + distance) % count) for i in range(co...  8.29 us
    pallas_call x1, Pallas kernels, outer_passes(): call(outer_kernel, (jax.ShapeDtypeStruct((4, 32, 1024), BF), jax.ShapeDty...  6.6 us
    ppermute x2, starting transfers between devices, shift_z(): return lax.ppermute(block, ('box', 'term'), route)  5.75 us
    pallas_call x1, Pallas kernels, prepare(): pl.pallas_call(prepare_kernel, out_shape=tuple((jax.ShapeDtypeStruct(shap...  4.02 us
    pallas_call x1, Pallas kernels, coarse_passes(): call(coarse_kernel, (jax.ShapeDtypeStruct((32, 1024), F32), jax.ShapeDtyp...  3.62 us
  transfers between devices with their start and end apart: 10, of which 5 were waited for; matrix products, arithmetic and copies ran while one was open for 0% of the time, Pallas kernels for 19%

profile of v8, /device:TPU:30, one launch (start us, length us, event | category | flops | bytes accessed | tf_op | source)
XLA Modules:
  0.0 78.8 jit_solution(12637853027936958862)
XLA Ops:
  0.0 0.0 copy-start
  0.0 0.0 copy-start.1
  0.0 0.0 copy-start.2
  0.0 0.1 pad_add_fusion.where
  0.1 4.0 %prepare.1 = (bf16[32,1024]{1,0:T(8,128)(2,1)S(1)}, bf16[4,32,1024]{2,1,0:T(8,128)(2,1)S(1)}, bf16[4,32,1024]{2,1,0:T(8,128)(2,1)S(1)}, bf16[5,32,1024]{2,1,0:T(...) custom-call(s32[3]{0:T(128)S(1)} %pad_add_fusion.where, ...), custom_call_target="tpu_custom_call" | custom-call | tf_op jit(solution)/shard_map/prepare/pallas_call | solution.py:195
  4.1 0.1 collective-permute-start
  4.2 5.7 %collective-permute-start.1 = (bf16[5,32,1024]{2,1,0:T(8,128)(2,1)S(1)}, bf16[5,32,1024]{2,1,0:T(8,128)(2,1)S(1)}, u32[]{:S(2)}, u32[]{:S(2)}) collective-permute-start(bf16[5,32,1024]{2,1,0:T(8,128)(2,1)S(1)} %get-tuple-element.28), channel_id=1, source_target_pairs={{0,255},{1,254},{2,253},{3,252},{4,0},{5,1},{6,2},{7,3},{8,7},{9,6... | collective-permute-start | bytes 983048 | tf_op jit(solution)/shard_map/ppermute | solution.py:510
  9.9 0.2 collective-permute-start.2
  10.1 1.8 %collective-permute-start.3 = (bf16[4,32,1024]{2,1,0:T(8,128)(2,1)S(1)}, bf16[4,32,1024]{2,1,0:T(8,128)(2,1)S(1)}, u32[]{:S(2)}, u32[]{:S(2)}) collective-permute-start(bf16[4,32,1024]{2,1,0:T(8,128)(2,1)S(1)} %get-tuple-element.25.low_x), channel_id=1, source_target_pairs={{0,192},{4,196},{8,200},{12,204},{16,208},{20,212},{24,216},{28,22... | collective-permute-start | bytes 786440 | tf_op jit(solution)/shard_map/ppermute | solution.py:496
  11.9 12.6 %collective-permute-done.zm = bf16[5,32,1024]{2,1,0:T(8,128)(2,1)S(1)} collective-permute-done((bf16[5,32,1024]{2,1,0:T(8,128)(2,1)S(1)}, bf16[5,32,1024]{2,1,0:T(8,128)(2,1)S(1)}, u32[]{:S(2)}, u32[]{:S(2)}) %collective-permute-start) | collective-permute-done | bytes 327712 | tf_op jit(solution)/shard_map/ppermute | solution.py:510
  24.5 0.1 collective-permute-done.1.zp
  24.7 0.3 collective-permute-start.4
  25.0 1.9 %collective-permute-start.5 = (bf16[4,32,1024]{2,1,0:T(8,128)(2,1)S(1)}, bf16[4,32,1024]{2,1,0:T(8,128)(2,1)S(1)}, u32[]{:S(2)}, u32[]{:S(2)}) collective-permute-start(bf16[4,32,1024]{2,1,0:T(8,128)(2,1)S(1)} %pad_maximum_fusion.1), channel_id=1, source_target_pairs={{0,192},{4,196},{8,200},{12,204},{16,208},{20,212},{24,216},{28,22... | collective-permute-start | bytes 786440 | tf_op jit(solution)/shard_map/ppermute | solution.py:496
  26.9 1.5 %collective-permute-start.6 = (bf16[3,32,1024]{2,1,0:T(8,128)(2,1)S(1)}, bf16[3,32,1024]{2,1,0:T(8,128)(2,1)S(1)}, u32[]{:S(2)}, u32[]{:S(2)}) collective-permute-start(bf16[3,32,1024]{2,1,0:T(8,128)(2,1)S(1)} %pad_maximum_fusion.2), channel_id=1, source_target_pairs={{0,64},{4,68},{8,72},{12,76},{16,80},{20,84},{24,88},{28,92},{32,9... | collective-permute-start | bytes 589832 | tf_op jit(solution)/shard_map/ppermute | solution.py:496
  28.4 0.0 collective-permute-done.2.xm_own
  28.4 0.6 collective-permute-start.7
  29.0 0.0 copy-done
  29.0 0.0 copy-done.1
  29.0 0.0 copy-done.2
  29.0 3.0 %weights.1 = (bf16[8,512,256]{2,1,0:T(8,128)(2,1)S(1)}, bf16[8,64,128]{2,1,0:T(8,128)(2,1)S(1)}, bf16[2,128,256]{2,1,0:T(8,128)(2,1)S(1)}, bf16[8,384,128]{2,1,0...) custom-call(s32[8]{0:T(128)S(1)} %copy-done.2, bf16[16,3,32,32]{3,2,1,0:T(8,128)(2,1)S(1)} %copy-done, ...), custom_call_target="tpu_custom_call" | custom-call | tf_op jit(solution)/shard_map/weights/pallas_call | solution.py:104
  32.0 3.0 %shard_map.55.inner = bf16[8,16,64,256]{3,2,1,0:T(8,128)(2,1)S(1)} custom-call(bf16[4,32,1024]{2,1,0:T(8,128)(2,1)S(1)} %get-tuple-element.25.low_x, bf16[4,32,1024]{2,1,0:T(8,128)(2,1)S(1)} %get-tuple-element.26.high_x, bf16[5,32,1024]{2,1,0:T(8,128)(2,1)S(1)} %collective-permute-done.zm, bf16[5,32,1024]{2,1,0:T(8,128)(2,1)S(1)} %collective-permute-done.1.zp, ...), custom_call_target="tpu_custom_call" | custom-call | tf_op jit(solution)/shard_map/pallas_call | solution.py:244
  35.0 0.0 collective-permute-done.3.xp_own
  35.0 0.0 collective-permute-done.4.xm_far
  35.1 0.4 collective-permute-done.5.xp_far
  35.5 6.6 %shard_map.56 = (bf16[4,32,1024]{2,1,0:T(8,128)(2,1)S(1)}, bf16[4,32,1024]{2,1,0:T(8,128)(2,1)S(1)}, bf16[16,256,512]{2,1,0:T(8,128)(2,1)S(1)}) custom-call(bf16[8,16,64,256]{3,2,1,0:T(8,128)(2,1)S(1)} %shard_map.55.inner, bf16[4,32,1024]{2,1,0:T(8,128)(2,1)S(1)} %collective-permute-done.2.xm_own, bf16[4,32,1024]{2,1,0:T(8,128)(2,1)S(1)} %collective-permute-done.3.xp_own, ...), custom_call_target="tpu_custom_call" | custom-call | tf_op jit(solution)/shard_map/pallas_call | solution.py:326
  42.1 0.0 collective-permute-done.6.xm
  42.1 0.0 collective-permute-done.7.xp
  42.1 3.6 %shard_map.58 = (f32[32,1024]{1,0:T(8,128)S(1)}, bf16[5,32,1024]{2,1,0:T(8,128)(2,1)S(1)}, bf16[5,32,1024]{2,1,0:T(8,128)(2,1)S(1)}) custom-call(bf16[32,1024]{1,0:T(8,128)(2,1)S(1)} %get-tuple-element.33.par, bf16[5,32,1024]{2,1,0:T(8,128)(2,1)S(1)} %collective-permute-done.zm, bf16[5,32,1024]{2,1,0:T(8,128)(2,1)S(1)} %collective-permute-done.1.zp, ...), custom_call_target="tpu_custom_call" | custom-call | tf_op jit(solution)/shard_map/pallas_call | solution.py:442
  45.7 6.6 %collective-permute-start.8 = (bf16[5,32,1024]{2,1,0:T(8,128)(2,1)S(1)}, bf16[5,32,1024]{2,1,0:T(8,128)(2,1)S(1)}, u32[]{:S(2)}, u32[]{:S(2)}) collective-permute-start(bf16[5,32,1024]{2,1,0:T(8,128)(2,1)S(1)} %get-tuple-element.40), channel_id=1, source_target_pairs={{0,16},{4,20},{8,24},{12,28},{16,32},{20,36},{24,40},{28,44},{32,4... | collective-permute-start | bytes 983048 | tf_op jit(solution)/shard_map/ppermute | solution.py:496
  52.3 0.0 collective-permute-start.9
  52.3 2.5 %shard_map.57.own = f32[8,32,1024]{2,1,0:T(8,128)S(1)} custom-call(bf16[16,256,512]{2,1,0:T(8,128)(2,1)S(1)} %get-tuple-element.32.packed, bf16[2,128,256]{2,1,0:T(8,128)(2,1)S(1)} %get-tuple-element.31.my), custom_call_target="tpu_custom_call" | custom-call | tf_op jit(solution)/shard_map/pallas_call | solution.py:363
  54.8 2.1 %collective-permute-done.8.low = bf16[5,32,1024]{2,1,0:T(8,128)(2,1)S(1)} collective-permute-done((bf16[5,32,1024]{2,1,0:T(8,128)(2,1)S(1)}, bf16[5,32,1024]{2,1,0:T(8,128)(2,1)S(1)}, u32[]{:S(2)}, u32[]{:S(2)}) %collective-permute-start.8) | collective-permute-done | bytes 327712 | tf_op jit(solution)/shard_map/ppermute | solution.py:496
  56.9 5.8 %collective-permute-done.9.high = bf16[5,32,1024]{2,1,0:T(8,128)(2,1)S(1)} collective-permute-done((bf16[5,32,1024]{2,1,0:T(8,128)(2,1)S(1)}, bf16[5,32,1024]{2,1,0:T(8,128)(2,1)S(1)}, u32[]{:S(2)}, u32[]{:S(2)}) %collective-permute-start.9) | collective-permute-done | bytes 327712 | tf_op jit(solution)/shard_map/ppermute | solution.py:496
  62.7 1.8 %shard_map.59 = bf16[8,32,1024]{2,1,0:T(8,128)(2,1)S(1)} custom-call(f32[8,32,1024]{2,1,0:T(8,128)S(1)} %shard_map.57.own, f32[32,1024]{1,0:T(8,128)S(1)} %get-tuple-element.39.own_c, bf16[5,32,1024]{2,1,0:T(8,128)(2,1)S(1)} %collective-permute-done.8.low, bf16[5,32,1024]{2,1,0:T(8,128)(2,1)S(1)} %collective-permute-done.9.high, ...), custom_call_target="tpu_custom_call" | custom-call | tf_op jit(solution)/shard_map/pallas_call | solution.py:487
  64.5 13.2 %all_to_all.5 = bf16[4,2,32,1024]{3,2,1,0:T(8,128)(2,1)S(1)} all-to-all(bf16[4,2,32,1024]{3,2,1,0:T(8,128)(2,1)S(1)} %bitcast.5), channel_id=1, replica_groups=mesh['box'=64,'term'=4] {'term'}, dimensions={0} | all-to-all | bytes 1048576 | tf_op jit(solution)/shard_map/all_to_all | solution.py:542
  77.7 1.1 %convert_element_type.3 = f32[4,2,32,1024]{3,2,1,0:T(8,128)} convert(bf16[4,2,32,1024]{3,2,1,0:T(8,128)(2,1)S(1)} %all_to_all.5) | non-fusion elementwise | flops 262144 | bytes 1572864 | tf_op jit(solution)/shard_map/convert_element_type | solution.py:543
  (7 shorter events, 0.1 us)
Async XLA Ops:
  0.0 29.0 %copy-start = (bf16[16,3,32,32]{3,2,1,0:T(8,128)(2,1)S(1)}, bf16[16,3,32,32]{3,2,1,0:T(8,128)(2,1)}, u32[]{:S(2)}) copy-start(bf16[16,3,32,32]{3,2,1,0:T(8,128)(2,1)} %fine.1) | copy-start | bytes 294916
  0.0 29.0 %copy-start.1 = (bf16[16,3,32,32]{3,2,1,0:T(8,128)(2,1)S(1)}, bf16[16,3,32,32]{3,2,1,0:T(8,128)(2,1)}, u32[]{:S(2)}) copy-start(bf16[16,3,32,32]{3,2,1,0:T(8,128)(2,1)} %coarse.1) | copy-start | bytes 294916
  0.0 29.0 %copy-start.2 = (s32[8]{0:T(128)S(1)}, s32[8]{0:T(128)}, u32[]{:S(2)}) copy-start(s32[8]{0:T(128)} %exponents.1) | copy-start | bytes 100
  4.1 20.4 %collective-permute-start = (bf16[5,32,1024]{2,1,0:T(8,128)(2,1)S(1)}, bf16[5,32,1024]{2,1,0:T(8,128)(2,1)S(1)}, u32[]{:S(2)}, u32[]{:S(2)}) collective-permute-start(bf16[5,32,1024]{2,1,0:T(8,128)(2,1)S(1)} %get-tuple-element.27), channel_id=1, source_target_pairs={{0,4},{1,5},{2,6},{3,7},{4,11},{5,10},{6,9},{7,8},{8,12},{9,13},{1... | collective-permute-start | bytes 983048 | tf_op jit(solution)/shard_map/ppermute | solution.py:510
  4.2 20.4 %collective-permute-start.1 = (bf16[5,32,1024]{2,1,0:T(8,128)(2,1)S(1)}, bf16[5,32,1024]{2,1,0:T(8,128)(2,1)S(1)}, u32[]{:S(2)}, u32[]{:S(2)}) collective-permute-start(bf16[5,32,1024]{2,1,0:T(8,128)(2,1)S(1)} %get-tuple-element.28), channel_id=1, source_target_pairs={{0,255},{1,254},{2,253},{3,252},{4,0},{5,1},{6,2},{7,3},{8,7},{9,6... | collective-permute-start | bytes 983048 | tf_op jit(solution)/shard_map/ppermute | solution.py:510
  9.9 18.5 %collective-permute-start.2 = (bf16[4,32,1024]{2,1,0:T(8,128)(2,1)S(1)}, bf16[4,32,1024]{2,1,0:T(8,128)(2,1)S(1)}, u32[]{:S(2)}, u32[]{:S(2)}) collective-permute-start(bf16[4,32,1024]{2,1,0:T(8,128)(2,1)S(1)} %get-tuple-element.26.high_x), channel_id=1, source_target_pairs={{0,64},{4,68},{8,72},{12,76},{16,80},{20,84},{24,88},{28,92},{32,9... | collective-permute-start | bytes 786440 | tf_op jit(solution)/shard_map/ppermute | solution.py:496
  10.1 24.9 %collective-permute-start.3 = (bf16[4,32,1024]{2,1,0:T(8,128)(2,1)S(1)}, bf16[4,32,1024]{2,1,0:T(8,128)(2,1)S(1)}, u32[]{:S(2)}, u32[]{:S(2)}) collective-permute-start(bf16[4,32,1024]{2,1,0:T(8,128)(2,1)S(1)} %get-tuple-element.25.low_x), channel_id=1, source_target_pairs={{0,192},{4,196},{8,200},{12,204},{16,208},{20,212},{24,216},{28,22... | collective-permute-start | bytes 786440 | tf_op jit(solution)/shard_map/ppermute | solution.py:496
  24.7 10.4 %collective-permute-start.4 = (bf16[4,32,1024]{2,1,0:T(8,128)(2,1)S(1)}, bf16[4,32,1024]{2,1,0:T(8,128)(2,1)S(1)}, u32[]{:S(2)}, u32[]{:S(2)}) collective-permute-start(bf16[4,32,1024]{2,1,0:T(8,128)(2,1)S(1)} %pad_maximum_fusion), channel_id=1, source_target_pairs={{0,64},{4,68},{8,72},{12,76},{16,80},{20,84},{24,88},{28,92},{32,9... | collective-permute-start | bytes 786440 | tf_op jit(solution)/shard_map/ppermute | solution.py:496
  25.0 10.5 %collective-permute-start.5 = (bf16[4,32,1024]{2,1,0:T(8,128)(2,1)S(1)}, bf16[4,32,1024]{2,1,0:T(8,128)(2,1)S(1)}, u32[]{:S(2)}, u32[]{:S(2)}) collective-permute-start(bf16[4,32,1024]{2,1,0:T(8,128)(2,1)S(1)} %pad_maximum_fusion.1), channel_id=1, source_target_pairs={{0,192},{4,196},{8,200},{12,204},{16,208},{20,212},{24,216},{28,22... | collective-permute-start | bytes 786440 | tf_op jit(solution)/shard_map/ppermute | solution.py:496
  26.9 15.2 %collective-permute-start.6 = (bf16[3,32,1024]{2,1,0:T(8,128)(2,1)S(1)}, bf16[3,32,1024]{2,1,0:T(8,128)(2,1)S(1)}, u32[]{:S(2)}, u32[]{:S(2)}) collective-permute-start(bf16[3,32,1024]{2,1,0:T(8,128)(2,1)S(1)} %pad_maximum_fusion.2), channel_id=1, source_target_pairs={{0,64},{4,68},{8,72},{12,76},{16,80},{20,84},{24,88},{28,92},{32,9... | collective-permute-start | bytes 589832 | tf_op jit(solution)/shard_map/ppermute | solution.py:496
  28.4 13.7 %collective-permute-start.7 = (bf16[3,32,1024]{2,1,0:T(8,128)(2,1)S(1)}, bf16[3,32,1024]{2,1,0:T(8,128)(2,1)S(1)}, u32[]{:S(2)}, u32[]{:S(2)}) collective-permute-start(bf16[3,32,1024]{2,1,0:T(8,128)(2,1)S(1)} %pad_maximum_fusion.2), channel_id=1, source_target_pairs={{0,192},{4,196},{8,200},{12,204},{16,208},{20,212},{24,216},{28,22... | collective-permute-start | bytes 589832 | tf_op jit(solution)/shard_map/ppermute | solution.py:496
  45.7 11.2 %collective-permute-start.8 = (bf16[5,32,1024]{2,1,0:T(8,128)(2,1)S(1)}, bf16[5,32,1024]{2,1,0:T(8,128)(2,1)S(1)}, u32[]{:S(2)}, u32[]{:S(2)}) collective-permute-start(bf16[5,32,1024]{2,1,0:T(8,128)(2,1)S(1)} %get-tuple-element.40), channel_id=1, source_target_pairs={{0,16},{4,20},{8,24},{12,28},{16,32},{20,36},{24,40},{28,44},{32,4... | collective-permute-start | bytes 983048 | tf_op jit(solution)/shard_map/ppermute | solution.py:496
  52.3 10.4 %collective-permute-start.9 = (bf16[5,32,1024]{2,1,0:T(8,128)(2,1)S(1)}, bf16[5,32,1024]{2,1,0:T(8,128)(2,1)S(1)}, u32[]{:S(2)}, u32[]{:S(2)}) collective-permute-start(bf16[5,32,1024]{2,1,0:T(8,128)(2,1)S(1)} %get-tuple-element.41), channel_id=1, source_target_pairs={{0,240},{4,244},{8,248},{12,252},{16,0},{20,4},{24,8},{28,12},{32,... | collective-permute-start | bytes 983048 | tf_op jit(solution)/shard_map/ppermute | solution.py:496

commit v9 on v8

--- a/solution.py
+++ b/solution.py
@@ -216,7 +216,6 @@
 
 PITCH_U = 68
 PITCH_CU = 36
-PITCH_CV = 100
 
 
 def fill_left(left, sources, row):
@@ -340,7 +339,21 @@
     )(*operands)
 
 
-def own_kernel(packed, my, out, done):
+def own_kernel(packed, my, packed_c, my_c, out, out_c, done, done_c):
+    inner = jnp.concatenate([my_c[j * 96 + 32 : j * 96 + 64, :] for j in range(4)], axis=0)
+
+    def rows_c(k):
+        fold_four(dot(inner, packed_c[k]), done_c, pl.multiple_of(k * (4 * PITCH_CU), 8), PITCH_CU, 32)
+
+    repeat(8, 4, rows_c)
+
+    lane_c = lax.broadcasted_iota(jnp.int32, (32, 128), 1) // 32
+
+    def relay_c(g):
+        out_c[:, pl.ds(pl.multiple_of(g * 128, 128), 128)] = gather_four(done_c, 4 * g, PITCH_CU, lane_c)
+
+    repeat(8, 8, relay_c)
+
     def rows(k):
         fold_rows(dot(my[1], packed[k]), done, pl.multiple_of(k * (4 * PITCH_U), 8), PITCH_U)
 
@@ -360,12 +373,33 @@
 
 
 def own_rows(*operands):
-    return call(own_kernel, jax.ShapeDtypeStruct((8, 32, 1024), F32), [pltpu.VMEM((64 * PITCH_U, 128), F32)])(*operands)
+    return call(
+        own_kernel,
+        (jax.ShapeDtypeStruct((8, 32, 1024), F32), jax.ShapeDtypeStruct((32, 1024), F32)),
+        [pltpu.VMEM((64 * PITCH_U, 128), F32), pltpu.VMEM((32 * PITCH_CU, 128), F32)],
+    )(*operands)
+
+
+def fold_four(passed, done, start, pitch, height):
+    for i in range(4):
+        lanes = passed[:, i * 128 : i * 128 + 128]
+        total = lanes[:height]
+        for j in range(1, 4):
+            total = total + pltpu.roll(lanes[j * height : j * height + height], 128 - 32 * j, 1)
+        done[pl.ds(start + i * pitch, height), :] = total
+
+
+def gather_four(done, first, pitch, lane):
+    block = done[pl.ds(first, 32, stride=pitch), :]
+    for j in range(1, 4):
+        part = done[pl.ds(first + j, 32, stride=pitch), :]
+        block = jnp.where(lane == j, pltpu.roll(part, 32 * j, 1), block)
+    return block
 
 
 def coarse_kernel(
     par, zm, zp, xm, xp, wz, wx, my, fine_up, fine_dn,
-    out, send_up, send_dn,
+    send_up, send_dn, packed,
     left, mid_a, mid_b, wide, done,
 ):
     send_up[:4] = fine_up[...]
@@ -404,18 +438,16 @@
             along_z(h + 1, mids[(h + 1) % 2])
         along_x(h, mids[h % 2])
 
+    outer = jnp.concatenate(
+        [my[j * 96 + vb * 32 : j * 96 + vb * 32 + 32, :] for j in range(4) for vb in (0, 2)], axis=0
+    )
+
     def rows(k):
         data = jnp.concatenate(
             [wide[pl.ds(4 * k + i, 64, stride=PITCH_CU), :].astype(BF) for i in range(4)], axis=1
         )
-        passed = dot(my[...], data)
-        start = pl.multiple_of(k * (4 * PITCH_CV), 8)
-        for i in range(4):
-            lanes = passed[:, i * 128 : i * 128 + 128]
-            total = lanes[:96]
-            for j in range(1, 4):
-                total = total + pltpu.roll(lanes[j * 96 : j * 96 + 96], 128 - 32 * j, 1)
-            done[pl.ds(start + i * PITCH_CV, 96), :] = total
+        packed[k] = data
+        fold_four(dot(outer, data), done, pl.multiple_of(k * (4 * PITCH_U), 8), PITCH_U, 64)
 
     repeat(8, 4, rows)
 
@@ -423,17 +455,8 @@
 
     def relay(g):
         at = pl.multiple_of(g * 128, 128)
-        for vb in range(3):
-            block = done[pl.ds(vb * 32 + 4 * g, 32, stride=PITCH_CV), :]
-            for j in range(1, 4):
-                part = done[pl.ds(vb * 32 + 4 * g + j, 32, stride=PITCH_CV), :]
-                block = jnp.where(lane == j, pltpu.roll(part, 32 * j, 1), block)
-            if vb == 0:
-                send_dn[4, :, pl.ds(at, 128)] = block.astype(BF)
-            elif vb == 2:
-                send_up[4, :, pl.ds(at, 128)] = block.astype(BF)
-            else:
-                out[:, pl.ds(at, 128)] = block
+        for side, target in enumerate((send_dn, send_up)):
+            target[4, :, pl.ds(at, 128)] = gather_four(done, side * 32 + 4 * g, PITCH_U, lane).astype(BF)
 
     repeat(8, 8, relay)
 
@@ -442,16 +465,16 @@
     return call(
         coarse_kernel,
         (
-            jax.ShapeDtypeStruct((32, 1024), F32),
             jax.ShapeDtypeStruct((5, 32, 1024), BF),
             jax.ShapeDtypeStruct((5, 32, 1024), BF),
+            jax.ShapeDtypeStruct((8, 64, 512), BF),
         ),
         [
             pltpu.VMEM((768, 384), BF),
             pltpu.VMEM((8, 96, 256), BF),
             pltpu.VMEM((8, 96, 256), BF),
             pltpu.VMEM((64 * PITCH_CU, 128), F32),
-            pltpu.VMEM((32 * PITCH_CV, 128), F32),
+            pltpu.VMEM((32 * PITCH_U, 128), F32),
         ],
     )(*operands)
 
@@ -533,10 +556,10 @@
     cxp = shift(planes, -16)
 
     send_up, send_dn, packed = outer_passes(mid, xm_own, xp_own, xm_far, xp_far, wz, wx, my)
-    out_c, full_up, full_dn = coarse_passes(par, zm, zp, cxm, cxp, cwz, cwx, cmy, send_up, send_dn)
+    full_up, full_dn, packed_c = coarse_passes(par, zm, zp, cxm, cxp, cwz, cwx, cmy, send_up, send_dn)
     low = shift(full_up, 4)
     high = shift(full_dn, -4)
-    out = own_rows(packed, my)
+    out, out_c = own_rows(packed, my, packed_c, cmy)
     total = finish(out, out_c, low, high, fz, ky, st2)
     groups = lax.axis_size("term")
     mine = lax.all_to_all(total.reshape(groups, 2, 32, 1024), "term", 0, 0)

time: 79 us -> 78.5 us (level)
  waiting for transfers between devices: 21 us -> 19.9 us
    ppermute x8, waiting for transfers between devices: 8.29 us -> 7.27 us  [shift(): lax.ppermute(block, 'box', [(i, (i + distance) % count) for i in range(co...]
  transfers between devices with their start and end apart: 10 -> 10, of which waited for: 5 -> 5; matrix products, arithmetic and copies ran while one was open for 0% -> 0% of each run, Pallas kernels for 19% -> 21%
where the time goes in v9:
time: 78.5 us; the launch traced here: 78.3 us
  Pallas kernels  25 us (32%)
  waiting for transfers between devices  19.9 us (25%)
  starting transfers between devices  18.7 us (24%)
  blocking collectives  13.2 us (17%)
  other arithmetic  1.24 us (2%)
    all_to_all x1, blocking collectives, steps(): mine = lax.all_to_all(total.reshape(groups, 2, 32, 1024), 'term', 0, 0)  13.2 us
    ppermute x8, starting transfers between devices, shift(): lax.ppermute(block, 'box', [(i, (i + distance) % count) for i in range(co...  12.9 us
    ppermute x2, waiting for transfers between devices, shift_z(): return lax.ppermute(block, ('box', 'term'), route)  12.7 us
    ppermute x8, waiting for transfers between devices, shift(): lax.ppermute(block, 'box', [(i, (i + distance) % count) for i in range(co...  7.27 us
    pallas_call x1, Pallas kernels, outer_passes(): call(outer_kernel, (jax.ShapeDtypeStruct((4, 32, 1024), BF), jax.ShapeDty...  6.6 us
    ppermute x2, starting transfers between devices, shift_z(): return lax.ppermute(block, ('box', 'term'), route)  5.75 us
    pallas_call x1, Pallas kernels, prepare(): pl.pallas_call(prepare_kernel, out_shape=tuple((jax.ShapeDtypeStruct(shap...  4.02 us
    pallas_call x1, Pallas kernels, own_rows(): call(own_kernel, (jax.ShapeDtypeStruct((8, 32, 1024), F32), jax.ShapeDtyp...  3.54 us
  transfers between devices with their start and end apart: 10, of which 5 were waited for; matrix products, arithmetic and copies ran while one was open for 0% of the time, Pallas kernels for 21%

profile of v9, /device:TPU:30, one launch (start us, length us, event | category | flops | bytes accessed | tf_op | source)
XLA Modules:
  0.0 78.3 jit_solution(15705018365765031436)
XLA Ops:
  0.0 0.0 copy-start
  0.0 0.0 copy-start.1
  0.0 0.0 copy-start.2
  0.0 0.1 pad_add_fusion.where
  0.1 4.0 %prepare.1 = (bf16[32,1024]{1,0:T(8,128)(2,1)S(1)}, bf16[4,32,1024]{2,1,0:T(8,128)(2,1)S(1)}, bf16[4,32,1024]{2,1,0:T(8,128)(2,1)S(1)}, bf16[5,32,1024]{2,1,0:T(...) custom-call(s32[3]{0:T(128)S(1)} %pad_add_fusion.where, ...), custom_call_target="tpu_custom_call" | custom-call | tf_op jit(solution)/shard_map/prepare/pallas_call | solution.py:195
  4.1 0.1 collective-permute-start
  4.2 5.7 %collective-permute-start.1 = (bf16[5,32,1024]{2,1,0:T(8,128)(2,1)S(1)}, bf16[5,32,1024]{2,1,0:T(8,128)(2,1)S(1)}, u32[]{:S(2)}, u32[]{:S(2)}) collective-permute-start(bf16[5,32,1024]{2,1,0:T(8,128)(2,1)S(1)} %get-tuple-element.30), channel_id=1, source_target_pairs={{0,255},{1,254},{2,253},{3,252},{4,0},{5,1},{6,2},{7,3},{8,7},{9,6... | collective-permute-start | bytes 983048 | tf_op jit(solution)/shard_map/ppermute | solution.py:533
  9.9 0.2 collective-permute-start.2
  10.1 1.8 %collective-permute-start.3 = (bf16[4,32,1024]{2,1,0:T(8,128)(2,1)S(1)}, bf16[4,32,1024]{2,1,0:T(8,128)(2,1)S(1)}, u32[]{:S(2)}, u32[]{:S(2)}) collective-permute-start(bf16[4,32,1024]{2,1,0:T(8,128)(2,1)S(1)} %get-tuple-element.27.low_x), channel_id=1, source_target_pairs={{0,192},{4,196},{8,200},{12,204},{16,208},{20,212},{24,216},{28,22... | collective-permute-start | bytes 786440 | tf_op jit(solution)/shard_map/ppermute | solution.py:519
  11.9 12.6 %collective-permute-done.zm = bf16[5,32,1024]{2,1,0:T(8,128)(2,1)S(1)} collective-permute-done((bf16[5,32,1024]{2,1,0:T(8,128)(2,1)S(1)}, bf16[5,32,1024]{2,1,0:T(8,128)(2,1)S(1)}, u32[]{:S(2)}, u32[]{:S(2)}) %collective-permute-start) | collective-permute-done | bytes 327712 | tf_op jit(solution)/shard_map/ppermute | solution.py:533
  24.5 0.1 collective-permute-done.1.zp
  24.7 0.3 collective-permute-start.4
  25.0 1.9 %collective-permute-start.5 = (bf16[4,32,1024]{2,1,0:T(8,128)(2,1)S(1)}, bf16[4,32,1024]{2,1,0:T(8,128)(2,1)S(1)}, u32[]{:S(2)}, u32[]{:S(2)}) collective-permute-start(bf16[4,32,1024]{2,1,0:T(8,128)(2,1)S(1)} %pad_maximum_fusion.1), channel_id=1, source_target_pairs={{0,192},{4,196},{8,200},{12,204},{16,208},{20,212},{24,216},{28,22... | collective-permute-start | bytes 786440 | tf_op jit(solution)/shard_map/ppermute | solution.py:519
  26.9 1.5 %collective-permute-start.6 = (bf16[3,32,1024]{2,1,0:T(8,128)(2,1)S(1)}, bf16[3,32,1024]{2,1,0:T(8,128)(2,1)S(1)}, u32[]{:S(2)}, u32[]{:S(2)}) collective-permute-start(bf16[3,32,1024]{2,1,0:T(8,128)(2,1)S(1)} %pad_maximum_fusion.2), channel_id=1, source_target_pairs={{0,64},{4,68},{8,72},{12,76},{16,80},{20,84},{24,88},{28,92},{32,9... | collective-permute-start | bytes 589832 | tf_op jit(solution)/shard_map/ppermute | solution.py:519
  28.4 0.0 collective-permute-done.2.xm_own
  28.4 0.6 collective-permute-start.7
  29.0 0.0 copy-done
  29.0 0.0 copy-done.1
  29.0 0.0 copy-done.2
  29.0 3.0 %weights.1 = (bf16[8,512,256]{2,1,0:T(8,128)(2,1)S(1)}, bf16[8,64,128]{2,1,0:T(8,128)(2,1)S(1)}, bf16[2,128,256]{2,1,0:T(8,128)(2,1)S(1)}, bf16[8,384,128]{2,1,0...) custom-call(s32[8]{0:T(128)S(1)} %copy-done.2, bf16[16,3,32,32]{3,2,1,0:T(8,128)(2,1)S(1)} %copy-done, ...), custom_call_target="tpu_custom_call" | custom-call | tf_op jit(solution)/shard_map/weights/pallas_call | solution.py:104
  32.0 3.0 %shard_map.55.inner = bf16[8,16,64,256]{3,2,1,0:T(8,128)(2,1)S(1)} custom-call(bf16[4,32,1024]{2,1,0:T(8,128)(2,1)S(1)} %get-tuple-element.27.low_x, bf16[4,32,1024]{2,1,0:T(8,128)(2,1)S(1)} %get-tuple-element.28.high_x, bf16[5,32,1024]{2,1,0:T(8,128)(2,1)S(1)} %collective-permute-done.zm, bf16[5,32,1024]{2,1,0:T(8,128)(2,1)S(1)} %collective-permute-done.1.zp, ...), custom_call_target="tpu_custom_call" | custom-call | tf_op jit(solution)/shard_map/pallas_call | solution.py:243
  35.0 0.0 collective-permute-done.3.xp_own
  35.0 0.0 collective-permute-done.4.xm_far
  35.1 0.4 collective-permute-done.5.xp_far
  35.5 6.6 %shard_map.56 = (bf16[4,32,1024]{2,1,0:T(8,128)(2,1)S(1)}, bf16[4,32,1024]{2,1,0:T(8,128)(2,1)S(1)}, bf16[16,256,512]{2,1,0:T(8,128)(2,1)S(1)}) custom-call(bf16[8,16,64,256]{3,2,1,0:T(8,128)(2,1)S(1)} %shard_map.55.inner, bf16[4,32,1024]{2,1,0:T(8,128)(2,1)S(1)} %collective-permute-done.2.xm_own, bf16[4,32,1024]{2,1,0:T(8,128)(2,1)S(1)} %collective-permute-done.3.xp_own, ...), custom_call_target="tpu_custom_call" | custom-call | tf_op jit(solution)/shard_map/pallas_call | solution.py:325
  42.1 0.0 collective-permute-done.6.xm
  42.1 0.0 collective-permute-done.7.xp
  42.1 3.1 %shard_map.57 = (bf16[5,32,1024]{2,1,0:T(8,128)(2,1)S(1)}, bf16[5,32,1024]{2,1,0:T(8,128)(2,1)S(1)}, bf16[8,64,512]{2,1,0:T(8,128)(2,1)S(1)}) custom-call(bf16[32,1024]{1,0:T(8,128)(2,1)S(1)} %get-tuple-element.35.par, bf16[5,32,1024]{2,1,0:T(8,128)(2,1)S(1)} %collective-permute-done.zm, bf16[5,32,1024]{2,1,0:T(8,128)(2,1)S(1)} %collective-permute-done.1.zp, ...), custom_call_target="tpu_custom_call" | custom-call | tf_op jit(solution)/shard_map/pallas_call | solution.py:465
  45.2 6.6 %collective-permute-start.8 = (bf16[5,32,1024]{2,1,0:T(8,128)(2,1)S(1)}, bf16[5,32,1024]{2,1,0:T(8,128)(2,1)S(1)}, u32[]{:S(2)}, u32[]{:S(2)}) collective-permute-start(bf16[5,32,1024]{2,1,0:T(8,128)(2,1)S(1)} %get-tuple-element.44), channel_id=1, source_target_pairs={{0,16},{4,20},{8,24},{12,28},{16,32},{20,36},{24,40},{28,44},{32,4... | collective-permute-start | bytes 983048 | tf_op jit(solution)/shard_map/ppermute | solution.py:519
  51.8 0.0 collective-permute-start.9
  51.8 3.5 %shard_map.58 = (f32[8,32,1024]{2,1,0:T(8,128)S(1)}, f32[32,1024]{1,0:T(8,128)S(1)}) custom-call(bf16[16,256,512]{2,1,0:T(8,128)(2,1)S(1)} %get-tuple-element.34.packed, bf16[2,128,256]{2,1,0:T(8,128)(2,1)S(1)} %get-tuple-element.33.my, bf16[8,64,512]{2,1,0:T(8,128)(2,1)S(1)} %get-tuple-element.41.packed_c, bf16[384,64]{1,0:T(8,128)(2,1)S(1)} %get-tuple-element.38.my.my_c), custom_call_target="tpu_custom_call" | custom-call | tf_op jit(solution)/shard_map/pallas_call | solution.py:376
  55.3 1.0 %collective-permute-done.8.low = bf16[5,32,1024]{2,1,0:T(8,128)(2,1)S(1)} collective-permute-done((bf16[5,32,1024]{2,1,0:T(8,128)(2,1)S(1)}, bf16[5,32,1024]{2,1,0:T(8,128)(2,1)S(1)}, u32[]{:S(2)}, u32[]{:S(2)}) %collective-permute-start.8) | collective-permute-done | bytes 327712 | tf_op jit(solution)/shard_map/ppermute | solution.py:519
  56.4 5.8 %collective-permute-done.9.high = bf16[5,32,1024]{2,1,0:T(8,128)(2,1)S(1)} collective-permute-done((bf16[5,32,1024]{2,1,0:T(8,128)(2,1)S(1)}, bf16[5,32,1024]{2,1,0:T(8,128)(2,1)S(1)}, u32[]{:S(2)}, u32[]{:S(2)}) %collective-permute-start.9) | collective-permute-done | bytes 327712 | tf_op jit(solution)/shard_map/ppermute | solution.py:519
  62.2 1.8 %shard_map.59 = bf16[8,32,1024]{2,1,0:T(8,128)(2,1)S(1)} custom-call(f32[8,32,1024]{2,1,0:T(8,128)S(1)} %get-tuple-element.42.own, f32[32,1024]{1,0:T(8,128)S(1)} %get-tuple-element.43.own_c, bf16[5,32,1024]{2,1,0:T(8,128)(2,1)S(1)} %collective-permute-done.8.low, bf16[5,32,1024]{2,1,0:T(8,128)(2,1)S(1)} %collective-permute-done.9.high, ...), custom_call_target="tpu_custom_call" | custom-call | tf_op jit(solution)/shard_map/pallas_call | solution.py:510
  64.0 13.2 %all_to_all.5 = bf16[4,2,32,1024]{3,2,1,0:T(8,128)(2,1)S(1)} all-to-all(bf16[4,2,32,1024]{3,2,1,0:T(8,128)(2,1)S(1)} %bitcast.5), channel_id=1, replica_groups=mesh['box'=64,'term'=4] {'term'}, dimensions={0} | all-to-all | bytes 1048576 | tf_op jit(solution)/shard_map/all_to_all | solution.py:565
  77.2 1.1 %convert_element_type.3 = f32[4,2,32,1024]{3,2,1,0:T(8,128)} convert(bf16[4,2,32,1024]{3,2,1,0:T(8,128)(2,1)S(1)} %all_to_all.5) | non-fusion elementwise | flops 262144 | bytes 1572864 | tf_op jit(solution)/shard_map/convert_element_type | solution.py:566
  (7 shorter events, 0.1 us)
Async XLA Ops:
  0.0 29.0 %copy-start = (bf16[16,3,32,32]{3,2,1,0:T(8,128)(2,1)S(1)}, bf16[16,3,32,32]{3,2,1,0:T(8,128)(2,1)}, u32[]{:S(2)}) copy-start(bf16[16,3,32,32]{3,2,1,0:T(8,128)(2,1)} %fine.1) | copy-start | bytes 294916
  0.0 29.0 %copy-start.1 = (bf16[16,3,32,32]{3,2,1,0:T(8,128)(2,1)S(1)}, bf16[16,3,32,32]{3,2,1,0:T(8,128)(2,1)}, u32[]{:S(2)}) copy-start(bf16[16,3,32,32]{3,2,1,0:T(8,128)(2,1)} %coarse.1) | copy-start | bytes 294916
  0.0 29.0 %copy-start.2 = (s32[8]{0:T(128)S(1)}, s32[8]{0:T(128)}, u32[]{:S(2)}) copy-start(s32[8]{0:T(128)} %exponents.1) | copy-start | bytes 100
  4.1 20.4 %collective-permute-start = (bf16[5,32,1024]{2,1,0:T(8,128)(2,1)S(1)}, bf16[5,32,1024]{2,1,0:T(8,128)(2,1)S(1)}, u32[]{:S(2)}, u32[]{:S(2)}) collective-permute-start(bf16[5,32,1024]{2,1,0:T(8,128)(2,1)S(1)} %get-tuple-element.29), channel_id=1, source_target_pairs={{0,4},{1,5},{2,6},{3,7},{4,11},{5,10},{6,9},{7,8},{8,12},{9,13},{1... | collective-permute-start | bytes 983048 | tf_op jit(solution)/shard_map/ppermute | solution.py:533
  4.2 20.4 %collective-permute-start.1 = (bf16[5,32,1024]{2,1,0:T(8,128)(2,1)S(1)}, bf16[5,32,1024]{2,1,0:T(8,128)(2,1)S(1)}, u32[]{:S(2)}, u32[]{:S(2)}) collective-permute-start(bf16[5,32,1024]{2,1,0:T(8,128)(2,1)S(1)} %get-tuple-element.30), channel_id=1, source_target_pairs={{0,255},{1,254},{2,253},{3,252},{4,0},{5,1},{6,2},{7,3},{8,7},{9,6... | collective-permute-start | bytes 983048 | tf_op jit(solution)/shard_map/ppermute | solution.py:533
  9.9 18.5 %collective-permute-start.2 = (bf16[4,32,1024]{2,1,0:T(8,128)(2,1)S(1)}, bf16[4,32,1024]{2,1,0:T(8,128)(2,1)S(1)}, u32[]{:S(2)}, u32[]{:S(2)}) collective-permute-start(bf16[4,32,1024]{2,1,0:T(8,128)(2,1)S(1)} %get-tuple-element.28.high_x), channel_id=1, source_target_pairs={{0,64},{4,68},{8,72},{12,76},{16,80},{20,84},{24,88},{28,92},{32,9... | collective-permute-start | bytes 786440 | tf_op jit(solution)/shard_map/ppermute | solution.py:519
  10.1 24.9 %collective-permute-start.3 = (bf16[4,32,1024]{2,1,0:T(8,128)(2,1)S(1)}, bf16[4,32,1024]{2,1,0:T(8,128)(2,1)S(1)}, u32[]{:S(2)}, u32[]{:S(2)}) collective-permute-start(bf16[4,32,1024]{2,1,0:T(8,128)(2,1)S(1)} %get-tuple-element.27.low_x), channel_id=1, source_target_pairs={{0,192},{4,196},{8,200},{12,204},{16,208},{20,212},{24,216},{28,22... | collective-permute-start | bytes 786440 | tf_op jit(solution)/shard_map/ppermute | solution.py:519
  24.7 10.4 %collective-permute-start.4 = (bf16[4,32,1024]{2,1,0:T(8,128)(2,1)S(1)}, bf16[4,32,1024]{2,1,0:T(8,128)(2,1)S(1)}, u32[]{:S(2)}, u32[]{:S(2)}) collective-permute-start(bf16[4,32,1024]{2,1,0:T(8,128)(2,1)S(1)} %pad_maximum_fusion), channel_id=1, source_target_pairs={{0,64},{4,68},{8,72},{12,76},{16,80},{20,84},{24,88},{28,92},{32,9... | collective-permute-start | bytes 786440 | tf_op jit(solution)/shard_map/ppermute | solution.py:519
  25.0 10.5 %collective-permute-start.5 = (bf16[4,32,1024]{2,1,0:T(8,128)(2,1)S(1)}, bf16[4,32,1024]{2,1,0:T(8,128)(2,1)S(1)}, u32[]{:S(2)}, u32[]{:S(2)}) collective-permute-start(bf16[4,32,1024]{2,1,0:T(8,128)(2,1)S(1)} %pad_maximum_fusion.1), channel_id=1, source_target_pairs={{0,192},{4,196},{8,200},{12,204},{16,208},{20,212},{24,216},{28,22... | collective-permute-start | bytes 786440 | tf_op jit(solution)/shard_map/ppermute | solution.py:519
  26.9 15.2 %collective-permute-start.6 = (bf16[3,32,1024]{2,1,0:T(8,128)(2,1)S(1)}, bf16[3,32,1024]{2,1,0:T(8,128)(2,1)S(1)}, u32[]{:S(2)}, u32[]{:S(2)}) collective-permute-start(bf16[3,32,1024]{2,1,0:T(8,128)(2,1)S(1)} %pad_maximum_fusion.2), channel_id=1, source_target_pairs={{0,64},{4,68},{8,72},{12,76},{16,80},{20,84},{24,88},{28,92},{32,9... | collective-permute-start | bytes 589832 | tf_op jit(solution)/shard_map/ppermute | solution.py:519
  28.4 13.7 %collective-permute-start.7 = (bf16[3,32,1024]{2,1,0:T(8,128)(2,1)S(1)}, bf16[3,32,1024]{2,1,0:T(8,128)(2,1)S(1)}, u32[]{:S(2)}, u32[]{:S(2)}) collective-permute-start(bf16[3,32,1024]{2,1,0:T(8,128)(2,1)S(1)} %pad_maximum_fusion.2), channel_id=1, source_target_pairs={{0,192},{4,196},{8,200},{12,204},{16,208},{20,212},{24,216},{28,22... | collective-permute-start | bytes 589832 | tf_op jit(solution)/shard_map/ppermute | solution.py:519
  45.2 11.2 %collective-permute-start.8 = (bf16[5,32,1024]{2,1,0:T(8,128)(2,1)S(1)}, bf16[5,32,1024]{2,1,0:T(8,128)(2,1)S(1)}, u32[]{:S(2)}, u32[]{:S(2)}) collective-permute-start(bf16[5,32,1024]{2,1,0:T(8,128)(2,1)S(1)} %get-tuple-element.44), channel_id=1, source_target_pairs={{0,16},{4,20},{8,24},{12,28},{16,32},{20,36},{24,40},{28,44},{32,4... | collective-permute-start | bytes 983048 | tf_op jit(solution)/shard_map/ppermute | solution.py:519
  51.8 10.4 %collective-permute-start.9 = (bf16[5,32,1024]{2,1,0:T(8,128)(2,1)S(1)}, bf16[5,32,1024]{2,1,0:T(8,128)(2,1)S(1)}, u32[]{:S(2)}, u32[]{:S(2)}) collective-permute-start(bf16[5,32,1024]{2,1,0:T(8,128)(2,1)S(1)} %get-tuple-element.45), channel_id=1, source_target_pairs={{0,240},{4,244},{8,248},{12,252},{16,0},{20,4},{24,8},{28,12},{32,... | collective-permute-start | bytes 983048 | tf_op jit(solution)/shard_map/ppermute | solution.py:519
